TPU v7x, 128 devices: a whole 4x4x4 slice. The times are simulated.
128 devices in a mesh: gx: 16 (over x, z), gy: 8 (over y, core).
Axes of the slice: x: 4, y: 4, z: 4, core: 2. Of those that a mesh axis runs over, the one named last changes fastest.
Arguments:
- reference_scan: bfloat16 [256, 256, 2048], P('gx', 'gy'), may hold values from -6 to 6
- ref_gradient: bfloat16 [3, 256, 256, 2048], P(None, 'gx', 'gy'), may hold values from -6 to 6
- deformed_scan: bfloat16 [256, 256, 2048], P('gx', 'gy'), may hold values from -6 to 6
- interp_weights: bfloat16 [256, 256, 2048], P('gx', 'gy'), may hold values from 0 to 1
- sample_mask: int32 [256, 256, 2048], P('gx', 'gy'), may hold values from 0 to 1, as said below
- block_list: int32 [16, 32768], P('gx', 'gy'), may hold values from -1 to 8191, as said below
- offsets: int32 [2, 256, 256, 4], P(None, 'gx', 'gy'), may hold values from -4 to 4, as said below
Outputs:
- increment: float32 [3, 256, 256, 5], P(None, 'gx', 'gy')
- cg_residual: float32 [3, 256, 256, 5], P(None, 'gx', 'gy')
Inputs may be any that keep to these rules, and one draw needn't show every extreme that they name: sample_mask is 0 in every block of 128 voxels that its device's block_list does not name. `block_list`: each device's 4096 entries are first distinct local block indices, then -1 to the end; some device names exactly 4096 blocks. `offsets`: both ends of the range occur.
All inputs are finite; a program needn't handle non-finite values.
Results may differ from a plain program's by a relative error of at most 0.0045.
Values may be sent and summed in bfloat16 or wider, within the bound.
No kernel may reach another device: no remote copies, remote signals or barrier semaphores. Data moves between devices by JAX's collectives and lax.ppermute only.
A program may use at most 320 MiB of HBM per device.

v0:
```python
import jax
import jax.numpy as jnp
from jax import lax
from jax.sharding import PartitionSpec as P

BOUND = 4
ITERS = 3


tikhonov = 8.0


def extended(value, sides, width):
    for axis, dim in sides:
        devices, length = (lax.axis_size(axis), value.shape[dim])
        up = [(i, (i + 1) % devices) for i in range(devices - 1)]
        down = [(j, i) for i, j in up]
        last = lax.slice_in_dim(value, length - width, length, axis=dim)
        first = lax.slice_in_dim(value, 0, width, axis=dim)
        before = lax.ppermute(last, axis, up)
        after = lax.ppermute(first, axis, down)
        value = jnp.concatenate([before, value, after], axis=dim)
    return value


def from_behind(block, axis, distance):
    devices = range(lax.axis_size(axis))
    route = [(i - distance, i) for i in devices if i - distance in devices]
    return lax.ppermute(block, axis, route)


def shape_table():
    voxel = jnp.arange(512)
    coords = [
        ((voxel // 64).astype(jnp.float32) + 0.5) / 8.0,
        ((voxel // 8 % 8).astype(jnp.float32) + 0.5) / 8.0,
        ((voxel % 8).astype(jnp.float32) + 0.5) / 8.0,
    ]
    rows = []
    for node in range(8):
        bits = [node >> 2 & 1, node >> 1 & 1, node & 1]
        value = jnp.ones((512,), jnp.float32)
        for axis_pos in range(3):
            value = value * (coords[axis_pos] if bits[axis_pos] else 1.0 - coords[axis_pos])
        rows.append(value)
    return jnp.transpose(jnp.stack(rows).reshape(8, 4, 128), (1, 0, 2))


def block_terms(grad_rows, resid_rows, mask_rows, kinds, table):
    onehot = (kinds[:, None] == jnp.arange(4)[None, :]).astype(jnp.float32)
    shapes = jnp.einsum("bk,knv->bnv", onehot, table, precision=lax.Precision.HIGHEST)
    product = shapes[:, :, None, :] * grad_rows[:, None, :, :].astype(jnp.float32)
    jacobian = product.reshape(kinds.shape[0], 24, 128).astype(jnp.bfloat16)
    weighted = jacobian * mask_rows[:, None, :]
    hessian = jnp.einsum("bdv,bev->bde", weighted, jacobian, preferred_element_type=jnp.float32)
    gradient = jnp.einsum("bdv,bv->bd", weighted, resid_rows, preferred_element_type=jnp.float32)
    return (hessian, gradient)


def run_groups(grad_rows, resid_rows, mask_rows, kinds, table):
    count = kinds.shape[0]
    groups = 4
    packed = (
        grad_rows.reshape((groups, count // groups) + grad_rows.shape[1:]),
        resid_rows.reshape(groups, count // groups, 128),
        mask_rows.reshape(groups, count // groups, 128),
        kinds.reshape(groups, count // groups),
    )
    hessian, gradient = lax.map(
        lambda parts: block_terms(parts[0], parts[1], parts[2], parts[3], table), packed
    )
    return (hessian.reshape(count, 24, 24), gradient.reshape(count, 24))


def per_device(
    reference_scan, ref_gradient, deformed_scan, interp_weights, sample_mask, block_list, offsets
):
    tile_x, tile_y, column = reference_scan.shape
    elem_depth = column // 512
    padded = extended(deformed_scan, (("gx", 0), ("gy", 1)), BOUND + 1)
    margin = BOUND + 1
    span_y = padded.shape[1]
    flat_scan = padded.reshape(padded.shape[0] * span_y, elem_depth, 512)
    pos_x = jnp.arange(tile_x)[:, None, None]
    pos_y = jnp.arange(tile_y)[None, :, None]
    source = (pos_x + offsets[0] + margin) * span_y + pos_y + offsets[1] + margin
    layer = jnp.broadcast_to(jnp.arange(elem_depth)[None, None, :], source.shape)
    near = flat_scan[source, layer].astype(jnp.float32)
    far = flat_scan[source + span_y, layer].astype(jnp.float32)
    weights = interp_weights.reshape(tile_x, tile_y, elem_depth, 512).astype(jnp.float32)
    warped = weights * near + (1.0 - weights) * far
    residual_image = (
        reference_scan.reshape(tile_x, tile_y, elem_depth, 512).astype(jnp.float32) - warped
    ).astype(jnp.bfloat16)
    local_blocks = tile_x * tile_y * elem_depth * 4
    elements = local_blocks // 4
    grad_blocks = jnp.moveaxis(ref_gradient.reshape(3, local_blocks, 128), 0, 1)
    resid_blocks = residual_image.reshape(local_blocks, 128)
    mask_blocks = sample_mask.reshape(local_blocks, 128)
    entries = block_list.reshape(-1)
    listed = entries >= 0
    safe = jnp.maximum(entries, 0)
    table = shape_table()
    marks = jnp.zeros((local_blocks,), jnp.bfloat16).at[safe].add(listed.astype(jnp.bfloat16))
    mask_rows = mask_blocks.astype(jnp.bfloat16) * marks[:, None]
    hessian, gradient = run_groups(
        grad_blocks, resid_blocks, mask_rows, jnp.arange(local_blocks) % 4, table
    )
    elem_hess = hessian.reshape(elements, 4, 24, 24).sum(axis=1)
    elem_load = gradient.reshape(elements, 4, 24).sum(axis=1)
    stiffness = jnp.transpose(elem_hess, (1, 2, 0))
    loads = jnp.transpose(elem_load, (1, 0))

    def collect(values):
        parts = values.reshape(8, 3, tile_x, tile_y, elem_depth)
        total = jnp.zeros((3, tile_x + 1, tile_y + 1, elem_depth + 1), jnp.float32)
        for node in range(8):
            i_bit, j_bit, l_bit = (node >> 2 & 1, node >> 1 & 1, node & 1)
            total = total + jnp.pad(
                parts[node], ((0, 0), (i_bit, 1 - i_bit), (j_bit, 1 - j_bit), (l_bit, 1 - l_bit))
            )
        passed_y = from_behind(total[:, :, tile_y:], "gy", 1)
        total = total[:, :, :tile_y].at[:, :, 0:1].add(passed_y)
        passed_x = from_behind(total[:, tile_x:], "gx", 1)
        return total[:, :tile_x].at[:, 0:1].add(passed_x)

    def squares(vector):
        return lax.psum(jnp.sum(vector * vector), ("gx", "gy"))

    rhs = collect(loads)
    increment = jnp.zeros_like(rhs)
    cg_residual = rhs
    direction = rhs
    norm_now = squares(cg_residual)
    for sweep in range(ITERS):
        upper_x = from_behind(direction[:, :1], "gx", -1)
        wide = jnp.concatenate([direction, upper_x], axis=1)
        upper_y = from_behind(wide[:, :, :1], "gy", -1)
        wide = jnp.concatenate([wide, upper_y], axis=2)
        pieces = []
        for spread_node in range(8):
            spread_i_bit, spread_j_bit, spread_l_bit = (
                spread_node >> 2 & 1,
                spread_node >> 1 & 1,
                spread_node & 1,
            )
            pieces.append(
                wide[
                    :,
                    spread_i_bit : spread_i_bit + tile_x,
                    spread_j_bit : spread_j_bit + tile_y,
                    spread_l_bit : spread_l_bit + elem_depth,
                ]
            )
        images = jnp.einsum(
            "nzr,zr->nr",
            stiffness,
            jnp.stack(pieces).reshape(24, elements),
            precision=lax.Precision.HIGHEST,
        )
        image = collect(images) + tikhonov * direction
        step_size = norm_now / lax.psum(jnp.sum(direction * image), ("gx", "gy"))
        increment = increment + step_size * direction
        cg_residual = cg_residual - step_size * image
        norm_next = squares(cg_residual)
        direction = cg_residual + norm_next / norm_now * direction
        norm_now = norm_next
    return (increment, cg_residual)


def solution(mesh):
    return jax.shard_map(
        per_device,
        mesh=mesh,
        in_specs=(
            P("gx", "gy", None),
            P(None, "gx", "gy", None),
            P("gx", "gy", None),
            P("gx", "gy", None),
            P("gx", "gy", None),
            P("gx", "gy"),
            P(None, "gx", "gy", None),
        ),
        out_specs=(P(None, "gx", "gy", None), P(None, "gx", "gy", None)),
        check_vma=False,
    )
```

profile of v0, /device:TPU:1, one launch (start us, length us, event | category | flops | bytes accessed | tf_op | source)
XLA Modules:
  0.0 1116.2 jit_solution(5905203866867956288)
XLA Ops:
  3.0 5.2 collective-permute-start
  13.1 4.5 reshape.733
  17.6 4.5 reshape.734
  22.2 4.0 convert_element_type.286
  26.1 4.2 convert_element_type.287
  30.3 29.0 %scatter_custom_fusion = bf16[8192]{0:T(1024)(128)(2,1)S(1)} fusion(s32[4096]{0:T(1024)S(1)} %bitcast.232, bf16[4096]{0:T(1024)(128)(2,1)S(1)} %fusion.63, bf16[]{:T(256)} %constant.278.clone.1), kind=kCustom, calls=%fused_computation.158 | custom fusion | flops 4096 | bytes 16386 | tf_op jit(solution)/shard_map/scatter-add | solution.py:104
  59.4 10.5 reshape.725
  73.6 3.7 collective-permute-start.2
  84.9 4.4 collective-permute-done.3
  89.3 6.1 pad_maximum_fusion
  95.3 4.8 copy.263
  100.1 10.6 reshape.727
  110.7 26.2 %gather_fusion = bf16[2048,512]{1,0:T(8,128)(2,1)S(1)} fusion(bf16[1092,4,512]{2,1,0:T(4,128)(2,1)} %reshape.727, s32[2048]{0:T(1024)S(1)} %reshape.737), kind=kCustom, calls=%fused_computation | custom fusion | bytes 4210688 | tf_op jit(solution)/shard_map/gather | solution.py:88
  139.8 26.3 %gather_fusion.1 = bf16[2048,512]{1,0:T(8,128)(2,1)S(1)} fusion(bf16[1092,4,512]{2,1,0:T(4,128)(2,1)} %reshape.727, s32[2048]{0:T(1024)S(1)} %reshape.743), kind=kCustom, calls=%fused_computation.1 | custom fusion | bytes 4210688 | tf_op jit(solution)/shard_map/gather | solution.py:89
  169.0 6.7 subtract_convert_fusion
  175.7 278.2 %while.20 = (s32[]{:T(128)}, f32[4,2048,24,24]{3,2,1,0:T(8,128)}, f32[4,2048,24]{1,2,0:T(8,128)}, s32[4,2048]{1,0:T(4,128)S(1)}, f32[4,8,128]{2,0,1:T(4,128)S(1)...) while((s32[]{:T(128)}, f32[4,2048,24,24]{3,2,1,0:T(8,128)}, ...), condition=%wide.region_2.3_spmd, body=%wide.region_1.2_spmd.sunk | while | flops 434905088 | bytes 179807376 | solution.py:69
  189.9 3.5 fusion.101
  195.0 3.4 multiply_convert_fusion.2
  199.9 6.8 broadcast_multiply_fusion.3
  206.6 27.1 %bitcast_dynamic-update-slice_fusion.4 = f32[4,2048,24,24]{3,2,1,0:T(8,128)} fusion(f32[4,2048,24,24]{3,2,1,0:T(8,128)} %get-tuple-element.338, s32[]{:T(128)} %get-tuple-element.337, bf16[2048,24,128]{2,0,1:T(8,128)(2,1)} %bitcast.212, bf16[2048,24,128]{2,0,1:T(8,128)(2,1)} %broadcast_multiply_fusion.3), kind=kOutput, calls=%fused_computation.3.clone.1 | convolution fusion | flops 301989888 | bytes 50332160 | tf_op jit(solution)/shard_map/while/body/eval_jaxpr/bdv,bev->bde/dot_general | solution.py:55
  233.7 20.8 %fusion.102 = f32[2048,1,24]{2,1,0:T(1,128)S(1)} fusion(bf16[2048,24,128]{2,0,1:T(8,128)(2,1)} %broadcast_multiply_fusion.3, bf16[2048,128,1]{1,0,2:T(8,128)(2,1)S(1)} %dynamic-slice_bitcast_fusion.5), kind=kOutput, calls=%fused_computation.7.clone.1 | convolution fusion | flops 12582912 | bytes 13303808 | tf_op jit(solution)/shard_map/while/body/eval_jaxpr/bdv,bv->bd/dot_general | solution.py:56
  255.8 3.5 fusion.101
  260.9 3.4 multiply_convert_fusion.2
  265.8 6.8 broadcast_multiply_fusion.3
  272.5 27.0 %bitcast_dynamic-update-slice_fusion.4 = f32[4,2048,24,24]{3,2,1,0:T(8,128)} fusion(f32[4,2048,24,24]{3,2,1,0:T(8,128)} %get-tuple-element.338, s32[]{:T(128)} %get-tuple-element.337, bf16[2048,24,128]{2,0,1:T(8,128)(2,1)} %bitcast.212, bf16[2048,24,128]{2,0,1:T(8,128)(2,1)} %broadcast_multiply_fusion.3), kind=kOutput, calls=%fused_computation.3.clone.1 | convolution fusion | flops 301989888 | bytes 50332160 | tf_op jit(solution)/shard_map/while/body/eval_jaxpr/bdv,bev->bde/dot_general | solution.py:55
  299.6 20.8 %fusion.102 = f32[2048,1,24]{2,1,0:T(1,128)S(1)} fusion(bf16[2048,24,128]{2,0,1:T(8,128)(2,1)} %broadcast_multiply_fusion.3, bf16[2048,128,1]{1,0,2:T(8,128)(2,1)S(1)} %dynamic-slice_bitcast_fusion.5), kind=kOutput, calls=%fused_computation.7.clone.1 | convolution fusion | flops 12582912 | bytes 13303808 | tf_op jit(solution)/shard_map/while/body/eval_jaxpr/bdv,bv->bd/dot_general | solution.py:56
  321.7 3.5 fusion.101
  326.8 3.4 multiply_convert_fusion.2
  331.7 6.8 broadcast_multiply_fusion.3
  338.4 27.0 %bitcast_dynamic-update-slice_fusion.4 = f32[4,2048,24,24]{3,2,1,0:T(8,128)} fusion(f32[4,2048,24,24]{3,2,1,0:T(8,128)} %get-tuple-element.338, s32[]{:T(128)} %get-tuple-element.337, bf16[2048,24,128]{2,0,1:T(8,128)(2,1)} %bitcast.212, bf16[2048,24,128]{2,0,1:T(8,128)(2,1)} %broadcast_multiply_fusion.3), kind=kOutput, calls=%fused_computation.3.clone.1 | convolution fusion | flops 301989888 | bytes 50332160 | tf_op jit(solution)/shard_map/while/body/eval_jaxpr/bdv,bev->bde/dot_general | solution.py:55
  365.5 20.8 %fusion.102 = f32[2048,1,24]{2,1,0:T(1,128)S(1)} fusion(bf16[2048,24,128]{2,0,1:T(8,128)(2,1)} %broadcast_multiply_fusion.3, bf16[2048,128,1]{1,0,2:T(8,128)(2,1)S(1)} %dynamic-slice_bitcast_fusion.5), kind=kOutput, calls=%fused_computation.7.clone.1 | convolution fusion | flops 12582912 | bytes 13303808 | tf_op jit(solution)/shard_map/while/body/eval_jaxpr/bdv,bv->bd/dot_general | solution.py:56
  387.5 3.5 fusion.101
  397.5 6.8 broadcast_multiply_fusion.3
  404.3 27.1 %bitcast_dynamic-update-slice_fusion.4 = f32[4,2048,24,24]{3,2,1,0:T(8,128)} fusion(f32[4,2048,24,24]{3,2,1,0:T(8,128)} %get-tuple-element.338, s32[]{:T(128)} %get-tuple-element.337, bf16[2048,24,128]{2,0,1:T(8,128)(2,1)} %bitcast.212, bf16[2048,24,128]{2,0,1:T(8,128)(2,1)} %broadcast_multiply_fusion.3), kind=kOutput, calls=%fused_computation.3.clone.1 | convolution fusion | flops 301989888 | bytes 50332160 | tf_op jit(solution)/shard_map/while/body/eval_jaxpr/bdv,bev->bde/dot_general | solution.py:55
  431.5 20.8 %fusion.102 = f32[2048,1,24]{2,1,0:T(1,128)S(1)} fusion(bf16[2048,24,128]{2,0,1:T(8,128)(2,1)} %broadcast_multiply_fusion.3, bf16[2048,128,1]{1,0,2:T(8,128)(2,1)S(1)} %dynamic-slice_bitcast_fusion.5), kind=kOutput, calls=%fused_computation.7.clone.1 | convolution fusion | flops 12582912 | bytes 13303808 | tf_op jit(solution)/shard_map/while/body/eval_jaxpr/bdv,bv->bd/dot_general | solution.py:56
  453.9 3.6 copy.267
  457.4 10.4 reduce_sum.72
  467.9 4.6 fusion.82
  472.5 5.6 copy.298
  478.1 5.5 copy.299
  483.6 5.5 copy.300
  489.1 5.5 copy.301
  494.6 5.5 copy.302
  500.2 4.3 copy.303
  504.5 3.4 copy.304
  507.9 3.8 copy.305
  518.4 4.4 collective-permute-start.5
  522.8 41.1 %reduce_sum.74 = f32[2048,24,24]{2,1,0:T(8,128)} reduce(f32[2048,4,24,24]{3,2,1,0:T(8,128)} %bitcast.40, f32[]{:T(128)} %constant.271.clone.1), dimensions={1}, to_apply=%region_6.7 | reduce | flops 3538944 | bytes 23592964 | tf_op jit(solution)/shard_map/reduce_sum | solution.py:109
  568.9 3.5 collective-permute-start.7
  582.4 6.7 reshape.728
  589.4 14.2 %fusion.14 = f32[2048,24]{1,0:T(8,128)S(1)} fusion(f32[2048,24,24]{2,1,0:T(8,128)} %reduce_sum.74, f32[2048,24]{1,0:T(8,128)S(1)} %copy.307), kind=kLoop, calls=%fused_computation.24 | loop fusion | flops 2310144 | bytes 5111808
  626.2 71.0 %all-reduce.32 = (f32[]{:T(128)}, f32[]{:T(128)}) all-reduce(f32[]{:T(128)} %get-tuple-element.216, f32[]{:T(128)} %get-tuple-element.215), channel_id=1, replica_groups=mesh['gx'=16,'gy'=8] {'gx','gy'}, use_global_device_ids=true, to_apply=%region_5.6 | all-reduce | flops 2 | bytes 16 | tf_op jit(solution)/shard_map/psum | solution.py:128
  699.3 62.7 %psum.44 = f32[]{:T(128)} all-reduce(f32[]{:T(128)} %multiply_reduce_fusion.3), channel_id=1, replica_groups=mesh['gx'=16,'gy'=8] {'gx','gy'}, use_global_device_ids=true, to_apply=%region_10.11 | all-reduce | flops 1 | bytes 8 | tf_op jit(solution)/shard_map/psum | solution.py:128
  768.5 3.7 collective-permute-start.11
  781.3 7.2 reshape.729
  789.8 15.2 %fusion.15 = f32[2048,24]{1,0:T(8,128)} fusion(f32[2048,24,24]{2,1,0:T(8,128)} %reduce_sum.74, f32[2048,24]{1,0:T(8,128)S(1)} %copy.308), kind=kLoop, calls=%fused_computation.25 | loop fusion | flops 2310144 | bytes 5111808
  819.4 3.5 pad_add_fusion.1
  830.9 67.6 %psum.45 = f32[]{:T(128)} all-reduce(f32[]{:T(128)} %multiply_reduce_fusion.2), channel_id=1, replica_groups=mesh['gx'=16,'gy'=8] {'gx','gy'}, use_global_device_ids=true, to_apply=%region_12.13 | all-reduce | flops 1 | bytes 8 | tf_op jit(solution)/shard_map/psum | solution.py:162
  901.9 63.2 %psum.46 = f32[]{:T(128)} all-reduce(f32[]{:T(128)} %get-tuple-element.235), channel_id=1, replica_groups=mesh['gx'=16,'gy'=8] {'gx','gy'}, use_global_device_ids=true, to_apply=%region_14.15 | all-reduce | flops 1 | bytes 8 | tf_op jit(solution)/shard_map/psum | solution.py:128
  971.5 4.2 collective-permute-start.15
  983.7 6.7 reshape.730
  991.7 15.3 %fusion.16 = f32[2048,24]{1,0:T(8,128)} fusion(f32[2048,24,24]{2,1,0:T(8,128)} %reduce_sum.74, f32[2048,24]{1,0:T(8,128)} %copy.309), kind=kLoop, calls=%fused_computation.26 | loop fusion | flops 2310144 | bytes 5111808
  1024.5 3.8 pad_add_fusion
  1039.2 68.2 %psum.47 = f32[]{:T(128)} all-reduce(f32[]{:T(128)} %multiply_reduce_fusion), channel_id=1, replica_groups=mesh['gx'=16,'gy'=8] {'gx','gy'}, use_global_device_ids=true, to_apply=%region_16.17 | all-reduce | flops 1 | bytes 8 | tf_op jit(solution)/shard_map/psum | solution.py:162
  (206 shorter events, 179.9 us)
Async XLA Ops:
  0.6 11.6 %copy-start.6 = (s32[1,4096]{1,0:T(1,128)S(1)}, s32[1,4096]{1,0:T(1,128)}, u32[]{:S(2)}) copy-start(s32[1,4096]{1,0:T(1,128)} %param.30) | copy-start | bytes 49156
  0.6 11.7 %copy-start.5 = (s32[2,16,32,4]{2,3,1,0:T(4,128)S(1)}, s32[2,16,32,4]{2,3,1,0:T(4,128)}, u32[]{:S(2)}) copy-start(s32[2,16,32,4]{2,3,1,0:T(4,128)} %param.31) | copy-start | bytes 49156
  3.0 67.1 %collective-permute-start = (bf16[5,32,2048]{2,1,0:T(8,128)(2,1)}, bf16[5,32,2048]{2,1,0:T(8,128)(2,1)}, u32[]{:S(2)}, u32[]{:S(2)}) collective-permute-start(bf16[5,32,2048]{2,1,0:T(8,128)(2,1)} %get-tuple-element.241), channel_id=1, source_target_pairs={{0,8},{8,16},{16,24},{24,32},{32,40},{40,48},{48,56},{56,64},{64,7... | collective-permute-start | bytes 1966088 | tf_op jit(solution)/shard_map/ppermute | solution.py:20
  8.2 63.5 %collective-permute-start.1 = (bf16[5,32,2048]{2,1,0:T(8,128)(2,1)S(1)}, bf16[5,32,2048]{2,1,0:T(8,128)(2,1)}, u32[]{:S(2)}, u32[]{:S(2)}) collective-permute-start(bf16[5,32,2048]{2,1,0:T(8,128)(2,1)S(1)} %get-tuple-element.242), channel_id=1, source_target_pairs={{8,0},{16,8},{24,16},{32,24},{40,32},{48,40},{56,48},{64,56},{72,6... | collective-permute-start | bytes 1966088 | tf_op jit(solution)/shard_map/ppermute | solution.py:21
  69.9 9.6 copy-start.1
  73.6 11.2 %collective-permute-start.2 = (bf16[26,5,2048]{2,0,1:T(8,128)(2,1)S(1)}, bf16[26,5,2048]{2,0,1:T(8,128)(2,1)S(1)}, u32[]{:S(2)}, u32[]{:S(2)}) collective-permute-start(bf16[26,5,2048]{2,0,1:T(8,128)(2,1)S(1)} %get-tuple-element.239), channel_id=1, source_target_pairs={{0,1},{1,2},{2,3},{3,4},{4,5},{5,6},{6,7},{8,9},{9,10},{10,11},{11... | collective-permute-start | bytes 1597448 | tf_op jit(solution)/shard_map/ppermute | solution.py:20
  77.4 11.9 %collective-permute-start.3 = (bf16[26,5,2048]{2,0,1:T(8,128)(2,1)S(1)}, bf16[26,5,2048]{2,0,1:T(8,128)(2,1)S(1)}, u32[]{:S(2)}, u32[]{:S(2)}) collective-permute-start(bf16[26,5,2048]{2,0,1:T(8,128)(2,1)S(1)} %get-tuple-element.240), channel_id=1, source_target_pairs={{1,0},{2,1},{3,2},{4,3},{5,4},{6,5},{7,6},{9,8},{10,9},{11,10},{12... | collective-permute-start | bytes 1597448 | tf_op jit(solution)/shard_map/ppermute | solution.py:21
  198.4 8.3 copy-start
  264.3 8.3 copy-start
  330.2 8.3 copy-start
  396.0 8.3 copy-start
  472.5 27.7 %copy-start.4 = (f32[3,2048]{0,1:T(8,128)S(1)}, f32[3,2048]{0,1:T(8,128)}, u32[]{:S(2)}) copy-start(f32[3,2048]{0,1:T(8,128)} %get-tuple-element.246) | copy-start | bytes 73732
  515.1 3.1 collective-permute-start.4
  518.4 45.6 %collective-permute-start.5 = (f32[3,1,32,5]{3,2,1,0:T(8,128)S(1)}, f32[3,1,32,5]{3,2,1,0:T(8,128)S(1)}, u32[]{:S(2)}, u32[]{:S(2)}) collective-permute-start(f32[3,1,32,5]{3,2,1,0:T(8,128)S(1)} %slice.630), channel_id=1, source_target_pairs={{0,8},{8,16},{16,24},{24,32},{32,40},{40,48},{48,56},{56,64},{64,7... | collective-permute-start | bytes 5768 | tf_op jit(solution)/shard_map/ppermute | solution.py:29
  564.0 4.8 collective-permute-start.6
  568.9 6.9 collective-permute-start.7
  618.1 3.1 collective-permute-start.8
  621.4 3.9 collective-permute-start.9
  763.6 4.8 collective-permute-start.10
  768.5 6.2 collective-permute-start.11
  822.9 3.1 collective-permute-start.12
  826.2 3.0 collective-permute-start.13
  829.2 0.9 copy-start.3
  966.6 4.8 collective-permute-start.14
  971.5 5.7 collective-permute-start.15
  1028.3 3.1 collective-permute-start.16
  1033.9 2.8 collective-permute-start.17
  1037.5 0.9 copy-start.2
where the time goes:
time: 1130 us; the launch traced here: 1120 us
  blocking collectives  333 us (29%)
  local copies, waits for them, and re-layouts  262 us (23%)
  other arithmetic  222 us (20%)
  matrix products  205 us (18%)
  starting transfers between devices  45.8 us (4%)
  waiting for transfers between devices  24.7 us (2%)
  loops' own time  14.8 us (1%)
    psum x3, blocking collectives, squares(): return lax.psum(jnp.sum(vector * vector), ('gx', 'gy'))  197 us
    psum x2, blocking collectives, per_device(): step_size = norm_now / lax.psum(jnp.sum(direction * image), ('gx', 'gy'))  136 us
    dot_general x4, matrix products, block_terms(): jnp.einsum('bdv,bev->bde', weighted, jacobian, preferred_element_type=jnp...  108 us
    dot_general x4, matrix products, block_terms(): jnp.einsum('bdv,bv->bd', weighted, resid_rows, preferred_element_type=jnp...  83.3 us
    squeeze x32, local copies, waits for them, and re-layouts, collect(): parts[node]  78.3 us
    unnamed x16, other arithmetic  51.3 us
    reduce_sum x1, other arithmetic, per_device(): elem_hess = hessian.reshape(elements, 4, 24, 24).sum(axis=1)  41.1 us
    ppermute x14, starting transfers between devices, from_behind(): return lax.ppermute(block, axis, route)  33.4 us
  transfers between devices with their start and end apart: 18, of which 14 were waited for; matrix products, arithmetic and copies ran while one was open for 10% of the time, Pallas kernels for 0%

commit v1 on v0

v1 whole, which is shorter than its diff:
```python
import functools

import numpy as np

import jax
import jax.numpy as jnp
from jax import lax
from jax.experimental import pallas as pl
from jax.experimental.pallas import tpu as pltpu
from jax.sharding import PartitionSpec as P

F32 = jnp.float32
BF16 = jnp.bfloat16
TX, TY, TZ = 16, 32, 4
ROWS = TX * TY
COL = TZ * 512
PITCH = 40
GRID = 1024
HROWS = 112
TIKHONOV = 8.0
SCALE = 2.0**-8
PAIRS = [(0, 0), (0, 1), (0, 2), (1, 1), (1, 2), (2, 2)]
DOTS = [(0, 0), (0, 1), (0, 2), (0, 3), (1, 1), (1, 2), (1, 3), (2, 2), (2, 3)]
VMEM_LIMIT = 56 * 1024 * 1024


def voxel_factors():
    v = np.arange(512)
    coords = [(v // 64 + 0.5) / 8.0, (v // 8 % 8 + 0.5) / 8.0, (v % 8 + 0.5) / 8.0]
    return [(1.0 - t, t) for t in coords]


def hessian_table():
    s = voxel_factors()
    q = [(a * a, a * b, b * b) for a, b in s]
    table = np.zeros((HROWS, TZ, 512))
    for tj in range(3):
        for tl in range(3):
            for ti in range(3):
                t = (tj * 3 + tl) * 3 + ti
                for ez in range(TZ):
                    table[4 * t + ez, ez] = q[0][ti] * q[1][tj] * q[2][tl]
    return table.reshape(HROWS, COL).astype(jnp.bfloat16)


def load_table():
    s = voxel_factors()
    table = np.zeros((32, TZ, 512), np.float32)
    for j in range(2):
        for l in range(2):
            for i in range(2):
                for ez in range(TZ):
                    table[(j * 2 + l) * 8 + i * 4 + ez, ez] = s[0][i] * s[1][j] * s[2][l]
    table = table.reshape(32, COL)
    high = table.astype(jnp.bfloat16)
    low = (table - high.astype(np.float32)).astype(jnp.bfloat16)
    return np.concatenate([high, low], axis=0)


def edge_maps(low, high, xlo_lanes, xhi_lanes):
    ysend, ycoord = [], []
    for x in range(TX):
        for k in range(low):
            ysend.append(x * TY + TY - low + k)
            ycoord.append((x, k - low))
    for x in range(TX):
        for k in range(high):
            ysend.append(x * TY + k)
            ycoord.append((x, TY + k))
    lane_of = {c: n for n, c in enumerate(ycoord)}

    def strip(first, count, base):
        lanes, coord = [], []
        for x in range(first, first + count):
            for y in range(TY):
                lanes.append(x * TY + y)
                coord.append((x + base, y))
        for ys in (range(-low, 0), range(TY, TY + high)):
            for x in range(first, first + count):
                for y in ys:
                    lanes.append(ROWS + lane_of[(x, y)])
                    coord.append((x + base, y))
        return lanes, coord

    up, up_coord = strip(TX - low, low, -TX)
    down, down_coord = strip(0, high, TX)
    source = {}
    for x in range(TX):
        for y in range(TY):
            source[(x, y)] = x * TY + y
    for n, c in enumerate(ycoord):
        source[c] = ROWS + n
    for n, c in enumerate(up_coord):
        source[c] = ROWS + 128 + n
    for n, c in enumerate(down_coord):
        source[c] = ROWS + 128 + xlo_lanes + n
    grid = np.full((GRID,), -1)
    for (x, y), lane in source.items():
        grid[(x + 4) * PITCH + y + 4] = lane

    def row(values, lanes):
        out = np.full((1, lanes), -1, np.int32)
        out[0, : len(values)] = values
        return out

    xsend = np.concatenate([row(up, xlo_lanes), row(down, xhi_lanes)], axis=1)
    return row(ysend, 128), xsend, row(list(grid), GRID), low * TX


H_YSEND, H_XSEND, H_GRID, H_YLOW = edge_maps(3, 2, 128, 128)
L_YSEND, L_XSEND, L_GRID, L_YLOW = edge_maps(4, 3, 256, 128)
OWN_MAP = np.array(
    [[(x + 4) * PITCH + y + 4 for x in range(TX) for y in range(TY)]], np.int32
)


def onehot(index_row, depth):
    lanes = index_row.shape[1]
    rows = lax.broadcasted_iota(jnp.int32, (depth, lanes), 0)
    return jnp.where(rows == index_row, 1.0, 0.0).astype(BF16)


def select_lanes(value, choice, parts):
    total = None
    rest = value
    for part in range(parts):
        piece = rest.astype(BF16)
        term = jnp.dot(piece, choice, preferred_element_type=F32)
        total = term if total is None else total + term
        if part + 1 < parts:
            rest = rest - piece.astype(F32)
    return total


def matmul_nt(a, b):
    return lax.dot_general(a, b, (((1,), (1,)), ((), ())), preferred_element_type=F32)


def hessian_kernel(g_ref, m_ref, table_ref, index_ref, c_ref, cy_ref):
    step = pl.program_id(0)
    mask = m_ref[...].astype(F32).astype(BF16)
    for k, (c, d) in enumerate(PAIRS):
        x = (g_ref[c] * mask) * g_ref[d]
        c_ref[k * HROWS : (k + 1) * HROWS, :] = matmul_nt(table_ref[...], x)
    choice = onehot(index_ref[...] - step * 256, 256)
    part = select_lanes(c_ref[...], choice, 2)

    @pl.when(step == 0)
    def _():
        cy_ref[...] = part

    @pl.when(step > 0)
    def _():
        cy_ref[...] += part


def edge_kernel(ylow, own_ref, below_ref, above_ref, index_ref, y_ref, up_ref, down_ref):
    lane = lax.broadcasted_iota(jnp.int32, below_ref.shape, 1)
    ytile = jnp.where(lane < ylow, below_ref[...], above_ref[...])
    y_ref[...] = ytile
    source = jnp.concatenate([own_ref[...], ytile], axis=1)
    sent = select_lanes(source, onehot(index_ref[...], ROWS + 128), 2)
    ups = up_ref.shape[1]
    up_ref[...] = sent[:, :ups]
    down_ref[...] = sent[:, ups:]


def grid_kernel(own_ref, y_ref, xlo_ref, xhi_ref, index_ref, out_ref):
    source = jnp.concatenate([own_ref[...], y_ref[...], xlo_ref[...], xhi_ref[...]], axis=1)
    placed = select_lanes(source, onehot(index_ref[...], source.shape[1]), 2)
    for tile in range(GRID // 128):
        out_ref[tile] = placed[:, tile * 128 : (tile + 1) * 128]


def sample_slot(x, y):
    ymid = (y >= 0) & (y < TY)
    ylo = y < 0
    xmid = (x >= 0) & (x < TX)
    xlo = x < 0
    own = x * TY + y
    below = 512 + (x + 4) * TY + y
    above = 640 + (x - TX) * TY + y
    mid = jnp.where(xmid, own, jnp.where(xlo, below, above))
    left = jnp.where(
        xmid,
        800 + x * 4 + y + 4,
        jnp.where(xlo, 928 + (x + 4) * 4 + y + 4, 960 + (x - TX) * 4 + y + 4),
    )
    right = jnp.where(
        xmid,
        864 + x * 4 + y - TY,
        jnp.where(xlo, 944 + (x + 4) * 4 + y - TY, 992 + (x - TX) * 4 + y - TY),
    )
    return jnp.where(ymid, mid, jnp.where(ylo, left, right))


GHOST_AT = (0, 128, 288, 352, 416, 432, 448, 480)
GHOST_ROWS = (128, 160, 64, 64, 16, 16, 20, 20)


def warp_kernel(
    s_ref, w_ref, m_ref, g_ref, d_ref, p0, p1, p2, p3, p4, p5, p6, p7,
    o_ref, table_ref, index_ref, l_ref, ly_ref, ghost, image,
):
    ez = pl.program_id(0)
    ghost[448:512, :] = jnp.zeros((64, 512), BF16)
    for at, rows, piece in zip(GHOST_AT, GHOST_ROWS, (p0, p1, p2, p3, p4, p5, p6, p7)):
        ghost[at : at + rows, :] = piece[...]
    pick = lax.broadcasted_iota(jnp.int32, (ROWS, TZ), 1) == ez
    ox = jnp.sum(jnp.where(pick, o_ref[0], 0), axis=1, keepdims=True)
    oy = jnp.sum(jnp.where(pick, o_ref[1], 0), axis=1, keepdims=True)
    pos = lax.broadcasted_iota(jnp.int32, (ROWS, 1), 0)
    x = (pos >> 5) + ox
    y = (pos & 31) + oy
    near_slot = sample_slot(x, y)
    far_slot = sample_slot(x + 1, y)
    chunk = 256
    for first in range(0, ROWS, chunk):
        rows = slice(first, first + chunk)
        slot = jnp.concatenate([near_slot[rows], far_slot[rows]], axis=0)
        lane = lax.broadcasted_iota(jnp.int32, (2 * chunk, 512), 1)
        own = jnp.where(lane == slot, 1.0, 0.0).astype(BF16)
        other = jnp.where(lane + 512 == slot, 1.0, 0.0).astype(BF16)
        both = jnp.dot(own, d_ref[...], preferred_element_type=F32) + jnp.dot(
            other, ghost[...], preferred_element_type=F32
        )
        w = w_ref[rows, :].astype(F32)
        warped = w * both[:chunk] + (1.0 - w) * both[chunk:]
        resid = (s_ref[rows, :].astype(F32) - warped).astype(BF16)
        weighted = resid * m_ref[rows, :].astype(F32).astype(BF16)
        for c in range(3):
            image[c, rows, :] = g_ref[c, rows, :] * weighted

    @pl.when(ez == 0)
    def _():
        l_ref[...] = jnp.zeros_like(l_ref)

    for c in range(3):
        part = matmul_nt(table_ref[...], image[c])
        l_ref[c * 32 : (c + 1) * 32, :] += part[:32] + part[32:]

    @pl.when(ez == TZ - 1)
    def _():
        ly_ref[...] = select_lanes(l_ref[...], onehot(index_ref[...], ROWS), 2)


def powers_kernel(
    edge_ref, own_ref, y_ref, xlo_ref, xhi_ref, index_ref, coord_ref, own_index_ref, h_ref,
    v_ref, dots_ref, us, fs,
):
    row = lax.broadcasted_iota(jnp.int32, (8, GRID), 0)
    beyond_x = (coord_ref[0:1, :] >= TX) & (edge_ref[0] == 1)
    beyond_y = (coord_ref[1:2, :] >= TY) & (edge_ref[1] == 1)
    live = jnp.where(beyond_x | beyond_y, 0.0, 1.0)

    def scatter(f):
        out = []
        for c in range(3):
            sums = []
            for l in range(2):
                both = f(0, l, c) + pltpu.roll(f(1, l, c), 1, axis=1)
                split = jnp.where(row < 4, both, pltpu.roll(both, PITCH, axis=1))
                sums.append(split + pltpu.roll(split, 4, axis=0))
            a, b = sums
            lower = a + jnp.where((row & 3) == 0, 0.0, pltpu.roll(b, 1, axis=0))
            upper = b + jnp.where((row & 3) == 3, 0.0, pltpu.roll(a, 7, axis=0))
            out.append((lower * live, upper * live))
        return out

    def apply(u):
        for i in range(2):
            for j in range(2):
                shift = i * PITCH + j
                for d in range(3):
                    for l in range(2):
                        value = u[d][l]
                        if shift:
                            value = pltpu.roll(value, GRID - shift, axis=1)
                        us[((i * 2 + j) * 3 + d) * 2 + l] = value

        def tile_step(tile, carry):
            lanes = pl.ds(pl.multiple_of(tile * 128, 128), 128)
            uu = [us[k, :, lanes] for k in range(24)]
            acc = {}
            for k, (c, d) in enumerate(PAIRS):
                for tj in range(3):
                    for tl in range(3):
                        for i in range(2):
                            at = k * HROWS + (tj * 3 + tl) * 12 + i * 4
                            h = h_ref[tile, at : at + 8, :]
                            for mj in range(2):
                                nj = tj - mj
                                if nj not in (0, 1):
                                    continue
                                for ml in range(2):
                                    nl = tl - ml
                                    if nl not in (0, 1):
                                        continue
                                    for out_c, in_d in {(c, d), (d, c)}:
                                        term = h * uu[((i * 2 + mj) * 3 + in_d) * 2 + ml]
                                        key = (nj * 2 + nl) * 3 + out_c
                                        acc[key] = term if key not in acc else acc[key] + term
            for key in range(12):
                fs[key, :, lanes] = acc[key] * SCALE
            return carry

        lax.fori_loop(0, GRID // 128, tile_step, 0)
        return scatter(lambda j, l, c: fs[(j * 2 + l) * 3 + c])

    source = jnp.concatenate([own_ref[...], y_ref[...], xlo_ref[...], xhi_ref[...]], axis=1)
    loads = select_lanes(source, onehot(index_ref[...], source.shape[1]), 2)

    def load_rows(j, l, c):
        at = c * 32 + (j * 2 + l) * 8
        return loads[at : at + 8, :]

    vectors = [scatter(load_rows)]
    for _ in range(3):
        vectors.append(apply(vectors[-1]))
    pieces = []
    for vec in vectors:
        for lower, upper in vec:
            pieces.append(
                jnp.where(row < 4, lower, jnp.where(row == 4, pltpu.roll(upper, 1, axis=0), 0.0))
            )
    own = select_lanes(jnp.concatenate(pieces, axis=0), onehot(own_index_ref[...], GRID), 3)
    v_ref[...] = own
    lane = lax.broadcasted_iota(jnp.int32, (1, 128), 1)
    dots = jnp.zeros((1, 128), F32)
    for k, (a, b) in enumerate(DOTS):
        product = own[a * 24 : a * 24 + 24] * own[b * 24 : b * 24 + 24]
        total = jnp.sum(jnp.sum(product, axis=0, keepdims=True), axis=1, keepdims=True)
        dots = jnp.where(lane == k, total, dots)
    dots_ref[...] = jnp.broadcast_to(dots, dots_ref.shape)


def combine_kernel(v_ref, dots_ref, x_ref, r_ref):
    total = jnp.sum(dots_ref[...], axis=0, keepdims=True)
    gram = {}
    for k, (a, b) in enumerate(DOTS):
        gram[(a, b)] = gram[(b, a)] = total[:, k : k + 1]

    def inner(p, q):
        out = None
        for a, pa in p.items():
            for b, qb in q.items():
                term = pa * qb * gram[(a, b)]
                out = term if out is None else out + term
        return out

    def add(p, q, factor):
        out = dict(p)
        for a, qa in q.items():
            term = factor * qa
            out[a] = out[a] + term if a in out else term
        return out

    one = jnp.ones((1, 1), F32)
    increment, resid, direction = {}, {0: one}, {0: one}
    norm_now = gram[(0, 0)]
    for sweep in range(3):
        image = {}
        for a, pa in direction.items():
            image[a] = image[a] + TIKHONOV * pa if a in image else TIKHONOV * pa
            image[a + 1] = pa * (1.0 / SCALE)
        step_size = norm_now / inner(direction, image)
        increment = add(increment, direction, step_size)
        resid = add(resid, image, -step_size)
        if sweep < 2:
            norm_next = inner(resid, resid)
            direction = add(resid, direction, norm_next / norm_now)
            norm_now = norm_next
    for ref, coefs in ((x_ref, increment), (r_ref, resid)):
        for c in range(3):
            out = None
            for k, coef in coefs.items():
                at = (k * 3 + c) * 8
                term = coef * v_ref[at : at + 8, :]
                out = term if out is None else out + term
            ref[c] = jnp.transpose(out, (1, 0))[:, :5]


def whole(shape):
    return pl.BlockSpec(shape, lambda *_: (0,) * len(shape))


def call(kernel, outs, *args, name):
    return pl.pallas_call(
        kernel,
        out_shape=outs,
        in_specs=[pl.BlockSpec(memory_space=pltpu.VMEM)] * len(args),
        out_specs=jax.tree.map(lambda _: pl.BlockSpec(memory_space=pltpu.VMEM), outs),
        compiler_params=pltpu.CompilerParams(vmem_limit_bytes=VMEM_LIMIT),
        name=name,
    )(*args)


def struct(*shape):
    return jax.ShapeDtypeStruct(shape, F32)


def shifted(value, dx, dy):
    nx, ny = lax.axis_size("gx"), lax.axis_size("gy")
    pairs = []
    for x in range(nx):
        for y in range(ny):
            if 0 <= x + dx < nx and 0 <= y + dy < ny:
                pairs.append((x * ny + y, (x + dx) * ny + y + dy))
    return lax.ppermute(value, ("gx", "gy"), pairs)


def exchange(own, ysend, xsend, ylow, widths, name):
    rows = own.shape[0]
    below, above = shifted(ysend, 0, 1), shifted(ysend, 0, -1)
    ytile, up, down = call(
        functools.partial(edge_kernel, ylow),
        (struct(rows, 128), struct(rows, widths[0]), struct(rows, widths[1])),
        own, below, above, jnp.asarray(xsend),
        name=name,
    )
    return ytile, shifted(up, 1, 0), shifted(down, -1, 0)


def per_device(
    reference_scan, ref_gradient, deformed_scan, interp_weights, sample_mask, block_list, offsets
):
    scan = reference_scan.reshape(ROWS, COL)
    grad = ref_gradient.reshape(3, ROWS, COL)
    weights = interp_weights.reshape(ROWS, COL)
    mask = sample_mask.reshape(ROWS, COL)
    moved = deformed_scan.reshape(ROWS, COL)
    ylast = deformed_scan[:, TY - 4 :, :].reshape(TX * 4, COL)
    yfirst = deformed_scan[:, :4, :].reshape(TX * 4, COL)
    pieces = (
        shifted(moved[384:], 1, 0),
        shifted(moved[:160], -1, 0),
        shifted(ylast, 0, 1),
        shifted(yfirst, 0, -1),
        shifted(ylast[48:], 1, 1),
        shifted(yfirst[48:], 1, -1),
        shifted(ylast[:20], -1, 1),
        shifted(yfirst[:20], -1, -1),
    )
    coefs, coefs_y = pl.pallas_call(
        hessian_kernel,
        out_shape=(struct(6 * HROWS, ROWS), struct(6 * HROWS, 128)),
        grid=(2,),
        in_specs=[
            pl.BlockSpec((3, 256, COL), lambda i: (0, i, 0)),
            pl.BlockSpec((256, COL), lambda i: (i, 0)),
            whole((HROWS, COL)),
            whole((1, 128)),
        ],
        out_specs=(pl.BlockSpec((6 * HROWS, 256), lambda i: (0, i)), whole((6 * HROWS, 128))),
        compiler_params=pltpu.CompilerParams(vmem_limit_bytes=VMEM_LIMIT),
        name="hessian",
    )(grad, mask, jnp.asarray(hessian_table()), jnp.asarray(H_YSEND))
    coefs_ghost = exchange(coefs, coefs_y, H_XSEND, H_YLOW, (128, 128), "hessian_edges")

    lanes = lambda rows: pl.BlockSpec((rows, 512), lambda i: (0, i))
    loads, loads_y = pl.pallas_call(
        warp_kernel,
        out_shape=(struct(96, ROWS), struct(96, 128)),
        grid=(TZ,),
        in_specs=[
            lanes(ROWS), lanes(ROWS), lanes(ROWS),
            pl.BlockSpec((3, ROWS, 512), lambda i: (0, 0, i)),
            lanes(ROWS),
            *[lanes(rows) for rows in GHOST_ROWS],
            whole((2, ROWS, TZ)),
            lanes(64),
            whole((1, 128)),
        ],
        out_specs=(whole((96, ROWS)), whole((96, 128))),
        scratch_shapes=[pltpu.VMEM((512, 512), BF16), pltpu.VMEM((3, ROWS, 512), BF16)],
        compiler_params=pltpu.CompilerParams(vmem_limit_bytes=VMEM_LIMIT),
        name="warp",
    )(
        scan, weights, mask, grad, moved, *pieces, offsets.reshape(2, ROWS, TZ),
        jnp.asarray(load_table()), jnp.asarray(L_YSEND),
    )
    loads_ghost = exchange(loads, loads_y, L_XSEND, L_YLOW, (256, 128), "load_edges")
    stiffness = call(
        grid_kernel, struct(GRID // 128, 6 * HROWS, 128), coefs, *coefs_ghost,
        jnp.asarray(H_GRID), name="hessian_grid",
    )

    position = np.arange(GRID)
    coord = np.stack([position // PITCH - 4, position % PITCH - 4]).astype(np.int32)
    last = jnp.stack(
        [lax.axis_index("gx") == lax.axis_size("gx") - 1, lax.axis_index("gy") == lax.axis_size("gy") - 1]
    ).astype(jnp.int32)
    vmem = pl.BlockSpec(memory_space=pltpu.VMEM)
    devices = lax.axis_size("gx") * lax.axis_size("gy")
    vectors, dots = pl.pallas_call(
        powers_kernel,
        out_shape=(struct(96, ROWS), struct(devices, 128)),
        in_specs=[pl.BlockSpec(memory_space=pltpu.SMEM)] + [vmem] * 8,
        out_specs=(vmem, vmem),
        scratch_shapes=[pltpu.VMEM((24, 8, GRID), F32), pltpu.VMEM((12, 8, GRID), F32)],
        compiler_params=pltpu.CompilerParams(vmem_limit_bytes=VMEM_LIMIT),
        name="powers",
    )(
        last, loads, *loads_ghost, jnp.asarray(L_GRID), jnp.asarray(coord),
        jnp.asarray(OWN_MAP), stiffness,
    )
    dots = lax.all_to_all(dots, ("gx", "gy"), 0, 0, tiled=True)
    increment, resid = call(
        combine_kernel, (struct(3, ROWS, 5), struct(3, ROWS, 5)), vectors, dots, name="combine"
    )
    return (increment.reshape(3, TX, TY, 5), resid.reshape(3, TX, TY, 5))


def solution(mesh):
    return jax.shard_map(
        per_device,
        mesh=mesh,
        in_specs=(
            P("gx", "gy", None),
            P(None, "gx", "gy", None),
            P("gx", "gy", None),
            P("gx", "gy", None),
            P("gx", "gy", None),
            P("gx", "gy"),
            P(None, "gx", "gy", None),
        ),
        out_specs=(P(None, "gx", "gy", None), P(None, "gx", "gy", None)),
        check_vma=False,
    )
```

time: 1130 us -> 137 us (0.12); the launches traced: 1120 us -> 136 us
  blocking collectives: 333 us -> 21.3 us
  local copies, waits for them, and re-layouts: 262 us -> 12.1 us
  other arithmetic: 222 us -> 0.61 us
  matrix products: 205 us -> 0 us
  Pallas kernels: 0 us -> 46.7 us
  waiting for transfers between devices: 24.7 us -> 4.21 us
  loops' own time: 14.8 us -> 0 us
    psum x5 -> x0, blocking collectives: 333 us -> none  [the longest x3 197 us: squares(): return lax.psum(jnp.sum(vector * vector), ('gx', 'gy'))]
    dot_general x12 -> x0, matrix products: 205 us -> none  [the longest x4 108 us: block_terms(): jnp.einsum('bdv,bev->bde', weighted, jacobian, preferred_element_type=jnp...]
    squeeze x36 -> x0, local copies, waits for them, and re-layouts: 78.5 us -> none  [the longest x32 78.3 us: collect(): parts[node]]
    reduce_sum x7 -> x0, other arithmetic: 57 us -> none  [the longest x1 41.1 us: per_device(): elem_hess = hessian.reshape(elements, 4, 24, 24).sum(axis=1)]
    gather x2 -> x0, local copies, waits for them, and re-layouts: 52.5 us -> none  [the longest x1 26.3 us: per_device(): far = flat_scan[source + span_y, layer].astype(jnp.float32)]
    unnamed x16 -> x0, other arithmetic: 51.3 us -> none
    pallas_call x0 -> x7, Pallas kernels: none -> 46.7 us  [the longest x1 15.6 us: per_device(): pl.pallas_call(warp_kernel, out_shape=(struct(96, ROWS), struct(96, 128))...]
    reshape x5 -> x2, local copies, waits for them, and re-layouts: 41.6 us -> 0.13 us  [the longest x1 0.07 us: per_device(): ylast = deformed_scan[:, TY - 4:, :].reshape(TX * 4, COL)]
  transfers between devices with their start and end apart: 18 -> 16, of which waited for: 14 -> 2; matrix products, arithmetic and copies ran while one was open for 10% -> 4% of each run, Pallas kernels for 0% -> 20%
where the time goes in v1:
time: 137 us; the launch traced here: 136 us
  starting transfers between devices  49.9 us (36%)
  Pallas kernels  46.7 us (34%)
  blocking collectives  21.3 us (16%)
  local copies, waits for them, and re-layouts  12.1 us (9%)
  waiting for transfers between devices  4.21 us (3%)
    ppermute x16, starting transfers between devices, shifted(): return lax.ppermute(value, ('gx', 'gy'), pairs)  49.9 us
    all_to_all x1, blocking collectives, per_device(): dots = lax.all_to_all(dots, ('gx', 'gy'), 0, 0, tiled=True)  21.3 us
    pallas_call x1, Pallas kernels, per_device(): pl.pallas_call(warp_kernel, out_shape=(struct(96, ROWS), struct(96, 128))...  15.6 us
    pallas_call x4, Pallas kernels, call(): pl.pallas_call(kernel, out_shape=outs, in_specs=[pl.BlockSpec(memory_spac...  13.9 us
    unnamed x31, local copies, waits for them, and re-layouts  9.81 us
    pallas_call x1, Pallas kernels, per_device(): pl.pallas_call(hessian_kernel, out_shape=(struct(6 * HROWS, ROWS), struct...  8.63 us
    pallas_call x1, Pallas kernels, per_device(): pl.pallas_call(powers_kernel, out_shape=(struct(96, ROWS), struct(devices...  8.55 us
    ppermute x16, waiting for transfers between devices, shifted(): return lax.ppermute(value, ('gx', 'gy'), pairs)  4.21 us
  transfers between devices with their start and end apart: 16, of which 2 were waited for; matrix products, arithmetic and copies ran while one was open for 4% of the time, Pallas kernels for 20%

profile of v1, /device:TPU:1, one launch (start us, length us, event | category | flops | bytes accessed | tf_op | source)
XLA Modules:
  0.0 135.9 jit_solution(16299998259934953569)
XLA Ops:
  0.6 0.0 copy-start
  0.6 8.6 %hessian.1 = (f32[672,512]{1,0:T(8,128)}, f32[672,128]{1,0:T(8,128)}) custom-call(bf16[3,512,2048]{2,1,0:T(8,128)(2,1)} %bitcast.16, s32[512,2048]{1,0:T(8,128)} %bitcast.18, bf16[112,2048]{1,0:T(8,128)(2,1)} %constant.33.clone.table_ref, s32[1,128]{1,0:T(1,128)} %constant.34.clone.index_ref), custom_call_target="tpu_custom_call" | custom-call | tf_op jit(solution)/shard_map/hessian/pallas_call | solution.py:444
  9.3 4.6 %collective-permute-start.12 = (f32[672,128]{1,0:T(8,128)}, f32[672,128]{1,0:T(8,128)}, u32[]{:S(2)}, u32[]{:S(2)}) collective-permute-start(f32[672,128]{1,0:T(8,128)} %get-tuple-element.22), channel_id=1, source_target_pairs={{0,1},{1,2},{2,3},{3,4},{4,5},{5,6},{6,7},{8,9},{9,10},{10,11},{11... | collective-permute-start | bytes 1032200 | tf_op jit(solution)/shard_map/ppermute | solution.py:409
  13.9 1.9 %collective-permute-start.13 = (f32[672,128]{1,0:T(8,128)}, f32[672,128]{1,0:T(8,128)}, u32[]{:S(2)}, u32[]{:S(2)}) collective-permute-start(f32[672,128]{1,0:T(8,128)} %get-tuple-element.22), channel_id=1, source_target_pairs={{1,0},{2,1},{3,2},{4,3},{5,4},{6,5},{7,6},{9,8},{10,9},{11,10},{12... | collective-permute-start | bytes 1032200 | tf_op jit(solution)/shard_map/ppermute | solution.py:409
  15.8 0.0 copy-done
  15.8 0.1 fusion.1
  15.9 5.0 %collective-permute-start.4 = (bf16[16,2048]{1,0:T(8,128)(2,1)S(1)}, bf16[16,2048]{1,0:T(8,128)(2,1)S(1)}, u32[]{:S(2)}, u32[]{:S(2)}) collective-permute-start(bf16[16,2048]{1,0:T(8,128)(2,1)S(1)} %slice.53), channel_id=1, source_target_pairs={{0,9},{1,10},{2,11},{3,12},{4,13},{5,14},{6,15},{8,17},{9,18},{10,... | collective-permute-start | bytes 196616 | tf_op jit(solution)/shard_map/ppermute | solution.py:409
  20.9 2.4 %collective-permute-start.5 = (bf16[16,2048]{1,0:T(8,128)(2,1)S(1)}, bf16[16,2048]{1,0:T(8,128)(2,1)S(1)}, u32[]{:S(2)}, u32[]{:S(2)}) collective-permute-start(bf16[16,2048]{1,0:T(8,128)(2,1)S(1)} %slice.55), channel_id=1, source_target_pairs={{1,8},{2,9},{3,10},{4,11},{5,12},{6,13},{7,14},{9,16},{10,17},{11,... | collective-permute-start | bytes 196616 | tf_op jit(solution)/shard_map/ppermute | solution.py:409
  23.3 0.1 fusion
  23.4 1.3 collective-permute-start.6
  24.7 0.9 slice.48
  25.6 0.8 slice.46
  26.4 0.0 collective-permute-done.4.p4
  26.4 1.3 collective-permute-start.1
  27.7 0.0 collective-permute-done.5.p5
  27.7 0.6 copy-done.10
  28.3 7.8 %collective-permute-start = (bf16[128,2048]{1,0:T(8,128)(2,1)}, bf16[128,2048]{1,0:T(8,128)(2,1)}, u32[]{:S(2)}, u32[]{:S(2)}) collective-permute-start(bf16[128,2048]{1,0:T(8,128)(2,1)} %bitcast.7), channel_id=1, source_target_pairs={{0,8},{1,9},{2,10},{3,11},{4,12},{5,13},{6,14},{7,15},{8,16},{9,17... | collective-permute-start | bytes 1572872 | tf_op jit(solution)/shard_map/ppermute | solution.py:409
  36.1 0.3 fusion.2
  36.4 0.1 reshape.47
  36.5 0.0 collective-permute-done.6.p6
  36.5 0.0 copy-start.6
  36.5 2.4 %collective-permute-start.2 = (bf16[64,2048]{1,0:T(8,128)(2,1)S(1)}, bf16[64,2048]{1,0:T(8,128)(2,1)S(1)}, u32[]{:S(2)}, u32[]{:S(2)}) collective-permute-start(bf16[64,2048]{1,0:T(8,128)(2,1)S(1)} %reshape.47), channel_id=1, source_target_pairs={{0,1},{1,2},{2,3},{3,4},{4,5},{5,6},{6,7},{8,9},{9,10},{10,11},{11... | collective-permute-start | bytes 786440 | tf_op jit(solution)/shard_map/ppermute | solution.py:409
  38.9 0.0 collective-permute-done.12.below_ref
  38.9 1.3 collective-permute-start.7
  40.2 0.1 reshape.48
  40.3 0.0 collective-permute-done.13.above_ref
  40.3 2.0 %collective-permute-start.3 = (bf16[64,2048]{1,0:T(8,128)(2,1)S(1)}, bf16[64,2048]{1,0:T(8,128)(2,1)S(1)}, u32[]{:S(2)}, u32[]{:S(2)}) collective-permute-start(bf16[64,2048]{1,0:T(8,128)(2,1)S(1)} %reshape.48), channel_id=1, source_target_pairs={{1,0},{2,1},{3,2},{4,3},{5,4},{6,5},{7,6},{9,8},{10,9},{11,10},{12... | collective-permute-start | bytes 786440 | tf_op jit(solution)/shard_map/ppermute | solution.py:409
  42.3 3.1 %hessian_edges.1 = (f32[672,128]{1,0:T(8,128)}, f32[672,128]{1,0:T(8,128)}, f32[672,128]{1,0:T(8,128)}) custom-call(f32[672,512]{1,0:T(8,128)} %get-tuple-element.21.own_ref, f32[672,128]{1,0:T(8,128)} %collective-permute-done.12.below_ref, f32[672,128]{1,0:T(8,128)} %collective-permute-done.13.above_ref, s32[1,256]{1,0:T(1,128)} %constant.35.clone.index_ref), custom_call_target="tpu_custom_call" | custom-call | tf_op jit(solution)/shard_map/hessian_edges/pallas_call | solution.py:388
  45.3 0.5 collective-permute-done.7.p7
  45.8 3.9 %collective-permute-start.14 = (f32[672,128]{1,0:T(8,128)}, f32[672,128]{1,0:T(8,128)S(1)}, u32[]{:S(2)}, u32[]{:S(2)}) collective-permute-start(f32[672,128]{1,0:T(8,128)} %get-tuple-element.24), channel_id=1, source_target_pairs={{0,8},{1,9},{2,10},{3,11},{4,12},{5,13},{6,14},{7,15},{8,16},{9,17... | collective-permute-start | bytes 1032200 | tf_op jit(solution)/shard_map/ppermute | solution.py:409
  49.8 0.0 collective-permute-done.2.p2
  49.8 1.3 collective-permute-start.15
  51.1 1.9 %copy.24 = s32[2,16,32,4]{3,2,1,0:T(8,128)} copy(s32[2,16,32,4]{2,3,1,0:T(4,128)} %param.22) | data formatting | bytes 32768 | tf_op args[6]
  53.0 0.0 collective-permute-done.3.p3
  53.0 0.0 collective-permute-done.p0
  53.0 0.0 collective-permute-done.1.p1
  53.0 0.6 copy-done.5
  53.7 0.2 copy-done.1
  53.9 15.6 %warp.1 = (f32[96,512]{1,0:T(8,128)}, f32[96,128]{1,0:T(8,128)}) custom-call(bf16[512,2048]{1,0:T(8,128)(2,1)} %bitcast.22, bf16[512,2048]{1,0:T(8,128)(2,1)} %bitcast.23, s32[512,2048]{1,0:T(8,128)} %bitcast.19, bf16[3,512,2048]{2,1,0:T(8,128)(2,1)} %bitcast.17, bf16[512,2048]{1,0:T(8,128)(2,1)} %bitcast.20, bf16[128,2048]{1,0:T(8,128)(2,1)} %collective-permute-done.p0, ...), custom_call_target="tpu_custom_call" | custom-call | tf_op jit(solution)/shard_map/warp/pallas_call | solution.py:461
  69.5 7.2 %collective-permute-start.8 = (f32[96,128]{1,0:T(8,128)}, f32[96,128]{1,0:T(8,128)S(1)}, u32[]{:S(2)}, u32[]{:S(2)}) collective-permute-start(f32[96,128]{1,0:T(8,128)} %get-tuple-element.17), channel_id=1, source_target_pairs={{0,1},{1,2},{2,3},{3,4},{4,5},{5,6},{6,7},{8,9},{9,10},{10,11},{11... | collective-permute-start | bytes 147464 | tf_op jit(solution)/shard_map/ppermute | solution.py:409
  76.7 1.9 %collective-permute-start.9 = (f32[96,128]{1,0:T(8,128)}, f32[96,128]{1,0:T(8,128)S(1)}, u32[]{:S(2)}, u32[]{:S(2)}) collective-permute-start(f32[96,128]{1,0:T(8,128)} %get-tuple-element.17), channel_id=1, source_target_pairs={{1,0},{2,1},{3,2},{4,3},{5,4},{6,5},{7,6},{9,8},{10,9},{11,10},{12... | collective-permute-start | bytes 147464 | tf_op jit(solution)/shard_map/ppermute | solution.py:409
  78.7 0.0 collective-permute-done.8.below_ref
  78.7 0.0 copy-start.11
  78.7 3.7 %collective-permute-done.9.above_ref = f32[96,128]{1,0:T(8,128)S(1)} collective-permute-done((f32[96,128]{1,0:T(8,128)}, f32[96,128]{1,0:T(8,128)S(1)}, u32[]{:S(2)}, u32[]{:S(2)}) %collective-permute-start.9) | collective-permute-done | bytes 49184 | tf_op jit(solution)/shard_map/ppermute | solution.py:409
  82.3 0.6 copy-done.12
  83.0 2.0 %load_edges.1 = (f32[96,128]{1,0:T(8,128)}, f32[96,256]{1,0:T(8,128)}, f32[96,128]{1,0:T(8,128)}) custom-call(f32[96,512]{1,0:T(8,128)} %get-tuple-element.16.own_ref, f32[96,128]{1,0:T(8,128)} %copy-done.11, f32[96,128]{1,0:T(8,128)} %copy-done.12, s32[1,384]{1,0:T(1,128)} %constant.38.clone.index_ref), custom_call_target="tpu_custom_call" | custom-call | tf_op jit(solution)/shard_map/load_edges/pallas_call | solution.py:388
  84.9 4.2 %collective-permute-start.10 = (f32[96,256]{1,0:T(8,128)}, f32[96,256]{1,0:T(8,128)S(1)}, u32[]{:S(2)}, u32[]{:S(2)}) collective-permute-start(f32[96,256]{1,0:T(8,128)} %get-tuple-element.19), channel_id=1, source_target_pairs={{0,8},{1,9},{2,10},{3,11},{4,12},{5,13},{6,14},{7,15},{8,16},{9,17... | collective-permute-start | bytes 294920 | tf_op jit(solution)/shard_map/ppermute | solution.py:409
  89.2 1.5 %collective-permute-start.11 = (f32[96,128]{1,0:T(8,128)}, f32[96,128]{1,0:T(8,128)S(1)}, u32[]{:S(2)}, u32[]{:S(2)}) collective-permute-start(f32[96,128]{1,0:T(8,128)} %get-tuple-element.20), channel_id=1, source_target_pairs={{8,0},{9,1},{10,2},{11,3},{12,4},{13,5},{14,6},{15,7},{16,8},{17,9... | collective-permute-start | bytes 147464 | tf_op jit(solution)/shard_map/ppermute | solution.py:409
  90.7 0.6 add_convert_fusion.edge_ref
  91.3 0.0 collective-permute-done.14.xlo_ref
  91.3 0.0 collective-permute-done.15.xhi_ref
  91.3 0.7 copy-done.2
  92.0 0.1 copy-done.3
  92.2 6.3 %hessian_grid.1.h_ref = f32[8,672,128]{2,1,0:T(8,128)} custom-call(f32[672,512]{1,0:T(8,128)} %get-tuple-element.21.own_ref, f32[672,128]{1,0:T(8,128)} %get-tuple-element.23.y_ref, f32[672,128]{1,0:T(8,128)} %copy-done.2, f32[672,128]{1,0:T(8,128)} %copy-done.3, s32[1,1024]{1,0:T(1,128)} %constant.39.clone.index_ref), custom_call_target="tpu_custom_call" | custom-call | tf_op jit(solution)/shard_map/hessian_grid/pallas_call | solution.py:388
  98.4 0.0 collective-permute-done.11.xhi_ref
  98.4 0.0 collective-permute-done.10.xlo_ref
  98.4 0.0 copy-start.8
  98.5 0.6 copy-done.13
  99.1 0.0 copy-done.8
  99.1 8.5 %powers.1 = (f32[96,512]{1,0:T(8,128)}, f32[128,128]{1,0:T(8,128)}) custom-call(s32[2]{0:T(128)} %add_convert_fusion.edge_ref, f32[96,512]{1,0:T(8,128)} %get-tuple-element.16.own_ref, f32[96,128]{1,0:T(8,128)} %get-tuple-element.18.y_ref, f32[96,256]{1,0:T(8,128)} %copy-done.8, f32[96,128]{1,0:T(8,128)} %copy-done.13, s32[1,1024]{1,0:T(1,128)} %constant.40.clone.index_ref, ...), custom_call_target="tpu_custom_call" | custom-call | tf_op jit(solution)/shard_map/powers/pallas_call | solution.py:495
  107.6 21.3 %all_to_all.11 = f32[128,1,128]{2,1,0:T(1,128)} all-to-all(f32[128,1,128]{2,1,0:T(1,128)} %bitcast.27), channel_id=1, replica_groups=mesh['gx'=16,'gy'=8] {'gx','gy'}, dimensions={0} | all-to-all | bytes 131072 | tf_op jit(solution)/shard_map/all_to_all | solution.py:507
  128.9 2.6 %combine.1 = (f32[3,512,5]{2,1,0:T(8,128)}, f32[3,512,5]{2,1,0:T(8,128)}) custom-call(f32[96,512]{1,0:T(8,128)} %get-tuple-element.26.v_ref, f32[128,128]{1,0:T(8,128)} %bitcast.26), custom_call_target="tpu_custom_call" | custom-call | tf_op jit(solution)/shard_map/combine/pallas_call | solution.py:388
  131.5 2.2 %copy.26 = f32[3,16,32,5]{2,1,3,0:T(8,128)} copy(f32[3,16,32,5]{3,2,1,0:T(8,128)} %bitcast.25) | data formatting | bytes 61440
  133.7 2.2 %copy.27 = f32[3,16,32,5]{2,1,3,0:T(8,128)} copy(f32[3,16,32,5]{3,2,1,0:T(8,128)} %bitcast.24) | data formatting | bytes 61440
  (19 shorter events, 0.1 us)
Async XLA Ops:
  0.6 15.2 %copy-start = (bf16[16,32,2048]{2,1,0:T(8,128)(2,1)S(1)}, bf16[16,32,2048]{2,1,0:T(8,128)(2,1)}, u32[]{:S(2)}) copy-start(bf16[16,32,2048]{2,1,0:T(8,128)(2,1)} %param.19) | copy-start | bytes 6291460
  9.3 29.6 %collective-permute-start.12 = (f32[672,128]{1,0:T(8,128)}, f32[672,128]{1,0:T(8,128)}, u32[]{:S(2)}, u32[]{:S(2)}) collective-permute-start(f32[672,128]{1,0:T(8,128)} %get-tuple-element.22), channel_id=1, source_target_pairs={{0,1},{1,2},{2,3},{3,4},{4,5},{5,6},{6,7},{8,9},{9,10},{10,11},{11... | collective-permute-start | bytes 1032200 | tf_op jit(solution)/shard_map/ppermute | solution.py:409
  13.9 26.4 %collective-permute-start.13 = (f32[672,128]{1,0:T(8,128)}, f32[672,128]{1,0:T(8,128)}, u32[]{:S(2)}, u32[]{:S(2)}) collective-permute-start(f32[672,128]{1,0:T(8,128)} %get-tuple-element.22), channel_id=1, source_target_pairs={{1,0},{2,1},{3,2},{4,3},{5,4},{6,5},{7,6},{9,8},{10,9},{11,10},{12... | collective-permute-start | bytes 1032200 | tf_op jit(solution)/shard_map/ppermute | solution.py:409
  15.9 10.5 %collective-permute-start.4 = (bf16[16,2048]{1,0:T(8,128)(2,1)S(1)}, bf16[16,2048]{1,0:T(8,128)(2,1)S(1)}, u32[]{:S(2)}, u32[]{:S(2)}) collective-permute-start(bf16[16,2048]{1,0:T(8,128)(2,1)S(1)} %slice.53), channel_id=1, source_target_pairs={{0,9},{1,10},{2,11},{3,12},{4,13},{5,14},{6,15},{8,17},{9,18},{10,... | collective-permute-start | bytes 196616 | tf_op jit(solution)/shard_map/ppermute | solution.py:409
  20.9 6.8 %collective-permute-start.5 = (bf16[16,2048]{1,0:T(8,128)(2,1)S(1)}, bf16[16,2048]{1,0:T(8,128)(2,1)S(1)}, u32[]{:S(2)}, u32[]{:S(2)}) collective-permute-start(bf16[16,2048]{1,0:T(8,128)(2,1)S(1)} %slice.55), channel_id=1, source_target_pairs={{1,8},{2,9},{3,10},{4,11},{5,12},{6,13},{7,14},{9,16},{10,17},{11,... | collective-permute-start | bytes 196616 | tf_op jit(solution)/shard_map/ppermute | solution.py:409
  23.4 13.1 %collective-permute-start.6 = (bf16[20,2048]{1,0:T(8,128)(2,1)S(1)}, bf16[20,2048]{1,0:T(8,128)(2,1)S(1)}, u32[]{:S(2)}, u32[]{:S(2)}) collective-permute-start(bf16[20,2048]{1,0:T(8,128)(2,1)S(1)} %slice.57), channel_id=1, source_target_pairs={{8,1},{9,2},{10,3},{11,4},{12,5},{13,6},{14,7},{16,9},{17,10},{18,... | collective-permute-start | bytes 245768 | tf_op jit(solution)/shard_map/ppermute | solution.py:409
  26.4 1.3 copy-start.9
  26.4 26.6 %collective-permute-start.1 = (bf16[160,2048]{1,0:T(8,128)(2,1)}, bf16[160,2048]{1,0:T(8,128)(2,1)S(1)}, u32[]{:S(2)}, u32[]{:S(2)}) collective-permute-start(bf16[160,2048]{1,0:T(8,128)(2,1)} %bitcast.8), channel_id=1, source_target_pairs={{8,0},{9,1},{10,2},{11,3},{12,4},{13,5},{14,6},{15,7},{16,8},{17,9... | collective-permute-start | bytes 1966088 | tf_op jit(solution)/shard_map/ppermute | solution.py:409
  27.7 0.6 copy-start.10
  28.3 24.6 %collective-permute-start = (bf16[128,2048]{1,0:T(8,128)(2,1)}, bf16[128,2048]{1,0:T(8,128)(2,1)}, u32[]{:S(2)}, u32[]{:S(2)}) collective-permute-start(bf16[128,2048]{1,0:T(8,128)(2,1)} %bitcast.7), channel_id=1, source_target_pairs={{0,8},{1,9},{2,10},{3,11},{4,12},{5,13},{6,14},{7,15},{8,16},{9,17... | collective-permute-start | bytes 1572872 | tf_op jit(solution)/shard_map/ppermute | solution.py:409
  36.5 16.5 %copy-start.6 = (bf16[20,2048]{1,0:T(8,128)(2,1)}, bf16[20,2048]{1,0:T(8,128)(2,1)S(1)}, u32[]{:S(2)}) copy-start(bf16[20,2048]{1,0:T(8,128)(2,1)S(1)} %collective-permute-done.6.p6) | copy-start | bytes 245764
  36.5 13.3 %collective-permute-start.2 = (bf16[64,2048]{1,0:T(8,128)(2,1)S(1)}, bf16[64,2048]{1,0:T(8,128)(2,1)S(1)}, u32[]{:S(2)}, u32[]{:S(2)}) collective-permute-start(bf16[64,2048]{1,0:T(8,128)(2,1)S(1)} %reshape.47), channel_id=1, source_target_pairs={{0,1},{1,2},{2,3},{3,4},{4,5},{5,6},{6,7},{8,9},{9,10},{10,11},{11... | collective-permute-start | bytes 786440 | tf_op jit(solution)/shard_map/ppermute | solution.py:409
  38.9 6.9 %collective-permute-start.7 = (bf16[20,2048]{1,0:T(8,128)(2,1)S(1)}, bf16[20,2048]{1,0:T(8,128)(2,1)S(1)}, u32[]{:S(2)}, u32[]{:S(2)}) collective-permute-start(bf16[20,2048]{1,0:T(8,128)(2,1)S(1)} %slice.59), channel_id=1, source_target_pairs={{9,0},{10,1},{11,2},{12,3},{13,4},{14,5},{15,6},{17,8},{18,9},{19,... | collective-permute-start | bytes 245768 | tf_op jit(solution)/shard_map/ppermute | solution.py:409
  40.3 12.7 %collective-permute-start.3 = (bf16[64,2048]{1,0:T(8,128)(2,1)S(1)}, bf16[64,2048]{1,0:T(8,128)(2,1)S(1)}, u32[]{:S(2)}, u32[]{:S(2)}) collective-permute-start(bf16[64,2048]{1,0:T(8,128)(2,1)S(1)} %reshape.48), channel_id=1, source_target_pairs={{1,0},{2,1},{3,2},{4,3},{5,4},{6,5},{7,6},{9,8},{10,9},{11,10},{12... | collective-permute-start | bytes 786440 | tf_op jit(solution)/shard_map/ppermute | solution.py:409
  45.8 7.2 %copy-start.7 = (bf16[20,2048]{1,0:T(8,128)(2,1)}, bf16[20,2048]{1,0:T(8,128)(2,1)S(1)}, u32[]{:S(2)}) copy-start(bf16[20,2048]{1,0:T(8,128)(2,1)S(1)} %collective-permute-done.7.p7) | copy-start | bytes 245764
  45.8 45.5 %collective-permute-start.14 = (f32[672,128]{1,0:T(8,128)}, f32[672,128]{1,0:T(8,128)S(1)}, u32[]{:S(2)}, u32[]{:S(2)}) collective-permute-start(f32[672,128]{1,0:T(8,128)} %get-tuple-element.24), channel_id=1, source_target_pairs={{0,8},{1,9},{2,10},{3,11},{4,12},{5,13},{6,14},{7,15},{8,16},{9,17... | collective-permute-start | bytes 1032200 | tf_op jit(solution)/shard_map/ppermute | solution.py:409
  49.8 3.3 %copy-start.4 = (bf16[64,2048]{1,0:T(8,128)(2,1)}, bf16[64,2048]{1,0:T(8,128)(2,1)S(1)}, u32[]{:S(2)}) copy-start(bf16[64,2048]{1,0:T(8,128)(2,1)S(1)} %collective-permute-done.2.p2) | copy-start | bytes 786436
  49.8 41.5 %collective-permute-start.15 = (f32[672,128]{1,0:T(8,128)}, f32[672,128]{1,0:T(8,128)S(1)}, u32[]{:S(2)}, u32[]{:S(2)}) collective-permute-start(f32[672,128]{1,0:T(8,128)} %get-tuple-element.25), channel_id=1, source_target_pairs={{8,0},{9,1},{10,2},{11,3},{12,4},{13,5},{14,6},{15,7},{16,8},{17,9... | collective-permute-start | bytes 1032200 | tf_op jit(solution)/shard_map/ppermute | solution.py:409
  53.0 0.7 copy-start.5
  53.0 0.9 copy-start.1
  69.5 9.1 %collective-permute-start.8 = (f32[96,128]{1,0:T(8,128)}, f32[96,128]{1,0:T(8,128)S(1)}, u32[]{:S(2)}, u32[]{:S(2)}) collective-permute-start(f32[96,128]{1,0:T(8,128)} %get-tuple-element.17), channel_id=1, source_target_pairs={{0,1},{1,2},{2,3},{3,4},{4,5},{5,6},{6,7},{8,9},{9,10},{10,11},{11... | collective-permute-start | bytes 147464 | tf_op jit(solution)/shard_map/ppermute | solution.py:409
  76.7 5.6 %collective-permute-start.9 = (f32[96,128]{1,0:T(8,128)}, f32[96,128]{1,0:T(8,128)S(1)}, u32[]{:S(2)}, u32[]{:S(2)}) collective-permute-start(f32[96,128]{1,0:T(8,128)} %get-tuple-element.17), channel_id=1, source_target_pairs={{1,0},{2,1},{3,2},{4,3},{5,4},{6,5},{7,6},{9,8},{10,9},{11,10},{12... | collective-permute-start | bytes 147464 | tf_op jit(solution)/shard_map/ppermute | solution.py:409
  78.7 3.7 %copy-start.11 = (f32[96,128]{1,0:T(8,128)}, f32[96,128]{1,0:T(8,128)S(1)}, u32[]{:S(2)}) copy-start(f32[96,128]{1,0:T(8,128)S(1)} %collective-permute-done.8.below_ref) | copy-start | bytes 147460
  82.3 0.6 copy-start.12
  84.9 13.5 %collective-permute-start.10 = (f32[96,256]{1,0:T(8,128)}, f32[96,256]{1,0:T(8,128)S(1)}, u32[]{:S(2)}, u32[]{:S(2)}) collective-permute-start(f32[96,256]{1,0:T(8,128)} %get-tuple-element.19), channel_id=1, source_target_pairs={{0,8},{1,9},{2,10},{3,11},{4,12},{5,13},{6,14},{7,15},{8,16},{9,17... | collective-permute-start | bytes 294920 | tf_op jit(solution)/shard_map/ppermute | solution.py:409
  89.2 9.2 %collective-permute-start.11 = (f32[96,128]{1,0:T(8,128)}, f32[96,128]{1,0:T(8,128)S(1)}, u32[]{:S(2)}, u32[]{:S(2)}) collective-permute-start(f32[96,128]{1,0:T(8,128)} %get-tuple-element.20), channel_id=1, source_target_pairs={{8,0},{9,1},{10,2},{11,3},{12,4},{13,5},{14,6},{15,7},{16,8},{17,9... | collective-permute-start | bytes 147464 | tf_op jit(solution)/shard_map/ppermute | solution.py:409
  91.3 0.7 copy-start.2
  91.3 0.8 copy-start.3
  98.4 0.6 copy-start.13
  98.4 0.6 copy-start.8

commit v2 on v1

--- a/solution.py
+++ b/solution.py
@@ -17,11 +17,12 @@
 PITCH = 40
 GRID = 1024
 HROWS = 112
+CROWS = 6 * HROWS
 TIKHONOV = 8.0
 SCALE = 2.0**-8
 PAIRS = [(0, 0), (0, 1), (0, 2), (1, 1), (1, 2), (2, 2)]
 DOTS = [(0, 0), (0, 1), (0, 2), (0, 3), (1, 1), (1, 2), (1, 3), (2, 2), (2, 3)]
-VMEM_LIMIT = 56 * 1024 * 1024
+VMEM_LIMIT = 24 * 1024 * 1024
 
 
 def voxel_factors():
@@ -136,38 +137,80 @@
     return lax.dot_general(a, b, (((1,), (1,)), ((), ())), preferred_element_type=F32)
 
 
-def hessian_kernel(g_ref, m_ref, table_ref, index_ref, c_ref, cy_ref):
+def pack_y_kernel(end_ref, start_ref, last_ref, first_ref):
+    row = lax.broadcasted_iota(jnp.int32, (64, 128), 0)
+    pos = lax.broadcasted_iota(jnp.int32, (64, 128), 1)
+    for ref, out_ref, at in ((end_ref, last_ref, 4), (start_ref, first_ref, 0)):
+        choice = jnp.where(pos == (row >> 2) * 8 + (row & 3) + at, 1.0, 0.0).astype(BF16)
+        rows = ref[...].astype(F32).reshape(TX * 8, ref.shape[-1]).astype(BF16)
+        out_ref[...] = jnp.dot(choice, rows, preferred_element_type=F32).astype(BF16)
+
+
+def pack_x_kernel(d_ref, ylo_ref, yhi_ref, up_ref, down_ref, sems):
+    copies = []
+    for source, start, rows, target, at in (
+        (d_ref, 384, 128, up_ref, 0),
+        (ylo_ref, 48, 16, up_ref, 128),
+        (yhi_ref, 48, 16, up_ref, 144),
+        (d_ref, 0, 160, down_ref, 0),
+        (ylo_ref, 0, 24, down_ref, 160),
+        (yhi_ref, 0, 24, down_ref, 184),
+    ):
+        copies.append(
+            pltpu.make_async_copy(
+                source.at[pl.ds(start, rows)], target.at[pl.ds(at, rows)], sems.at[len(copies)]
+            )
+        )
+    for copy in copies:
+        copy.start()
+    for copy in copies:
+        copy.wait()
+
+
+def hessian_kernel(g_ref, m_ref, table_ref, yindex_ref, xindex_ref, c_ref, cy_ref, cx_ref):
     step = pl.program_id(0)
     mask = m_ref[...].astype(F32).astype(BF16)
     for k, (c, d) in enumerate(PAIRS):
         x = (g_ref[c] * mask) * g_ref[d]
-        c_ref[k * HROWS : (k + 1) * HROWS, :] = matmul_nt(table_ref[...], x)
-    choice = onehot(index_ref[...] - step * 256, 256)
-    part = select_lanes(c_ref[...], choice, 2)
-
-    @pl.when(step == 0)
-    def _():
-        cy_ref[...] = part
-
-    @pl.when(step > 0)
-    def _():
-        cy_ref[...] += part
-
-
-def edge_kernel(ylow, own_ref, below_ref, above_ref, index_ref, y_ref, up_ref, down_ref):
-    lane = lax.broadcasted_iota(jnp.int32, below_ref.shape, 1)
-    ytile = jnp.where(lane < ylow, below_ref[...], above_ref[...])
-    y_ref[...] = ytile
-    source = jnp.concatenate([own_ref[...], ytile], axis=1)
-    sent = select_lanes(source, onehot(index_ref[...], ROWS + 128), 2)
-    ups = up_ref.shape[1]
-    up_ref[...] = sent[:, :ups]
-    down_ref[...] = sent[:, ups:]
-
-
-def grid_kernel(own_ref, y_ref, xlo_ref, xhi_ref, index_ref, out_ref):
-    source = jnp.concatenate([own_ref[...], y_ref[...], xlo_ref[...], xhi_ref[...]], axis=1)
-    placed = select_lanes(source, onehot(index_ref[...], source.shape[1]), 2)
+        c_ref[k * HROWS : (k + 1) * HROWS, :] = matmul_nt(table_ref[...], x).astype(BF16)
+    for index_ref, ref in ((yindex_ref, cy_ref), (xindex_ref, cx_ref)):
+        choice = onehot(index_ref[...] - step * 256, 256)
+        part = jnp.dot(c_ref[...], choice, preferred_element_type=F32).astype(BF16)
+
+        @pl.when(step == 0)
+        def _():
+            ref[...] = part
+
+        @pl.when(step > 0)
+        def _():
+            ref[...] += part
+
+
+def edge_kernel(
+    l_ref, cx_ref, below_ref, above_ref, cindex_ref, lindex_ref, y_ref, up_ref, down_ref
+):
+    lane = lax.broadcasted_iota(jnp.int32, (1, 128), 1)
+    ytile_c = jnp.where(lane < H_YLOW, below_ref[:CROWS, :], above_ref[:CROWS, :])
+    ytile_l = jnp.where(lane < L_YLOW, below_ref[CROWS:, :], above_ref[CROWS:, :])
+    y_ref[:CROWS, :] = ytile_c
+    y_ref[CROWS:, :] = ytile_l
+    sent = jnp.dot(ytile_c, onehot(cindex_ref[...] - ROWS, 128), preferred_element_type=F32)
+    sent = sent.astype(BF16) + cx_ref[...]
+    up_ref[:CROWS, :] = sent[:, :128]
+    down_ref[:CROWS, :] = sent[:, 128:]
+    high = l_ref[...].astype(BF16)
+    low = (l_ref[...] - high.astype(F32)).astype(BF16)
+    source = jnp.concatenate([jnp.concatenate([high, low], axis=0), ytile_l], axis=1)
+    sent = jnp.dot(
+        source, onehot(lindex_ref[...], ROWS + 128), preferred_element_type=F32
+    ).astype(BF16)
+    up_ref[CROWS : CROWS + 192, :] = sent[:, :128]
+    up_ref[CROWS + 192 :, :] = sent[:, 128:256]
+    down_ref[CROWS:, :] = sent[:, 256:]
+
+
+def grid_kernel(own_ref, index_ref, out_ref):
+    placed = jnp.dot(own_ref[...], onehot(index_ref[...], ROWS), preferred_element_type=F32)
     for tile in range(GRID // 128):
         out_ref[tile] = placed[:, tile * 128 : (tile + 1) * 128]
 
@@ -177,59 +220,77 @@
     ylo = y < 0
     xmid = (x >= 0) & (x < TX)
     xlo = x < 0
-    own = x * TY + y
-    below = 512 + (x + 4) * TY + y
-    above = 640 + (x - TX) * TY + y
-    mid = jnp.where(xmid, own, jnp.where(xlo, below, above))
-    left = jnp.where(
-        xmid,
-        800 + x * 4 + y + 4,
-        jnp.where(xlo, 928 + (x + 4) * 4 + y + 4, 960 + (x - TX) * 4 + y + 4),
-    )
-    right = jnp.where(
-        xmid,
-        864 + x * 4 + y - TY,
-        jnp.where(xlo, 944 + (x + 4) * 4 + y - TY, 992 + (x - TX) * 4 + y - TY),
-    )
-    return jnp.where(ymid, mid, jnp.where(ylo, left, right))
-
-
-GHOST_AT = (0, 128, 288, 352, 416, 432, 448, 480)
-GHOST_ROWS = (128, 160, 64, 64, 16, 16, 20, 20)
+    mid = jnp.where(
+        xmid, x * TY + y, jnp.where(xlo, 512 + (x + 4) * TY + y, 672 + (x - TX) * TY + y)
+    )
+    left = jnp.where(xmid, 880 + x * 4, jnp.where(xlo, 640 + (x + 4) * 4, 832 + (x - TX) * 4))
+    right = jnp.where(xmid, 944 + x * 4, jnp.where(xlo, 656 + (x + 4) * 4, 856 + (x - TX) * 4))
+    return jnp.where(ymid, mid, jnp.where(ylo, left + y + 4, right + y - TY))
+
+
+def slot_columns(o_ref, ez):
+    layer = lax.broadcasted_iota(jnp.int32, (TX, TZ, TY), 1) == ez
+    ox, oy = (jnp.sum(jnp.where(layer, o_ref[axis], 0), axis=1) for axis in range(2))
+    x = lax.broadcasted_iota(jnp.int32, (TX, TY), 0) + ox
+    y = lax.broadcasted_iota(jnp.int32, (TX, TY), 1) + oy
+    near, far = sample_slot(x, y), sample_slot(x + 1, y)
+    parts = jnp.concatenate([near >> 7, near & 127, far >> 7, far & 127], axis=1)
+    row = lax.broadcasted_iota(jnp.int32, (ROWS, TX), 0)
+    col = lax.broadcasted_iota(jnp.int32, (ROWS, TX), 1)
+    spread = jnp.dot(
+        jnp.where(row >> 5 == col, 1.0, 0.0).astype(BF16),
+        parts.astype(F32).astype(BF16),
+        preferred_element_type=F32,
+    )
+    row = lax.broadcasted_iota(jnp.int32, (ROWS, 128), 0)
+    col = lax.broadcasted_iota(jnp.int32, (ROWS, 128), 1)
+    spread = jnp.where(row & 31 == col & 31, spread, 0.0).astype(BF16)
+    row = lax.broadcasted_iota(jnp.int32, (128, 512), 0)
+    col = lax.broadcasted_iota(jnp.int32, (128, 512), 1)
+    ones = jnp.where(row >> 5 == col >> 7, 1.0, 0.0).astype(BF16)
+    out = jnp.dot(spread, ones, preferred_element_type=F32).astype(BF16)
+    high = jnp.concatenate([out[:, :128], out[:, 256:384]], axis=0)
+    low = jnp.concatenate([out[:, 128:256], out[:, 384:]], axis=0)
+    return high, low
+
+
+def slot_onehot(high, low, first):
+    lane = lax.broadcasted_iota(jnp.int32, low.shape, 1).astype(F32).astype(BF16)
+    zero = jnp.zeros(low.shape, BF16)
+    hit = jnp.where(low == lane, jnp.ones(low.shape, BF16), zero)
+    return jnp.concatenate([jnp.where(high == float(first + k), hit, zero) for k in range(4)], axis=1)
+
+
+GHOST_AT = (0, 160, 368, 432)
+GHOST_ROWS = (160, 208, 64, 64)
+
+
+def own_samples_kernel(d_ref, o_ref, out_ref):
+    ez = pl.program_id(0)
+    high, low = slot_columns(o_ref, ez)
+    out_ref[...] = jnp.dot(
+        slot_onehot(high, low, 0), d_ref[...], preferred_element_type=F32
+    ).astype(BF16)
 
 
 def warp_kernel(
-    s_ref, w_ref, m_ref, g_ref, d_ref, p0, p1, p2, p3, p4, p5, p6, p7,
-    o_ref, table_ref, index_ref, l_ref, ly_ref, ghost, image,
+    s_ref, w_ref, m_ref, g_ref, n_ref, p0, p1, p2, p3, o_ref, table_ref, index_ref, cy_ref,
+    l_ref, msg_ref, ghost, image,
 ):
     ez = pl.program_id(0)
-    ghost[448:512, :] = jnp.zeros((64, 512), BF16)
-    for at, rows, piece in zip(GHOST_AT, GHOST_ROWS, (p0, p1, p2, p3, p4, p5, p6, p7)):
+    ghost[496:512, :] = jnp.zeros((16, 512), BF16)
+    for at, rows, piece in zip(GHOST_AT, GHOST_ROWS, (p0, p1, p2, p3)):
         ghost[at : at + rows, :] = piece[...]
-    pick = lax.broadcasted_iota(jnp.int32, (ROWS, TZ), 1) == ez
-    ox = jnp.sum(jnp.where(pick, o_ref[0], 0), axis=1, keepdims=True)
-    oy = jnp.sum(jnp.where(pick, o_ref[1], 0), axis=1, keepdims=True)
-    pos = lax.broadcasted_iota(jnp.int32, (ROWS, 1), 0)
-    x = (pos >> 5) + ox
-    y = (pos & 31) + oy
-    near_slot = sample_slot(x, y)
-    far_slot = sample_slot(x + 1, y)
-    chunk = 256
-    for first in range(0, ROWS, chunk):
-        rows = slice(first, first + chunk)
-        slot = jnp.concatenate([near_slot[rows], far_slot[rows]], axis=0)
-        lane = lax.broadcasted_iota(jnp.int32, (2 * chunk, 512), 1)
-        own = jnp.where(lane == slot, 1.0, 0.0).astype(BF16)
-        other = jnp.where(lane + 512 == slot, 1.0, 0.0).astype(BF16)
-        both = jnp.dot(own, d_ref[...], preferred_element_type=F32) + jnp.dot(
-            other, ghost[...], preferred_element_type=F32
-        )
-        w = w_ref[rows, :].astype(F32)
-        warped = w * both[:chunk] + (1.0 - w) * both[chunk:]
-        resid = (s_ref[rows, :].astype(F32) - warped).astype(BF16)
-        weighted = resid * m_ref[rows, :].astype(F32).astype(BF16)
-        for c in range(3):
-            image[c, rows, :] = g_ref[c, rows, :] * weighted
+    high, low = slot_columns(o_ref, ez)
+    both = jnp.dot(
+        slot_onehot(high, low, 4), ghost[...], preferred_element_type=F32
+    ) + n_ref[...].astype(F32)
+    w = w_ref[...].astype(F32)
+    warped = w * both[:ROWS] + (1.0 - w) * both[ROWS:]
+    resid = (s_ref[...].astype(F32) - warped).astype(BF16)
+    weighted = resid * m_ref[...].astype(F32).astype(BF16)
+    for c in range(3):
+        image[c] = g_ref[c] * weighted
 
     @pl.when(ez == 0)
     def _():
@@ -241,12 +302,19 @@
 
     @pl.when(ez == TZ - 1)
     def _():
-        ly_ref[...] = select_lanes(l_ref[...], onehot(index_ref[...], ROWS), 2)
+        choice = onehot(index_ref[...], ROWS)
+        loads = l_ref[...]
+        top = loads.astype(BF16)
+        rest = (loads - top.astype(F32)).astype(BF16)
+        msg_ref[:CROWS, :] = cy_ref[...]
+        msg_ref[CROWS:, :] = jnp.dot(
+            jnp.concatenate([top, rest], axis=0), choice, preferred_element_type=F32
+        ).astype(BF16)
 
 
 def powers_kernel(
-    edge_ref, own_ref, y_ref, xlo_ref, xhi_ref, index_ref, coord_ref, own_index_ref, h_ref,
-    v_ref, dots_ref, us, fs,
+    edge_ref, own_ref, y_ref, xlo_ref, xhi_ref, cindex_ref, index_ref, coord_ref, own_index_ref,
+    hown_ref, v_ref, dots_ref, us, fs, h_ref,
 ):
     row = lax.broadcasted_iota(jnp.int32, (8, GRID), 0)
     beyond_x = (coord_ref[0:1, :] >= TX) & (edge_ref[0] == 1)
@@ -307,8 +375,24 @@
         lax.fori_loop(0, GRID // 128, tile_step, 0)
         return scatter(lambda j, l, c: fs[(j * 2 + l) * 3 + c])
 
-    source = jnp.concatenate([own_ref[...], y_ref[...], xlo_ref[...], xhi_ref[...]], axis=1)
-    loads = select_lanes(source, onehot(index_ref[...], source.shape[1]), 2)
+    ghosts = jnp.concatenate([y_ref[:CROWS, :], xlo_ref[:CROWS, :], xhi_ref[:CROWS, :]], axis=1)
+    placed = jnp.dot(ghosts, onehot(cindex_ref[...] - ROWS, 384), preferred_element_type=F32)
+    for tile in range(GRID // 128):
+        h_ref[tile] = placed[:, tile * 128 : (tile + 1) * 128] + hown_ref[tile]
+    top = own_ref[...].astype(BF16)
+    rest = (own_ref[...] - top.astype(F32)).astype(BF16)
+    source = jnp.concatenate(
+        [
+            jnp.concatenate([top, rest], axis=0),
+            y_ref[CROWS:, :],
+            xlo_ref[CROWS : CROWS + 192, :],
+            xlo_ref[CROWS + 192 :, :],
+            xhi_ref[CROWS:, :],
+        ],
+        axis=1,
+    )
+    loads = jnp.dot(source, onehot(index_ref[...], GRID), preferred_element_type=F32)
+    loads = loads[:96] + loads[96:]
 
     def load_rows(j, l, c):
         at = c * 32 + (j * 2 + l) * 8
@@ -370,33 +454,52 @@
             norm_next = inner(resid, resid)
             direction = add(resid, direction, norm_next / norm_now)
             norm_now = norm_next
-    for ref, coefs in ((x_ref, increment), (r_ref, resid)):
+    at_x = lax.broadcasted_iota(jnp.int32, (TX, ROWS), 1) >> 5 == lax.broadcasted_iota(
+        jnp.int32, (TX, ROWS), 0
+    )
+    at_y = lax.broadcasted_iota(jnp.int32, (ROWS, TY), 0) & 31 == lax.broadcasted_iota(
+        jnp.int32, (ROWS, TY), 1
+    )
+    pieces = []
+    for coefs in (increment, resid):
         for c in range(3):
             out = None
             for k, coef in coefs.items():
                 at = (k * 3 + c) * 8
                 term = coef * v_ref[at : at + 8, :]
                 out = term if out is None else out + term
-            ref[c] = jnp.transpose(out, (1, 0))[:, :5]
+            for z in range(TZ + 1):
+                pieces.append(jnp.where(at_x, out[z : z + 1, :], 0.0))
+    split = select_lanes(
+        jnp.concatenate(pieces, axis=0), jnp.where(at_y, 1.0, 0.0).astype(BF16), 3
+    )
+    half = 3 * (TZ + 1) * TX
+    x_ref[...] = split[:half]
+    r_ref[...] = split[half:]
 
 
 def whole(shape):
     return pl.BlockSpec(shape, lambda *_: (0,) * len(shape))
 
 
-def call(kernel, outs, *args, name):
+def call(kernel, outs, *args, name, us):
     return pl.pallas_call(
         kernel,
         out_shape=outs,
         in_specs=[pl.BlockSpec(memory_space=pltpu.VMEM)] * len(args),
         out_specs=jax.tree.map(lambda _: pl.BlockSpec(memory_space=pltpu.VMEM), outs),
         compiler_params=pltpu.CompilerParams(vmem_limit_bytes=VMEM_LIMIT),
+        cost_estimate=cost(us),
         name=name,
     )(*args)
 
 
-def struct(*shape):
-    return jax.ShapeDtypeStruct(shape, F32)
+def struct(*shape, dtype=F32):
+    return jax.ShapeDtypeStruct(shape, dtype)
+
+
+def cost(us):
+    return pl.CostEstimate(flops=0, transcendentals=0, bytes_accessed=int(us * 3.0e6))
 
 
 def shifted(value, dx, dy):
@@ -409,18 +512,6 @@
     return lax.ppermute(value, ("gx", "gy"), pairs)
 
 
-def exchange(own, ysend, xsend, ylow, widths, name):
-    rows = own.shape[0]
-    below, above = shifted(ysend, 0, 1), shifted(ysend, 0, -1)
-    ytile, up, down = call(
-        functools.partial(edge_kernel, ylow),
-        (struct(rows, 128), struct(rows, widths[0]), struct(rows, widths[1])),
-        own, below, above, jnp.asarray(xsend),
-        name=name,
-    )
-    return ytile, shifted(up, 1, 0), shifted(down, -1, 0)
-
-
 def per_device(
     reference_scan, ref_gradient, deformed_scan, interp_weights, sample_mask, block_list, offsets
 ):
@@ -429,61 +520,109 @@
     weights = interp_weights.reshape(ROWS, COL)
     mask = sample_mask.reshape(ROWS, COL)
     moved = deformed_scan.reshape(ROWS, COL)
-    ylast = deformed_scan[:, TY - 4 :, :].reshape(TX * 4, COL)
-    yfirst = deformed_scan[:, :4, :].reshape(TX * 4, COL)
-    pieces = (
-        shifted(moved[384:], 1, 0),
-        shifted(moved[:160], -1, 0),
-        shifted(ylast, 0, 1),
-        shifted(yfirst, 0, -1),
-        shifted(ylast[48:], 1, 1),
-        shifted(yfirst[48:], 1, -1),
-        shifted(ylast[:20], -1, 1),
-        shifted(yfirst[:20], -1, -1),
-    )
-    coefs, coefs_y = pl.pallas_call(
+    moves = jnp.transpose(offsets, (0, 1, 3, 2))
+    lanes = lambda rows: pl.BlockSpec((rows, 512), lambda i: (0, i))
+    params = pltpu.CompilerParams(vmem_limit_bytes=VMEM_LIMIT)
+    bf = functools.partial(struct, dtype=BF16)
+
+    ends = deformed_scan.reshape(TX, TY // 8, 8, COL)
+    ylast, yfirst = pl.pallas_call(
+        pack_y_kernel,
+        out_shape=(bf(64, COL), bf(64, COL)),
+        grid=(2,),
+        in_specs=[
+            pl.BlockSpec((TX, None, 8, COL // 2), lambda i: (0, TY // 8 - 1, 0, i)),
+            pl.BlockSpec((TX, None, 8, COL // 2), lambda i: (0, 0, 0, i)),
+        ],
+        out_specs=(pl.BlockSpec((64, COL // 2), lambda i: (0, i)),) * 2,
+        compiler_params=params,
+        cost_estimate=cost(2),
+        name="pack_y",
+    )(ends, ends)
+    ylo, yhi = shifted(ylast, 0, 1), shifted(yfirst, 0, -1)
+    anywhere = pl.BlockSpec(memory_space=pl.ANY)
+    up, down = pl.pallas_call(
+        pack_x_kernel,
+        out_shape=(bf(160, COL), bf(208, COL)),
+        in_specs=[anywhere] * 3,
+        out_specs=(anywhere, anywhere),
+        scratch_shapes=[pltpu.SemaphoreType.DMA((6,))],
+        compiler_params=params,
+        cost_estimate=cost(2),
+        name="pack_x",
+    )(moved, ylo, yhi)
+    grad, mask, moves, up, down = lax.optimization_barrier((grad, mask, moves, up, down))
+    xlo, xhi = shifted(up, 1, 0), shifted(down, -1, 0)
+
+    coefs, coefs_y, coefs_x = pl.pallas_call(
         hessian_kernel,
-        out_shape=(struct(6 * HROWS, ROWS), struct(6 * HROWS, 128)),
+        out_shape=(bf(CROWS, ROWS), bf(CROWS, 128), bf(CROWS, 256)),
         grid=(2,),
         in_specs=[
             pl.BlockSpec((3, 256, COL), lambda i: (0, i, 0)),
             pl.BlockSpec((256, COL), lambda i: (i, 0)),
             whole((HROWS, COL)),
             whole((1, 128)),
+            whole((1, 256)),
         ],
-        out_specs=(pl.BlockSpec((6 * HROWS, 256), lambda i: (0, i)), whole((6 * HROWS, 128))),
-        compiler_params=pltpu.CompilerParams(vmem_limit_bytes=VMEM_LIMIT),
+        out_specs=(
+            pl.BlockSpec((CROWS, 256), lambda i: (0, i)),
+            whole((CROWS, 128)),
+            whole((CROWS, 256)),
+        ),
+        compiler_params=params,
+        cost_estimate=cost(9),
         name="hessian",
-    )(grad, mask, jnp.asarray(hessian_table()), jnp.asarray(H_YSEND))
-    coefs_ghost = exchange(coefs, coefs_y, H_XSEND, H_YLOW, (128, 128), "hessian_edges")
-
-    lanes = lambda rows: pl.BlockSpec((rows, 512), lambda i: (0, i))
-    loads, loads_y = pl.pallas_call(
+    )(
+        grad, mask, jnp.asarray(hessian_table()), jnp.asarray(H_YSEND),
+        jnp.asarray(np.where(H_XSEND < ROWS, H_XSEND, -1)),
+    )
+    own_samples = pl.pallas_call(
+        own_samples_kernel,
+        out_shape=bf(2 * ROWS, COL),
+        grid=(TZ,),
+        in_specs=[lanes(ROWS), whole((2, TX, TZ, TY))],
+        out_specs=lanes(2 * ROWS),
+        compiler_params=params,
+        cost_estimate=cost(7),
+        name="own_samples",
+    )(moved, moves)
+    stiffness = call(
+        grid_kernel, struct(GRID // 128, CROWS, 128), coefs, jnp.asarray(H_GRID),
+        name="hessian_grid", us=3,
+    )
+
+    loads, message = pl.pallas_call(
         warp_kernel,
-        out_shape=(struct(96, ROWS), struct(96, 128)),
+        out_shape=(struct(96, ROWS), bf(CROWS + 192, 128)),
         grid=(TZ,),
         in_specs=[
             lanes(ROWS), lanes(ROWS), lanes(ROWS),
             pl.BlockSpec((3, ROWS, 512), lambda i: (0, 0, i)),
-            lanes(ROWS),
+            lanes(2 * ROWS),
             *[lanes(rows) for rows in GHOST_ROWS],
-            whole((2, ROWS, TZ)),
+            whole((2, TX, TZ, TY)),
             lanes(64),
             whole((1, 128)),
+            whole((CROWS, 128)),
         ],
-        out_specs=(whole((96, ROWS)), whole((96, 128))),
+        out_specs=(whole((96, ROWS)), whole((CROWS + 192, 128))),
         scratch_shapes=[pltpu.VMEM((512, 512), BF16), pltpu.VMEM((3, ROWS, 512), BF16)],
-        compiler_params=pltpu.CompilerParams(vmem_limit_bytes=VMEM_LIMIT),
+        compiler_params=params,
+        cost_estimate=cost(9),
         name="warp",
     )(
-        scan, weights, mask, grad, moved, *pieces, offsets.reshape(2, ROWS, TZ),
-        jnp.asarray(load_table()), jnp.asarray(L_YSEND),
-    )
-    loads_ghost = exchange(loads, loads_y, L_XSEND, L_YLOW, (256, 128), "load_edges")
-    stiffness = call(
-        grid_kernel, struct(GRID // 128, 6 * HROWS, 128), coefs, *coefs_ghost,
-        jnp.asarray(H_GRID), name="hessian_grid",
-    )
+        scan, weights, mask, grad, own_samples, xlo, xhi, ylo, yhi, moves,
+        jnp.asarray(load_table()), jnp.asarray(L_YSEND), coefs_y,
+    )
+    below, above = shifted(message, 0, 1), shifted(message, 0, -1)
+    ytile, up, down = call(
+        edge_kernel,
+        (bf(CROWS + 192, 128), bf(CROWS + 384, 128), bf(CROWS + 192, 128)),
+        loads, coefs_x, below, above, jnp.asarray(H_XSEND), jnp.asarray(L_XSEND),
+        name="edges", us=2,
+    )
+    ghosts = (ytile, shifted(up, 1, 0), shifted(down, -1, 0))
 
     position = np.arange(GRID)
     coord = np.stack([position // PITCH - 4, position % PITCH - 4]).astype(np.int32)
@@ -495,20 +634,27 @@
     vectors, dots = pl.pallas_call(
         powers_kernel,
         out_shape=(struct(96, ROWS), struct(devices, 128)),
-        in_specs=[pl.BlockSpec(memory_space=pltpu.SMEM)] + [vmem] * 8,
+        in_specs=[pl.BlockSpec(memory_space=pltpu.SMEM)] + [vmem] * 9,
         out_specs=(vmem, vmem),
-        scratch_shapes=[pltpu.VMEM((24, 8, GRID), F32), pltpu.VMEM((12, 8, GRID), F32)],
-        compiler_params=pltpu.CompilerParams(vmem_limit_bytes=VMEM_LIMIT),
+        scratch_shapes=[
+            pltpu.VMEM((24, 8, GRID), F32),
+            pltpu.VMEM((12, 8, GRID), F32),
+            pltpu.VMEM((GRID // 128, CROWS, 128), F32),
+        ],
+        compiler_params=params,
+        cost_estimate=cost(9),
         name="powers",
     )(
-        last, loads, *loads_ghost, jnp.asarray(L_GRID), jnp.asarray(coord),
+        last, loads, *ghosts, jnp.asarray(H_GRID), jnp.asarray(L_GRID), jnp.asarray(coord),
         jnp.asarray(OWN_MAP), stiffness,
     )
     dots = lax.all_to_all(dots, ("gx", "gy"), 0, 0, tiled=True)
     increment, resid = call(
-        combine_kernel, (struct(3, ROWS, 5), struct(3, ROWS, 5)), vectors, dots, name="combine"
-    )
-    return (increment.reshape(3, TX, TY, 5), resid.reshape(3, TX, TY, 5))
+        combine_kernel, (struct(240, TY), struct(240, TY)), vectors, dots, name="combine", us=3
+    )
+    return tuple(
+        jnp.transpose(out.reshape(3, TZ + 1, TX, TY), (0, 2, 3, 1)) for out in (increment, resid)
+    )
 
 
 def solution(mesh):

time: 137 us -> 103 us (0.75)
  starting transfers between devices: 49.9 us -> 24.9 us
  Pallas kernels: 46.7 us -> 31.5 us
  waiting for transfers between devices: 4.21 us -> 18.1 us
  local copies, waits for them, and re-layouts: 12.1 us -> 1.69 us
  blocking collectives: 21.3 us -> 25.3 us
    ppermute x16 -> x8, starting transfers between devices: 49.9 us -> 24.9 us  [shifted(): return lax.ppermute(value, ('gx', 'gy'), pairs)]
    ppermute x16 -> x8, waiting for transfers between devices: 4.21 us -> 18.1 us  [shifted(): return lax.ppermute(value, ('gx', 'gy'), pairs)]
    pallas_call x4 -> x3, Pallas kernels: 13.9 us -> 2.66 us  [call(): pl.pallas_call(kernel, out_shape=outs, in_specs=[pl.BlockSpec(memory_spac...]
    unnamed x31 -> x36, local copies, waits for them, and re-layouts: 9.81 us -> 1.69 us
    all_to_all x1, blocking collectives: 21.3 us -> 25.3 us  [per_device(): dots = lax.all_to_all(dots, ('gx', 'gy'), 0, 0, tiled=True)]
    slice x9 -> x0, local copies, waits for them, and re-layouts: 2.2 us -> none  [the longest x1 0.88 us: per_device(): moved[:160]]
    pallas_call x2 -> x5, Pallas kernels: 24.2 us -> 22.2 us  [the longest x1 10 us: per_device(): pl.pallas_call(warp_kernel, out_shape=(struct(96, ROWS), bf(CROWS + 192,...]
    pallas_call x1, Pallas kernels: 8.55 us -> 6.64 us  [per_device(): pl.pallas_call(powers_kernel, out_shape=(struct(96, ROWS), struct(devices...]
  transfers between devices with their start and end apart: 16 -> 8, of which waited for: 2 -> 6; matrix products, arithmetic and copies ran while one was open for 4% -> 0% of each run, Pallas kernels for 20% -> 11%
where the time goes in v2:
time: 103 us
  Pallas kernels  31.5 us (31%)
  blocking collectives  25.3 us (25%)
  starting transfers between devices  24.9 us (24%)
  waiting for transfers between devices  18.1 us (18%)
  local copies, waits for them, and re-layouts  1.69 us (2%)
    all_to_all x1, blocking collectives, per_device(): dots = lax.all_to_all(dots, ('gx', 'gy'), 0, 0, tiled=True)  25.3 us
    ppermute x8, starting transfers between devices, shifted(): return lax.ppermute(value, ('gx', 'gy'), pairs)  24.9 us
    ppermute x8, waiting for transfers between devices, shifted(): return lax.ppermute(value, ('gx', 'gy'), pairs)  18.1 us
    pallas_call x1, Pallas kernels, per_device(): pl.pallas_call(warp_kernel, out_shape=(struct(96, ROWS), bf(CROWS + 192,...  10 us
    pallas_call x1, Pallas kernels, per_device(): pl.pallas_call(powers_kernel, out_shape=(struct(96, ROWS), struct(devices...  6.64 us
    pallas_call x1, Pallas kernels, per_device(): pl.pallas_call(hessian_kernel, out_shape=(bf(CROWS, ROWS), bf(CROWS, 128)...  6.08 us
    pallas_call x1, Pallas kernels, per_device(): pl.pallas_call(own_samples_kernel, out_shape=bf(2 * ROWS, COL), grid=(TZ,...  4.78 us
    pallas_call x3, Pallas kernels, call(): pl.pallas_call(kernel, out_shape=outs, in_specs=[pl.BlockSpec(memory_spac...  2.66 us
  transfers between devices with their start and end apart: 8, of which 6 were waited for; matrix products, arithmetic and copies ran while one was open for 0% of the time, Pallas kernels for 11%

profile of v2, /device:TPU:1, one launch (start us, length us, event | category | flops | bytes accessed | tf_op | source)
XLA Modules:
  0.0 102.6 jit_solution(1448227487261530191)
XLA Ops:
  0.6 0.0 copy-start
  0.6 1.6 %copy-done = bf16[16,32,2048]{2,1,0:T(8,128)(2,1)S(1)} copy-done((bf16[16,32,2048]{2,1,0:T(8,128)(2,1)S(1)}, bf16[16,32,2048]{2,1,0:T(8,128)(2,1)}, u32[]{:S(2)}) %copy-start) | copy-done | bytes 2097176
  2.2 0.0 copy-start.6
  2.2 0.0 slice-start
  2.2 0.6 pack_y.1
  2.8 4.7 %collective-permute-start = (bf16[64,2048]{1,0:T(8,128)(2,1)S(1)}, bf16[64,2048]{1,0:T(8,128)(2,1)S(1)}, u32[]{:S(2)}, u32[]{:S(2)}) collective-permute-start(bf16[64,2048]{1,0:T(8,128)(2,1)S(1)} %get-tuple-element.23), channel_id=1, source_target_pairs={{0,1},{1,2},{2,3},{3,4},{4,5},{5,6},{6,7},{8,9},{9,10},{10,11},{11... | collective-permute-start | bytes 786440 | tf_op jit(solution)/shard_map/ppermute | solution.py:512
  7.5 1.9 %collective-permute-start.1 = (bf16[64,2048]{1,0:T(8,128)(2,1)S(1)}, bf16[64,2048]{1,0:T(8,128)(2,1)S(1)}, u32[]{:S(2)}, u32[]{:S(2)}) collective-permute-start(bf16[64,2048]{1,0:T(8,128)(2,1)S(1)} %get-tuple-element.24), channel_id=1, source_target_pairs={{1,0},{2,1},{3,2},{4,3},{5,4},{6,5},{7,6},{9,8},{10,9},{11,10},{12... | collective-permute-start | bytes 786440 | tf_op jit(solution)/shard_map/ppermute | solution.py:512
  9.5 1.4 %collective-permute-done.ylo_ref.p2 = bf16[64,2048]{1,0:T(8,128)(2,1)S(1)} collective-permute-done((bf16[64,2048]{1,0:T(8,128)(2,1)S(1)}, bf16[64,2048]{1,0:T(8,128)(2,1)S(1)}, u32[]{:S(2)}, u32[]{:S(2)}) %collective-permute-start) | collective-permute-done | bytes 262176 | tf_op jit(solution)/shard_map/ppermute | solution.py:512
  10.8 4.4 %collective-permute-done.1.yhi_ref.p3 = bf16[64,2048]{1,0:T(8,128)(2,1)S(1)} collective-permute-done((bf16[64,2048]{1,0:T(8,128)(2,1)S(1)}, bf16[64,2048]{1,0:T(8,128)(2,1)S(1)}, u32[]{:S(2)}, u32[]{:S(2)}) %collective-permute-start.1) | collective-permute-done | bytes 262176 | tf_op jit(solution)/shard_map/ppermute | solution.py:512
  15.2 0.0 slice-start.1
  15.2 0.7 pack_x.1
  16.0 0.0 copy-start.1
  16.0 0.0 copy-start.4
  16.0 0.0 copy-start.13
  16.0 0.0 copy-start.15
  16.0 1.6 %collective-permute-start.3 = (bf16[208,2048]{1,0:T(8,128)(2,1)S(1)}, bf16[208,2048]{1,0:T(8,128)(2,1)S(1)}, u32[]{:S(2)}, u32[]{:S(2)}) collective-permute-start(bf16[208,2048]{1,0:T(8,128)(2,1)S(1)} %get-tuple-element.31), channel_id=1, source_target_pairs={{8,0},{9,1},{10,2},{11,3},{12,4},{13,5},{14,6},{15,7},{16,8},{17,9... | collective-permute-start | bytes 2555912 | tf_op jit(solution)/shard_map/ppermute | solution.py:512
  17.6 4.2 %collective-permute-start.2 = (bf16[160,2048]{1,0:T(8,128)(2,1)S(1)}, bf16[160,2048]{1,0:T(8,128)(2,1)S(1)}, u32[]{:S(2)}, u32[]{:S(2)}) collective-permute-start(bf16[160,2048]{1,0:T(8,128)(2,1)S(1)} %get-tuple-element.30), channel_id=1, source_target_pairs={{0,8},{1,9},{2,10},{3,11},{4,12},{5,13},{6,14},{7,15},{8,16},{9,17... | collective-permute-start | bytes 1966088 | tf_op jit(solution)/shard_map/ppermute | solution.py:512
  21.8 0.0 copy-done.6
  21.8 4.8 %own_samples.1.n_ref = bf16[1024,2048]{1,0:T(8,128)(2,1)S(1)} custom-call(bf16[512,2048]{1,0:T(8,128)(2,1)S(1)} %bitcast.22, s32[2,16,4,32]{3,2,1,0:T(4,128)S(1)} %bitcast.31), custom_call_target="tpu_custom_call" | custom-call | bytes 21000000 | tf_op jit(solution)/shard_map/own_samples/pallas_call | solution.py:580
  26.6 0.0 slice-done
  26.6 0.0 slice-done.1
  26.6 0.0 copy-done.1
  26.6 0.0 copy-done.4
  26.6 0.0 copy-done.13
  26.6 0.0 copy-done.15
  26.7 0.0 copy-start.2
  26.7 0.0 copy-start.3
  26.7 0.0 copy-start.5
  26.7 0.0 copy-start.14
  26.7 6.1 %hessian.1 = (bf16[672,512]{1,0:T(8,128)(2,1)S(1)}, bf16[672,128]{1,0:T(8,128)(2,1)S(1)}, bf16[672,256]{1,0:T(8,128)(2,1)S(1)}) custom-call(bf16[3,512,2048]{2,1,0:T(8,128)(2,1)S(1)} %bitcast.25, s32[512,2048]{1,0:T(8,128)S(1)} %bitcast.27, bf16[112,2048]{1,0:T(8,128)(2,1)S(1)} %copy-done.4, s32[1,128]{1,0:T(1,128)S(1)} %copy-done.15, s32[1,256]{1,0:T(1,128)S(1)} %copy-done.13), custom_call_target="tpu_custom_call" | custom-call | bytes 27000000 | tf_op jit(solution)/shard_map/hessian/pallas_call | solution.py:557
  32.8 0.0 collective-permute-done.2.p0
  32.8 2.2 %collective-permute-done.3.p1 = bf16[208,2048]{1,0:T(8,128)(2,1)S(1)} collective-permute-done((bf16[208,2048]{1,0:T(8,128)(2,1)S(1)}, bf16[208,2048]{1,0:T(8,128)(2,1)S(1)}, u32[]{:S(2)}, u32[]{:S(2)}) %collective-permute-start.3) | collective-permute-done | bytes 852000 | tf_op jit(solution)/shard_map/ppermute | solution.py:512
  35.1 0.0 copy-done.2
  35.1 0.0 copy-done.3
  35.1 0.0 copy-done.5
  35.1 0.0 copy-done.14
  35.1 0.0 copy-start.11
  35.1 0.0 copy-start.12
  35.1 0.0 copy-start.7
  35.1 10.0 %warp.1 = (f32[96,512]{1,0:T(8,128)S(1)}, bf16[864,128]{1,0:T(8,128)(2,1)S(1)}) custom-call(bf16[512,2048]{1,0:T(8,128)(2,1)S(1)} %bitcast.29, bf16[512,2048]{1,0:T(8,128)(2,1)S(1)} %bitcast.30, s32[512,2048]{1,0:T(8,128)S(1)} %bitcast.28, bf16[3,512,2048]{2,1,0:T(8,128)(2,1)S(1)} %bitcast.26, bf16[1024,2048]{1,0:T(8,128)(2,1)S(1)} %own_samples.1.n_ref, ...), custom_call_target="tpu_custom_call" | custom-call | bytes 27000000 | tf_op jit(solution)/shard_map/warp/pallas_call | solution.py:595
  45.1 0.0 copy-start.8
  45.1 0.0 copy-start.9
  45.2 0.0 copy-start.10
  45.2 5.7 %collective-permute-start.4 = (bf16[864,128]{1,0:T(8,128)(2,1)S(1)}, bf16[864,128]{1,0:T(8,128)(2,1)S(1)}, u32[]{:S(2)}, u32[]{:S(2)}) collective-permute-start(bf16[864,128]{1,0:T(8,128)(2,1)S(1)} %get-tuple-element.35), channel_id=1, source_target_pairs={{0,1},{1,2},{2,3},{3,4},{4,5},{5,6},{6,7},{8,9},{9,10},{10,11},{11... | collective-permute-start | bytes 663560 | tf_op jit(solution)/shard_map/ppermute | solution.py:512
  50.9 1.9 %collective-permute-start.5 = (bf16[864,128]{1,0:T(8,128)(2,1)S(1)}, bf16[864,128]{1,0:T(8,128)(2,1)S(1)}, u32[]{:S(2)}, u32[]{:S(2)}) collective-permute-start(bf16[864,128]{1,0:T(8,128)(2,1)S(1)} %get-tuple-element.35), channel_id=1, source_target_pairs={{1,0},{2,1},{3,2},{4,3},{5,4},{6,5},{7,6},{9,8},{10,9},{11,10},{12... | collective-permute-start | bytes 663560 | tf_op jit(solution)/shard_map/ppermute | solution.py:512
  52.8 0.9 collective-permute-done.4.below_ref
  53.8 4.4 %collective-permute-done.5.above_ref = bf16[864,128]{1,0:T(8,128)(2,1)S(1)} collective-permute-done((bf16[864,128]{1,0:T(8,128)(2,1)S(1)}, bf16[864,128]{1,0:T(8,128)(2,1)S(1)}, u32[]{:S(2)}, u32[]{:S(2)}) %collective-permute-start.5) | collective-permute-done | bytes 221216 | tf_op jit(solution)/shard_map/ppermute | solution.py:512
  58.2 0.0 copy-done.11
  58.2 0.0 copy-done.12
  58.2 0.4 edges.1
  58.6 3.6 %collective-permute-start.6 = (bf16[1056,128]{1,0:T(8,128)(2,1)S(1)}, bf16[1056,128]{1,0:T(8,128)(2,1)S(1)}, u32[]{:S(2)}, u32[]{:S(2)}) collective-permute-start(bf16[1056,128]{1,0:T(8,128)(2,1)S(1)} %get-tuple-element.37), channel_id=1, source_target_pairs={{0,8},{1,9},{2,10},{3,11},{4,12},{5,13},{6,14},{7,15},{8,16},{9,17... | collective-permute-start | bytes 811016 | tf_op jit(solution)/shard_map/ppermute | solution.py:512
  62.1 1.3 %collective-permute-start.7 = (bf16[864,128]{1,0:T(8,128)(2,1)S(1)}, bf16[864,128]{1,0:T(8,128)(2,1)S(1)}, u32[]{:S(2)}, u32[]{:S(2)}) collective-permute-start(bf16[864,128]{1,0:T(8,128)(2,1)S(1)} %get-tuple-element.38), channel_id=1, source_target_pairs={{8,0},{9,1},{10,2},{11,3},{12,4},{13,5},{14,6},{15,7},{16,8},{17,9... | collective-permute-start | bytes 663560 | tf_op jit(solution)/shard_map/ppermute | solution.py:512
  63.4 0.1 add_convert_fusion.edge_ref
  63.5 0.0 copy-done.7
  63.5 0.9 hessian_grid.1.hown_ref
  64.4 4.8 %collective-permute-done.7.xhi_ref = bf16[864,128]{1,0:T(8,128)(2,1)S(1)} collective-permute-done((bf16[864,128]{1,0:T(8,128)(2,1)S(1)}, bf16[864,128]{1,0:T(8,128)(2,1)S(1)}, u32[]{:S(2)}, u32[]{:S(2)}) %collective-permute-start.7) | collective-permute-done | bytes 221216 | tf_op jit(solution)/shard_map/ppermute | solution.py:512
  69.2 0.0 collective-permute-done.6.xlo_ref
  69.2 0.0 copy-done.8
  69.2 0.0 copy-done.9
  69.2 0.0 copy-done.10
  69.2 6.6 %powers.1 = (f32[96,512]{1,0:T(8,128)S(1)}, f32[128,128]{1,0:T(8,128)S(1)}) custom-call(s32[2]{0:T(128)S(1)} %add_convert_fusion.edge_ref, f32[96,512]{1,0:T(8,128)S(1)} %get-tuple-element.33.l_ref.own_ref, bf16[864,128]{1,0:T(8,128)(2,1)S(1)} %get-tuple-element.36.y_ref, bf16[1056,128]{1,0:T(8,128)(2,1)S(1)} %collective-permute-done.6.xlo_ref, ...), custom_call_target="tpu_custom_call" | custom-call | bytes 27000000 | tf_op jit(solution)/shard_map/powers/pallas_call | solution.py:634
  75.8 25.3 %all_to_all.11 = f32[128,1,128]{2,1,0:T(1,128)S(1)} all-to-all(f32[128,1,128]{2,1,0:T(1,128)S(1)} %bitcast.34), channel_id=1, replica_groups=mesh['gx'=16,'gy'=8] {'gx','gy'}, dimensions={0} | all-to-all | bytes 131072 | tf_op jit(solution)/shard_map/all_to_all | solution.py:651
  101.2 1.4 %combine.1 = (f32[240,32]{1,0:T(8,128)}, f32[240,32]{1,0:T(8,128)}) custom-call(f32[96,512]{1,0:T(8,128)S(1)} %get-tuple-element.40.v_ref, f32[128,128]{1,0:T(8,128)S(1)} %bitcast.33), custom_call_target="tpu_custom_call" | custom-call | bytes 9000000 | tf_op jit(solution)/shard_map/combine/pallas_call | solution.py:486
  (1 shorter events, 0.0 us)
Async XLA Ops:
  0.6 1.6 %copy-start = (bf16[16,32,2048]{2,1,0:T(8,128)(2,1)S(1)}, bf16[16,32,2048]{2,1,0:T(8,128)(2,1)}, u32[]{:S(2)}) copy-start(bf16[16,32,2048]{2,1,0:T(8,128)(2,1)} %param.20) | copy-start | bytes 6291460
  2.2 19.6 %copy-start.6 = (s32[2,16,32,4]{2,3,1,0:T(4,128)S(1)}, s32[2,16,32,4]{2,3,1,0:T(4,128)}, u32[]{:S(2)}) copy-start(s32[2,16,32,4]{2,3,1,0:T(4,128)} %param.23) | copy-start | bytes 49156
  2.2 24.4 %slice-start = ((s8[6291456]{0:T(1024)(128)(4,1)}), s8[4194304]{0:T(1024)(128)(4,1)S(1)}, s32[]{:S(2)}) async-start(s8[6291456]{0:T(1024)(128)(4,1)} %bitcast.23), calls=%async_computation.1 | async-start | bytes 8388608
  2.8 8.0 %collective-permute-start = (bf16[64,2048]{1,0:T(8,128)(2,1)S(1)}, bf16[64,2048]{1,0:T(8,128)(2,1)S(1)}, u32[]{:S(2)}, u32[]{:S(2)}) collective-permute-start(bf16[64,2048]{1,0:T(8,128)(2,1)S(1)} %get-tuple-element.23), channel_id=1, source_target_pairs={{0,1},{1,2},{2,3},{3,4},{4,5},{5,6},{6,7},{8,9},{9,10},{10,11},{11... | collective-permute-start | bytes 786440 | tf_op jit(solution)/shard_map/ppermute | solution.py:512
  7.5 7.7 %collective-permute-start.1 = (bf16[64,2048]{1,0:T(8,128)(2,1)S(1)}, bf16[64,2048]{1,0:T(8,128)(2,1)S(1)}, u32[]{:S(2)}, u32[]{:S(2)}) collective-permute-start(bf16[64,2048]{1,0:T(8,128)(2,1)S(1)} %get-tuple-element.24), channel_id=1, source_target_pairs={{1,0},{2,1},{3,2},{4,3},{5,4},{6,5},{7,6},{9,8},{10,9},{11,10},{12... | collective-permute-start | bytes 786440 | tf_op jit(solution)/shard_map/ppermute | solution.py:512
  15.2 11.4 %slice-start.1 = ((s8[6291456]{0:T(1024)(128)(4,1)}), s8[2097152]{0:T(1024)(128)(4,1)S(1)}, s32[]{:S(2)}) async-start(s8[6291456]{0:T(1024)(128)(4,1)} %bitcast.23), calls=%async_computation.2 | async-start | bytes 4194304
  16.0 10.7 %copy-start.1 = (s32[16,32,2048]{2,1,0:T(8,128)S(1)}, s32[16,32,2048]{2,1,0:T(8,128)}, u32[]{:S(2)}) copy-start(s32[16,32,2048]{2,1,0:T(8,128)} %param.22) | copy-start | bytes 12582916
  16.0 10.6 %copy-start.4 = (bf16[112,2048]{1,0:T(8,128)(2,1)S(1)}, bf16[112,2048]{1,0:T(8,128)(2,1)}, u32[]{:S(2)}) copy-start(bf16[112,2048]{1,0:T(8,128)(2,1)} %constant.35.clone.table_ref) | copy-start | bytes 1376260
  16.0 10.6 %copy-start.13 = (s32[1,256]{1,0:T(1,128)S(1)}, s32[1,256]{1,0:T(1,128)}, u32[]{:S(2)}) copy-start(s32[1,256]{1,0:T(1,128)} %constant.37.clone.xindex_ref) | copy-start | bytes 3076
  16.0 10.6 %copy-start.15 = (s32[1,128]{1,0:T(1,128)S(1)}, s32[1,128]{1,0:T(1,128)}, u32[]{:S(2)}) copy-start(s32[1,128]{1,0:T(1,128)} %constant.36.clone.yindex_ref) | copy-start | bytes 1540
  16.0 19.0 %collective-permute-start.3 = (bf16[208,2048]{1,0:T(8,128)(2,1)S(1)}, bf16[208,2048]{1,0:T(8,128)(2,1)S(1)}, u32[]{:S(2)}, u32[]{:S(2)}) collective-permute-start(bf16[208,2048]{1,0:T(8,128)(2,1)S(1)} %get-tuple-element.31), channel_id=1, source_target_pairs={{8,0},{9,1},{10,2},{11,3},{12,4},{13,5},{14,6},{15,7},{16,8},{17,9... | collective-permute-start | bytes 2555912 | tf_op jit(solution)/shard_map/ppermute | solution.py:512
  17.6 15.2 %collective-permute-start.2 = (bf16[160,2048]{1,0:T(8,128)(2,1)S(1)}, bf16[160,2048]{1,0:T(8,128)(2,1)S(1)}, u32[]{:S(2)}, u32[]{:S(2)}) collective-permute-start(bf16[160,2048]{1,0:T(8,128)(2,1)S(1)} %get-tuple-element.30), channel_id=1, source_target_pairs={{0,8},{1,9},{2,10},{3,11},{4,12},{5,13},{6,14},{7,15},{8,16},{9,17... | collective-permute-start | bytes 1966088 | tf_op jit(solution)/shard_map/ppermute | solution.py:512
  26.7 8.4 %copy-start.2 = (bf16[16,32,2048]{2,1,0:T(8,128)(2,1)S(1)}, bf16[16,32,2048]{2,1,0:T(8,128)(2,1)}, u32[]{:S(2)}) copy-start(bf16[16,32,2048]{2,1,0:T(8,128)(2,1)} %param.18) | copy-start | bytes 6291460
  26.7 8.4 %copy-start.3 = (bf16[16,32,2048]{2,1,0:T(8,128)(2,1)S(1)}, bf16[16,32,2048]{2,1,0:T(8,128)(2,1)}, u32[]{:S(2)}) copy-start(bf16[16,32,2048]{2,1,0:T(8,128)(2,1)} %param.21) | copy-start | bytes 6291460
  26.7 8.4 %copy-start.5 = (bf16[64,2048]{1,0:T(8,128)(2,1)S(1)}, bf16[64,2048]{1,0:T(8,128)(2,1)}, u32[]{:S(2)}) copy-start(bf16[64,2048]{1,0:T(8,128)(2,1)} %constant.39.clone.table_ref) | copy-start | bytes 786436
  26.7 8.4 %copy-start.14 = (s32[1,128]{1,0:T(1,128)S(1)}, s32[1,128]{1,0:T(1,128)}, u32[]{:S(2)}) copy-start(s32[1,128]{1,0:T(1,128)} %constant.40.clone.index_ref) | copy-start | bytes 1540
  35.1 23.1 %copy-start.11 = (s32[1,384]{1,0:T(1,128)S(1)}, s32[1,384]{1,0:T(1,128)}, u32[]{:S(2)}) copy-start(s32[1,384]{1,0:T(1,128)} %constant.42.clone.lindex_ref) | copy-start | bytes 4612
  35.1 23.1 %copy-start.12 = (s32[1,256]{1,0:T(1,128)S(1)}, s32[1,256]{1,0:T(1,128)}, u32[]{:S(2)}) copy-start(s32[1,256]{1,0:T(1,128)} %constant.41.clone.cindex_ref) | copy-start | bytes 3076
  35.1 28.4 %copy-start.7 = (s32[1,1024]{1,0:T(1,128)S(1)}, s32[1,1024]{1,0:T(1,128)}, u32[]{:S(2)}) copy-start(s32[1,1024]{1,0:T(1,128)} %constant.38.clone.index_ref.cindex_ref) | copy-start | bytes 12292
  45.1 24.1 %copy-start.8 = (s32[2,1024]{1,0:T(2,128)S(1)}, s32[2,1024]{1,0:T(2,128)}, u32[]{:S(2)}) copy-start(s32[2,1024]{1,0:T(2,128)} %constant.44.clone.coord_ref) | copy-start | bytes 24580
  45.1 24.1 %copy-start.9 = (s32[1,1024]{1,0:T(1,128)S(1)}, s32[1,1024]{1,0:T(1,128)}, u32[]{:S(2)}) copy-start(s32[1,1024]{1,0:T(1,128)} %constant.43.clone.index_ref) | copy-start | bytes 12292
  45.2 24.0 %copy-start.10 = (s32[1,512]{1,0:T(1,128)S(1)}, s32[1,512]{1,0:T(1,128)}, u32[]{:S(2)}) copy-start(s32[1,512]{1,0:T(1,128)} %constant.45.clone.own_index_ref) | copy-start | bytes 6148
  45.2 8.6 %collective-permute-start.4 = (bf16[864,128]{1,0:T(8,128)(2,1)S(1)}, bf16[864,128]{1,0:T(8,128)(2,1)S(1)}, u32[]{:S(2)}, u32[]{:S(2)}) collective-permute-start(bf16[864,128]{1,0:T(8,128)(2,1)S(1)} %get-tuple-element.35), channel_id=1, source_target_pairs={{0,1},{1,2},{2,3},{3,4},{4,5},{5,6},{6,7},{8,9},{9,10},{10,11},{11... | collective-permute-start | bytes 663560 | tf_op jit(solution)/shard_map/ppermute | solution.py:512
  50.9 7.3 %collective-permute-start.5 = (bf16[864,128]{1,0:T(8,128)(2,1)S(1)}, bf16[864,128]{1,0:T(8,128)(2,1)S(1)}, u32[]{:S(2)}, u32[]{:S(2)}) collective-permute-start(bf16[864,128]{1,0:T(8,128)(2,1)S(1)} %get-tuple-element.35), channel_id=1, source_target_pairs={{1,0},{2,1},{3,2},{4,3},{5,4},{6,5},{7,6},{9,8},{10,9},{11,10},{12... | collective-permute-start | bytes 663560 | tf_op jit(solution)/shard_map/ppermute | solution.py:512
  58.6 10.6 %collective-permute-start.6 = (bf16[1056,128]{1,0:T(8,128)(2,1)S(1)}, bf16[1056,128]{1,0:T(8,128)(2,1)S(1)}, u32[]{:S(2)}, u32[]{:S(2)}) collective-permute-start(bf16[1056,128]{1,0:T(8,128)(2,1)S(1)} %get-tuple-element.37), channel_id=1, source_target_pairs={{0,8},{1,9},{2,10},{3,11},{4,12},{5,13},{6,14},{7,15},{8,16},{9,17... | collective-permute-start | bytes 811016 | tf_op jit(solution)/shard_map/ppermute | solution.py:512
  62.1 7.1 %collective-permute-start.7 = (bf16[864,128]{1,0:T(8,128)(2,1)S(1)}, bf16[864,128]{1,0:T(8,128)(2,1)S(1)}, u32[]{:S(2)}, u32[]{:S(2)}) collective-permute-start(bf16[864,128]{1,0:T(8,128)(2,1)S(1)} %get-tuple-element.38), channel_id=1, source_target_pairs={{8,0},{9,1},{10,2},{11,3},{12,4},{13,5},{14,6},{15,7},{16,8},{17,9... | collective-permute-start | bytes 663560 | tf_op jit(solution)/shard_map/ppermute | solution.py:512

commit v3 on v2

--- a/solution.py
+++ b/solution.py
@@ -22,7 +22,6 @@
 SCALE = 2.0**-8
 PAIRS = [(0, 0), (0, 1), (0, 2), (1, 1), (1, 2), (2, 2)]
 DOTS = [(0, 0), (0, 1), (0, 2), (0, 3), (1, 1), (1, 2), (1, 3), (2, 2), (2, 3)]
-VMEM_LIMIT = 24 * 1024 * 1024
 
 
 def voxel_factors():
@@ -41,7 +40,8 @@
                 t = (tj * 3 + tl) * 3 + ti
                 for ez in range(TZ):
                     table[4 * t + ez, ez] = q[0][ti] * q[1][tj] * q[2][tl]
-    return table.reshape(HROWS, COL).astype(jnp.bfloat16)
+    table = np.concatenate([table, np.zeros((128 - HROWS, TZ, 512))])
+    return np.ascontiguousarray(table.reshape(128, COL).T).astype(jnp.bfloat16)
 
 
 def load_table():
@@ -55,7 +55,8 @@
     table = table.reshape(32, COL)
     high = table.astype(jnp.bfloat16)
     low = (table - high.astype(np.float32)).astype(jnp.bfloat16)
-    return np.concatenate([high, low], axis=0)
+    both = np.concatenate([high, low, np.zeros((64, COL), high.dtype)], axis=0)
+    return np.ascontiguousarray(both.T)
 
 
 def edge_maps(low, high, xlo_lanes, xhi_lanes):
@@ -115,6 +116,41 @@
 )
 
 
+def lane_maps():
+    position = np.arange(GRID)
+    rows = np.full((8, GRID), -1, np.int32)
+    rows[0] = H_GRID
+    rows[1] = L_GRID
+    rows[2] = position // PITCH - 4
+    rows[3] = position % PITCH - 4
+    rows[4, :512] = OWN_MAP
+    rows[5, :128] = H_YSEND
+    rows[5, 128:384] = np.where(H_XSEND < ROWS, H_XSEND, -1)
+    rows[5, 384:640] = H_XSEND
+    rows[6, :128] = L_YSEND
+    rows[6, 128:512] = L_XSEND
+    return rows
+
+
+MAP = {
+    "h_grid": (0, 0, 1024),
+    "l_grid": (1, 0, 1024),
+    "x": (2, 0, 1024),
+    "y": (3, 0, 1024),
+    "own": (4, 0, 512),
+    "h_ysend": (5, 0, 128),
+    "h_xown": (5, 128, 384),
+    "h_xsend": (5, 384, 640),
+    "l_ysend": (6, 0, 128),
+    "l_xsend": (6, 128, 512),
+}
+
+
+def lane_map(maps_ref, name):
+    row, first, last = MAP[name]
+    return maps_ref[row : row + 1, first:last]
+
+
 def onehot(index_row, depth):
     lanes = index_row.shape[1]
     rows = lax.broadcasted_iota(jnp.int32, (depth, lanes), 0)
@@ -122,79 +158,83 @@
 
 
 def select_lanes(value, choice, parts):
-    total = None
-    rest = value
+    pieces, rest = [], value
     for part in range(parts):
-        piece = rest.astype(BF16)
-        term = jnp.dot(piece, choice, preferred_element_type=F32)
-        total = term if total is None else total + term
-        if part + 1 < parts:
-            rest = rest - piece.astype(F32)
+        pieces.append(rest.astype(BF16))
+        rest = rest - pieces[-1].astype(F32)
+    stacked = jnp.dot(jnp.concatenate(pieces, axis=0), choice, preferred_element_type=F32)
+    rows = value.shape[0]
+    total = stacked[:rows]
+    for part in range(1, parts):
+        total = total + stacked[part * rows : (part + 1) * rows]
     return total
 
 
-def matmul_nt(a, b):
-    return lax.dot_general(a, b, (((1,), (1,)), ((), ())), preferred_element_type=F32)
-
-
-def pack_y_kernel(end_ref, start_ref, last_ref, first_ref):
+def run_copies(sems, *moves):
+    copies = [
+        pltpu.make_async_copy(source, target, sems.at[k])
+        for k, (source, target) in enumerate(moves)
+    ]
+    for copy in copies:
+        copy.start()
+    return copies
+
+
+def pack_kernel(d_ref, up_ref, down_ref, last_ref, first_ref, ends, sems):
+    copies = run_copies(
+        sems,
+        (d_ref.at[pl.ds(0, TX), pl.ds(TY // 8 - 1, 1)], ends.at[0]),
+        (d_ref.at[pl.ds(0, TX), pl.ds(0, 1)], ends.at[1]),
+        (d_ref.at[pl.ds(TX - 4, 4)], up_ref),
+        (d_ref.at[pl.ds(0, 5)], down_ref),
+    )
     row = lax.broadcasted_iota(jnp.int32, (64, 128), 0)
     pos = lax.broadcasted_iota(jnp.int32, (64, 128), 1)
-    for ref, out_ref, at in ((end_ref, last_ref, 4), (start_ref, first_ref, 0)):
+    for k, (out_ref, at) in enumerate(((last_ref, 4), (first_ref, 0))):
         choice = jnp.where(pos == (row >> 2) * 8 + (row & 3) + at, 1.0, 0.0).astype(BF16)
-        rows = ref[...].astype(F32).reshape(TX * 8, ref.shape[-1]).astype(BF16)
+        copies[k].wait()
+        rows = ends[k].astype(F32).reshape(TX * 8, COL).astype(BF16)
         out_ref[...] = jnp.dot(choice, rows, preferred_element_type=F32).astype(BF16)
-
-
-def pack_x_kernel(d_ref, ylo_ref, yhi_ref, up_ref, down_ref, sems):
-    copies = []
-    for source, start, rows, target, at in (
-        (d_ref, 384, 128, up_ref, 0),
-        (ylo_ref, 48, 16, up_ref, 128),
-        (yhi_ref, 48, 16, up_ref, 144),
-        (d_ref, 0, 160, down_ref, 0),
-        (ylo_ref, 0, 24, down_ref, 160),
-        (yhi_ref, 0, 24, down_ref, 184),
-    ):
-        copies.append(
-            pltpu.make_async_copy(
-                source.at[pl.ds(start, rows)], target.at[pl.ds(at, rows)], sems.at[len(copies)]
-            )
-        )
-    for copy in copies:
-        copy.start()
-    for copy in copies:
-        copy.wait()
-
-
-def hessian_kernel(g_ref, m_ref, table_ref, yindex_ref, xindex_ref, c_ref, cy_ref, cx_ref):
-    step = pl.program_id(0)
-    mask = m_ref[...].astype(F32).astype(BF16)
-    for k, (c, d) in enumerate(PAIRS):
-        x = (g_ref[c] * mask) * g_ref[d]
-        c_ref[k * HROWS : (k + 1) * HROWS, :] = matmul_nt(table_ref[...], x).astype(BF16)
-    for index_ref, ref in ((yindex_ref, cy_ref), (xindex_ref, cx_ref)):
-        choice = onehot(index_ref[...] - step * 256, 256)
-        part = jnp.dot(c_ref[...], choice, preferred_element_type=F32).astype(BF16)
-
-        @pl.when(step == 0)
-        def _():
-            ref[...] = part
-
-        @pl.when(step > 0)
-        def _():
-            ref[...] += part
+    copies[2].wait()
+    copies[3].wait()
+
+
+def corner_kernel(ylo_ref, yhi_ref, after_ref, up_ref, down_ref):
+    up_ref[:16, :] = ylo_ref[48:, :]
+    up_ref[16:, :] = yhi_ref[48:, :]
+    down_ref[:24, :] = ylo_ref[:24, :]
+    down_ref[24:, :] = yhi_ref[:24, :]
+
+
+def hessian_kernel(g_ref, m_ref, table_ref, maps_ref, c_ref, cy_ref, cx_ref, mg_ref):
+    chunk = 256
+
+    def step(i, carry):
+        rows = pl.ds(pl.multiple_of(i * chunk, chunk), chunk)
+        mask = m_ref[rows, :].astype(F32).astype(BF16)
+        for c in range(3):
+            mg_ref[c, rows, :] = g_ref[c, rows, :] * mask
+        for k, (c, d) in enumerate(PAIRS):
+            x = mg_ref[c, rows, :] * g_ref[d, rows, :]
+            sums = jnp.dot(x, table_ref[...], preferred_element_type=F32)
+            c_ref[k * HROWS : (k + 1) * HROWS, rows] = jnp.transpose(sums, (1, 0))[:HROWS].astype(BF16)
+        return carry
+
+    lax.fori_loop(0, ROWS // chunk, step, 0)
+    for name, ref in (("h_ysend", cy_ref), ("h_xown", cx_ref)):
+        choice = onehot(lane_map(maps_ref, name), ROWS)
+        ref[...] = jnp.dot(c_ref[...], choice, preferred_element_type=F32).astype(BF16)
 
 
 def edge_kernel(
-    l_ref, cx_ref, below_ref, above_ref, cindex_ref, lindex_ref, y_ref, up_ref, down_ref
+    l_ref, cx_ref, below_ref, above_ref, maps_ref, y_ref, up_ref, down_ref
 ):
     lane = lax.broadcasted_iota(jnp.int32, (1, 128), 1)
     ytile_c = jnp.where(lane < H_YLOW, below_ref[:CROWS, :], above_ref[:CROWS, :])
     ytile_l = jnp.where(lane < L_YLOW, below_ref[CROWS:, :], above_ref[CROWS:, :])
     y_ref[:CROWS, :] = ytile_c
     y_ref[CROWS:, :] = ytile_l
-    sent = jnp.dot(ytile_c, onehot(cindex_ref[...] - ROWS, 128), preferred_element_type=F32)
+    sent = jnp.dot(ytile_c, onehot(lane_map(maps_ref, "h_xsend") - ROWS, 128), preferred_element_type=F32)
     sent = sent.astype(BF16) + cx_ref[...]
     up_ref[:CROWS, :] = sent[:, :128]
     down_ref[:CROWS, :] = sent[:, 128:]
@@ -202,17 +242,31 @@
     low = (l_ref[...] - high.astype(F32)).astype(BF16)
     source = jnp.concatenate([jnp.concatenate([high, low], axis=0), ytile_l], axis=1)
     sent = jnp.dot(
-        source, onehot(lindex_ref[...], ROWS + 128), preferred_element_type=F32
+        source, onehot(lane_map(maps_ref, "l_xsend"), ROWS + 128), preferred_element_type=F32
     ).astype(BF16)
     up_ref[CROWS : CROWS + 192, :] = sent[:, :128]
     up_ref[CROWS + 192 :, :] = sent[:, 128:256]
     down_ref[CROWS:, :] = sent[:, 256:]
 
 
-def grid_kernel(own_ref, index_ref, out_ref):
-    placed = jnp.dot(own_ref[...], onehot(index_ref[...], ROWS), preferred_element_type=F32)
+def grid_kernel(
+    own_ref, l_ref, y_ref, maps_ref,
+    out_ref, lout_ref, hchoice_ref, lchoice_ref, ochoice_ref,
+):
+    h_map, l_map = lane_map(maps_ref, "h_grid"), lane_map(maps_ref, "l_grid")
+    source = jnp.concatenate([own_ref[...], y_ref[:CROWS, :]], axis=1)
+    placed = jnp.dot(source, onehot(h_map, ROWS + 128), preferred_element_type=F32)
     for tile in range(GRID // 128):
         out_ref[tile] = placed[:, tile * 128 : (tile + 1) * 128]
+    top = l_ref[...].astype(BF16)
+    rest = (l_ref[...] - top.astype(F32)).astype(BF16)
+    source = jnp.concatenate([jnp.concatenate([top, rest], axis=0), y_ref[CROWS:, :]], axis=1)
+    placed = jnp.dot(source, onehot(l_map, ROWS + 128), preferred_element_type=F32)
+    lout_ref[...] = placed[:96] + placed[96:]
+    hchoice_ref[:, :256] = onehot(h_map[:, :256] - (ROWS + 128), 128)
+    hchoice_ref[:, 256:] = onehot(h_map[:, 768:896] - (ROWS + 256), 128)
+    lchoice_ref[...] = onehot(l_map - (ROWS + 128), 384)
+    ochoice_ref[...] = onehot(lane_map(maps_ref, "own"), GRID)
 
 
 def sample_slot(x, y):
@@ -261,64 +315,66 @@
     return jnp.concatenate([jnp.where(high == float(first + k), hit, zero) for k in range(4)], axis=1)
 
 
-GHOST_AT = (0, 160, 368, 432)
-GHOST_ROWS = (160, 208, 64, 64)
-
-
-def own_samples_kernel(d_ref, o_ref, out_ref):
-    ez = pl.program_id(0)
-    high, low = slot_columns(o_ref, ez)
-    out_ref[...] = jnp.dot(
-        slot_onehot(high, low, 0), d_ref[...], preferred_element_type=F32
+GHOST_AT = (0, 128, 160, 320, 368, 432)
+GHOST_ROWS = (128, 32, 160, 48, 64, 64)
+
+
+def blend(both, w):
+    w = w.astype(F32)
+    return w * both[:ROWS] + (1.0 - w) * both[ROWS:]
+
+
+def own_samples_kernel(s_ref, w_ref, d_ref, o_ref, out_ref, after_ref):
+    after_ref[...] = jnp.zeros_like(after_ref)
+    for ez in range(TZ):
+        lanes = slice(ez * 512, (ez + 1) * 512)
+        high, low = slot_columns(o_ref, ez)
+        both = jnp.dot(
+            slot_onehot(high, low, 0), d_ref[:, lanes], preferred_element_type=F32
+        )
+        out_ref[:, lanes] = s_ref[:, lanes].astype(F32) - blend(both, w_ref[:, lanes])
+
+
+def warp_kernel(
+    t_ref, w_ref, mg_ref, p0, p1, p2, p3, p4, p5, o_ref, table_ref, maps_ref, cy_ref,
+    l_ref, msg_ref, ghost,
+):
+    for at, rows, piece in zip(GHOST_AT, GHOST_ROWS, (p0, p1, p2, p3, p4, p5)):
+        ghost[at : at + rows, :] = piece[...]
+    ghost[496:512, :] = jnp.zeros((16, COL), BF16)
+    sums = [None] * 3
+    for ez in range(TZ):
+        lanes = slice(ez * 512, (ez + 1) * 512)
+        high, low = slot_columns(o_ref, ez)
+        both = jnp.dot(
+            slot_onehot(high, low, 4), ghost[:, lanes], preferred_element_type=F32
+        )
+        resid = (t_ref[:, lanes] - blend(both, w_ref[:, lanes])).astype(BF16)
+        for c in range(3):
+            part = jnp.dot(
+                mg_ref[c, :, lanes] * resid, table_ref[lanes, :], preferred_element_type=F32
+            )
+            sums[c] = part if ez == 0 else sums[c] + part
+    for c in range(3):
+        part = jnp.transpose(sums[c], (1, 0))
+        l_ref[c * 32 : (c + 1) * 32, :] = part[:32] + part[32:64]
+    choice = onehot(lane_map(maps_ref, "l_ysend"), ROWS)
+    loads = l_ref[...]
+    top = loads.astype(BF16)
+    rest = (loads - top.astype(F32)).astype(BF16)
+    msg_ref[:CROWS, :] = cy_ref[...]
+    msg_ref[CROWS:, :] = jnp.dot(
+        jnp.concatenate([top, rest], axis=0), choice, preferred_element_type=F32
     ).astype(BF16)
 
 
-def warp_kernel(
-    s_ref, w_ref, m_ref, g_ref, n_ref, p0, p1, p2, p3, o_ref, table_ref, index_ref, cy_ref,
-    l_ref, msg_ref, ghost, image,
-):
-    ez = pl.program_id(0)
-    ghost[496:512, :] = jnp.zeros((16, 512), BF16)
-    for at, rows, piece in zip(GHOST_AT, GHOST_ROWS, (p0, p1, p2, p3)):
-        ghost[at : at + rows, :] = piece[...]
-    high, low = slot_columns(o_ref, ez)
-    both = jnp.dot(
-        slot_onehot(high, low, 4), ghost[...], preferred_element_type=F32
-    ) + n_ref[...].astype(F32)
-    w = w_ref[...].astype(F32)
-    warped = w * both[:ROWS] + (1.0 - w) * both[ROWS:]
-    resid = (s_ref[...].astype(F32) - warped).astype(BF16)
-    weighted = resid * m_ref[...].astype(F32).astype(BF16)
-    for c in range(3):
-        image[c] = g_ref[c] * weighted
-
-    @pl.when(ez == 0)
-    def _():
-        l_ref[...] = jnp.zeros_like(l_ref)
-
-    for c in range(3):
-        part = matmul_nt(table_ref[...], image[c])
-        l_ref[c * 32 : (c + 1) * 32, :] += part[:32] + part[32:]
-
-    @pl.when(ez == TZ - 1)
-    def _():
-        choice = onehot(index_ref[...], ROWS)
-        loads = l_ref[...]
-        top = loads.astype(BF16)
-        rest = (loads - top.astype(F32)).astype(BF16)
-        msg_ref[:CROWS, :] = cy_ref[...]
-        msg_ref[CROWS:, :] = jnp.dot(
-            jnp.concatenate([top, rest], axis=0), choice, preferred_element_type=F32
-        ).astype(BF16)
-
-
 def powers_kernel(
-    edge_ref, own_ref, y_ref, xlo_ref, xhi_ref, cindex_ref, index_ref, coord_ref, own_index_ref,
-    hown_ref, v_ref, dots_ref, us, fs, h_ref,
+    edge_ref, lown_ref, xlo_ref, xhi_ref, hchoice_ref, lchoice_ref, maps_ref, ochoice_ref,
+    hown_ref, v_ref, dots_ref, h_ref, us, fs,
 ):
     row = lax.broadcasted_iota(jnp.int32, (8, GRID), 0)
-    beyond_x = (coord_ref[0:1, :] >= TX) & (edge_ref[0] == 1)
-    beyond_y = (coord_ref[1:2, :] >= TY) & (edge_ref[1] == 1)
+    beyond_x = (lane_map(maps_ref, "x") >= TX) & (edge_ref[0] == 1)
+    beyond_y = (lane_map(maps_ref, "y") >= TY) & (edge_ref[1] == 1)
     live = jnp.where(beyond_x | beyond_y, 0.0, 1.0)
 
     def scatter(f):
@@ -375,24 +431,17 @@
         lax.fori_loop(0, GRID // 128, tile_step, 0)
         return scatter(lambda j, l, c: fs[(j * 2 + l) * 3 + c])
 
-    ghosts = jnp.concatenate([y_ref[:CROWS, :], xlo_ref[:CROWS, :], xhi_ref[:CROWS, :]], axis=1)
-    placed = jnp.dot(ghosts, onehot(cindex_ref[...] - ROWS, 384), preferred_element_type=F32)
-    for tile in range(GRID // 128):
-        h_ref[tile] = placed[:, tile * 128 : (tile + 1) * 128] + hown_ref[tile]
-    top = own_ref[...].astype(BF16)
-    rest = (own_ref[...] - top.astype(F32)).astype(BF16)
+    placed = jnp.dot(xlo_ref[:CROWS, :], hchoice_ref[:, :256], preferred_element_type=F32)
+    for tile in range(2):
+        h_ref[tile] = hown_ref[tile] + placed[:, tile * 128 : (tile + 1) * 128]
+    h_ref[6] = hown_ref[6] + jnp.dot(
+        xhi_ref[:CROWS, :], hchoice_ref[:, 256:], preferred_element_type=F32
+    )
     source = jnp.concatenate(
-        [
-            jnp.concatenate([top, rest], axis=0),
-            y_ref[CROWS:, :],
-            xlo_ref[CROWS : CROWS + 192, :],
-            xlo_ref[CROWS + 192 :, :],
-            xhi_ref[CROWS:, :],
-        ],
-        axis=1,
-    )
-    loads = jnp.dot(source, onehot(index_ref[...], GRID), preferred_element_type=F32)
-    loads = loads[:96] + loads[96:]
+        [xlo_ref[CROWS : CROWS + 192, :], xlo_ref[CROWS + 192 :, :], xhi_ref[CROWS:, :]], axis=1
+    )
+    placed = jnp.dot(source, lchoice_ref[...], preferred_element_type=F32)
+    loads = lown_ref[...] + placed[:96] + placed[96:]
 
     def load_rows(j, l, c):
         at = c * 32 + (j * 2 + l) * 8
@@ -407,7 +456,7 @@
             pieces.append(
                 jnp.where(row < 4, lower, jnp.where(row == 4, pltpu.roll(upper, 1, axis=0), 0.0))
             )
-    own = select_lanes(jnp.concatenate(pieces, axis=0), onehot(own_index_ref[...], GRID), 3)
+    own = select_lanes(jnp.concatenate(pieces, axis=0), ochoice_ref[...], 3)
     v_ref[...] = own
     lane = lax.broadcasted_iota(jnp.int32, (1, 128), 1)
     dots = jnp.zeros((1, 128), F32)
@@ -482,13 +531,14 @@
     return pl.BlockSpec(shape, lambda *_: (0,) * len(shape))
 
 
-def call(kernel, outs, *args, name, us):
+def call(kernel, outs, *args, name, us, scratch=(), vmem=8):
     return pl.pallas_call(
         kernel,
         out_shape=outs,
         in_specs=[pl.BlockSpec(memory_space=pltpu.VMEM)] * len(args),
         out_specs=jax.tree.map(lambda _: pl.BlockSpec(memory_space=pltpu.VMEM), outs),
-        compiler_params=pltpu.CompilerParams(vmem_limit_bytes=VMEM_LIMIT),
+        scratch_shapes=scratch,
+        compiler_params=pltpu.CompilerParams(vmem_limit_bytes=vmem * 2**20),
         cost_estimate=cost(us),
         name=name,
     )(*args)
@@ -499,7 +549,7 @@
 
 
 def cost(us):
-    return pl.CostEstimate(flops=0, transcendentals=0, bytes_accessed=int(us * 3.0e6))
+    return pl.CostEstimate(flops=int(us * 1.1e9), transcendentals=0, bytes_accessed=0)
 
 
 def shifted(value, dx, dy):
@@ -521,132 +571,87 @@
     mask = sample_mask.reshape(ROWS, COL)
     moved = deformed_scan.reshape(ROWS, COL)
     moves = jnp.transpose(offsets, (0, 1, 3, 2))
+    maps = jnp.asarray(lane_maps())
     lanes = lambda rows: pl.BlockSpec((rows, 512), lambda i: (0, i))
-    params = pltpu.CompilerParams(vmem_limit_bytes=VMEM_LIMIT)
+    params = pltpu.CompilerParams(vmem_limit_bytes=8 * 2**20)
     bf = functools.partial(struct, dtype=BF16)
 
-    ends = deformed_scan.reshape(TX, TY // 8, 8, COL)
-    ylast, yfirst = pl.pallas_call(
-        pack_y_kernel,
-        out_shape=(bf(64, COL), bf(64, COL)),
-        grid=(2,),
-        in_specs=[
-            pl.BlockSpec((TX, None, 8, COL // 2), lambda i: (0, TY // 8 - 1, 0, i)),
-            pl.BlockSpec((TX, None, 8, COL // 2), lambda i: (0, 0, 0, i)),
+    vmem = pl.BlockSpec(memory_space=pltpu.VMEM)
+    up, down, ylast, yfirst = pl.pallas_call(
+        pack_kernel,
+        out_shape=(bf(4, TY // 8, 8, COL), bf(5, TY // 8, 8, COL), bf(64, COL), bf(64, COL)),
+        in_specs=[pl.BlockSpec(memory_space=pltpu.HBM)],
+        out_specs=(vmem,) * 4,
+        scratch_shapes=[
+            pltpu.VMEM((2, TX, 1, 8, COL), BF16),
+            pltpu.SemaphoreType.DMA((4,)),
         ],
-        out_specs=(pl.BlockSpec((64, COL // 2), lambda i: (0, i)),) * 2,
         compiler_params=params,
-        cost_estimate=cost(2),
-        name="pack_y",
-    )(ends, ends)
+        cost_estimate=cost(8),
+        name="pack",
+    )(deformed_scan.reshape(TX, TY // 8, 8, COL))
+    xlo = shifted(up.reshape(128, COL), 1, 0)
+    xhi = shifted(down.reshape(160, COL), -1, 0)
+    moves, ylast = lax.optimization_barrier((moves, ylast))
     ylo, yhi = shifted(ylast, 0, 1), shifted(yfirst, 0, -1)
-    anywhere = pl.BlockSpec(memory_space=pl.ANY)
-    up, down = pl.pallas_call(
-        pack_x_kernel,
-        out_shape=(bf(160, COL), bf(208, COL)),
-        in_specs=[anywhere] * 3,
-        out_specs=(anywhere, anywhere),
-        scratch_shapes=[pltpu.SemaphoreType.DMA((6,))],
-        compiler_params=params,
-        cost_estimate=cost(2),
-        name="pack_x",
-    )(moved, ylo, yhi)
-    grad, mask, moves, up, down = lax.optimization_barrier((grad, mask, moves, up, down))
-    xlo, xhi = shifted(up, 1, 0), shifted(down, -1, 0)
-
-    coefs, coefs_y, coefs_x = pl.pallas_call(
+    partial_image, after = call(
+        own_samples_kernel, (struct(ROWS, COL), struct(8, 128)), scan, weights, moved, moves,
+        name="own_samples", us=5, vmem=14,
+    )
+    up, down = call(
+        corner_kernel, (bf(32, COL), bf(48, COL)), ylo, yhi, after, name="corners", us=6
+    )
+    maps_late, up = lax.optimization_barrier((maps, up))
+    clo, chi = shifted(up, 1, 0), shifted(down, -1, 0)
+
+    coefs, coefs_y, coefs_x, masked = call(
         hessian_kernel,
-        out_shape=(bf(CROWS, ROWS), bf(CROWS, 128), bf(CROWS, 256)),
-        grid=(2,),
-        in_specs=[
-            pl.BlockSpec((3, 256, COL), lambda i: (0, i, 0)),
-            pl.BlockSpec((256, COL), lambda i: (i, 0)),
-            whole((HROWS, COL)),
-            whole((1, 128)),
-            whole((1, 256)),
-        ],
-        out_specs=(
-            pl.BlockSpec((CROWS, 256), lambda i: (0, i)),
-            whole((CROWS, 128)),
-            whole((CROWS, 256)),
-        ),
-        compiler_params=params,
-        cost_estimate=cost(9),
-        name="hessian",
-    )(
-        grad, mask, jnp.asarray(hessian_table()), jnp.asarray(H_YSEND),
-        jnp.asarray(np.where(H_XSEND < ROWS, H_XSEND, -1)),
-    )
-    own_samples = pl.pallas_call(
-        own_samples_kernel,
-        out_shape=bf(2 * ROWS, COL),
-        grid=(TZ,),
-        in_specs=[lanes(ROWS), whole((2, TX, TZ, TY))],
-        out_specs=lanes(2 * ROWS),
-        compiler_params=params,
-        cost_estimate=cost(7),
-        name="own_samples",
-    )(moved, moves)
-    stiffness = call(
-        grid_kernel, struct(GRID // 128, CROWS, 128), coefs, jnp.asarray(H_GRID),
-        name="hessian_grid", us=3,
-    )
-
-    loads, message = pl.pallas_call(
+        (bf(CROWS, ROWS), bf(CROWS, 128), bf(CROWS, 256), bf(3, ROWS, COL)),
+        grad, mask, jnp.asarray(hessian_table()), maps_late,
+        name="hessian", us=6,
+    )
+    loads, message = call(
         warp_kernel,
-        out_shape=(struct(96, ROWS), bf(CROWS + 192, 128)),
-        grid=(TZ,),
-        in_specs=[
-            lanes(ROWS), lanes(ROWS), lanes(ROWS),
-            pl.BlockSpec((3, ROWS, 512), lambda i: (0, 0, i)),
-            lanes(2 * ROWS),
-            *[lanes(rows) for rows in GHOST_ROWS],
-            whole((2, TX, TZ, TY)),
-            lanes(64),
-            whole((1, 128)),
-            whole((CROWS, 128)),
-        ],
-        out_specs=(whole((96, ROWS)), whole((CROWS + 192, 128))),
-        scratch_shapes=[pltpu.VMEM((512, 512), BF16), pltpu.VMEM((3, ROWS, 512), BF16)],
-        compiler_params=params,
-        cost_estimate=cost(9),
-        name="warp",
-    )(
-        scan, weights, mask, grad, own_samples, xlo, xhi, ylo, yhi, moves,
-        jnp.asarray(load_table()), jnp.asarray(L_YSEND), coefs_y,
+        (struct(96, ROWS), bf(CROWS + 192, 128)),
+        partial_image, weights, masked, xlo, clo, xhi, chi, ylo, yhi, moves,
+        jnp.asarray(load_table()), maps, coefs_y,
+        name="warp", us=6, vmem=14, scratch=[pltpu.VMEM((512, COL), BF16)],
     )
     below, above = shifted(message, 0, 1), shifted(message, 0, -1)
     ytile, up, down = call(
         edge_kernel,
         (bf(CROWS + 192, 128), bf(CROWS + 384, 128), bf(CROWS + 192, 128)),
-        loads, coefs_x, below, above, jnp.asarray(H_XSEND), jnp.asarray(L_XSEND),
+        loads, coefs_x, below, above, maps,
         name="edges", us=2,
     )
-    ghosts = (ytile, shifted(up, 1, 0), shifted(down, -1, 0))
-
-    position = np.arange(GRID)
-    coord = np.stack([position // PITCH - 4, position % PITCH - 4]).astype(np.int32)
+    ghosts = (shifted(up, 1, 0), shifted(down, -1, 0))
+    stiffness, loads_grid, *choices = call(
+        grid_kernel,
+        (
+            struct(GRID // 128, CROWS, 128), struct(96, GRID),
+            bf(128, 384), bf(384, GRID), bf(GRID, ROWS),
+        ),
+        coefs, loads, ytile, maps,
+        name="grid", us=3,
+    )
+
     last = jnp.stack(
         [lax.axis_index("gx") == lax.axis_size("gx") - 1, lax.axis_index("gy") == lax.axis_size("gy") - 1]
     ).astype(jnp.int32)
-    vmem = pl.BlockSpec(memory_space=pltpu.VMEM)
     devices = lax.axis_size("gx") * lax.axis_size("gy")
-    vectors, dots = pl.pallas_call(
+    vectors, dots, _ = pl.pallas_call(
         powers_kernel,
-        out_shape=(struct(96, ROWS), struct(devices, 128)),
-        in_specs=[pl.BlockSpec(memory_space=pltpu.SMEM)] + [vmem] * 9,
-        out_specs=(vmem, vmem),
-        scratch_shapes=[
-            pltpu.VMEM((24, 8, GRID), F32),
-            pltpu.VMEM((12, 8, GRID), F32),
-            pltpu.VMEM((GRID // 128, CROWS, 128), F32),
-        ],
+        out_shape=(struct(96, ROWS), struct(devices, 128), struct(GRID // 128, CROWS, 128)),
+        in_specs=[pl.BlockSpec(memory_space=pltpu.SMEM)] + [vmem] * 8,
+        out_specs=(vmem,) * 3,
+        scratch_shapes=[pltpu.VMEM((24, 8, GRID), F32), pltpu.VMEM((12, 8, GRID), F32)],
+        input_output_aliases={8: 2},
         compiler_params=params,
-        cost_estimate=cost(9),
+        cost_estimate=cost(6),
         name="powers",
     )(
-        last, loads, *ghosts, jnp.asarray(H_GRID), jnp.asarray(L_GRID), jnp.asarray(coord),
-        jnp.asarray(OWN_MAP), stiffness,
+        last, loads_grid, *ghosts, choices[0], choices[1], maps, choices[2],
+        stiffness,
     )
     dots = lax.all_to_all(dots, ("gx", "gy"), 0, 0, tiled=True)
     increment, resid = call(

time: 103 us -> 92.2 us (0.90)
  waiting for transfers between devices: 18.1 us -> 9.57 us
  Pallas kernels: 31.5 us -> 24.8 us
  starting transfers between devices: 24.9 us -> 29.9 us
    pallas_call x5 -> x1, Pallas kernels: 22.2 us -> 0.8 us  [per_device(): pl.pallas_call(pack_kernel, out_shape=(bf(4, TY // 8, 8, COL), bf(5, TY /...]
    pallas_call x3 -> x7, Pallas kernels: 2.66 us -> 18.4 us  [call(): pl.pallas_call(kernel, out_shape=outs, in_specs=[pl.BlockSpec(memory_spac...]
    ppermute x8 -> x10, waiting for transfers between devices: 18.1 us -> 9.57 us  [shifted(): return lax.ppermute(value, ('gx', 'gy'), pairs)]
    ppermute x8 -> x10, starting transfers between devices: 24.9 us -> 29.9 us  [shifted(): return lax.ppermute(value, ('gx', 'gy'), pairs)]
    pallas_call x1, Pallas kernels: 6.64 us -> 5.59 us  [per_device(): pl.pallas_call(powers_kernel, out_shape=(struct(96, ROWS), struct(devices...]
  transfers between devices with their start and end apart: 8 -> 10, of which waited for: 6 -> 4; matrix products, arithmetic and copies ran while one was open for 0% -> 0% of each run, Pallas kernels for 11% -> 11%
where the time goes in v3:
time: 92.2 us; the launch traced here: 91.8 us
  starting transfers between devices  29.9 us (32%)
  blocking collectives  24.9 us (27%)
  Pallas kernels  24.8 us (27%)
  waiting for transfers between devices  9.57 us (10%)
  local copies, waits for them, and re-layouts  1.64 us (2%)
  between operations  0.96 us (1%)
    ppermute x10, starting transfers between devices, shifted(): return lax.ppermute(value, ('gx', 'gy'), pairs)  29.9 us
    all_to_all x1, blocking collectives, per_device(): dots = lax.all_to_all(dots, ('gx', 'gy'), 0, 0, tiled=True)  24.9 us
    pallas_call x7, Pallas kernels, call(): pl.pallas_call(kernel, out_shape=outs, in_specs=[pl.BlockSpec(memory_spac...  18.4 us
    ppermute x10, waiting for transfers between devices, shifted(): return lax.ppermute(value, ('gx', 'gy'), pairs)  9.57 us
    pallas_call x1, Pallas kernels, per_device(): pl.pallas_call(powers_kernel, out_shape=(struct(96, ROWS), struct(devices...  5.59 us
  transfers between devices with their start and end apart: 10, of which 4 were waited for; matrix products, arithmetic and copies ran while one was open for 0% of the time, Pallas kernels for 11%

profile of v3, /device:TPU:1, one launch (start us, length us, event | category | flops | bytes accessed | tf_op | source)
XLA Modules:
  0.0 91.8 jit_solution(5781117943520901587)
XLA Ops:
  0.6 0.0 copy-start.2
  0.6 1.6 %copy-done.2 = bf16[16,32,2048]{2,1,0:T(8,128)(2,1)S(1)} copy-done((bf16[16,32,2048]{2,1,0:T(8,128)(2,1)S(1)}, bf16[16,32,2048]{2,1,0:T(8,128)(2,1)}, u32[]{:S(2)}) %copy-start.2) | copy-done | bytes 2097176
  2.2 0.0 copy-start.1
  2.2 0.0 copy-start.3
  2.2 0.0 copy-start.4
  2.2 0.0 copy-start.5
  2.2 0.8 pack.1
  3.0 4.9 %collective-permute-start = (bf16[64,2048]{1,0:T(8,128)(2,1)S(1)}, bf16[64,2048]{1,0:T(8,128)(2,1)S(1)}, u32[]{:S(2)}, u32[]{:S(2)}) collective-permute-start(bf16[64,2048]{1,0:T(8,128)(2,1)S(1)} %get-tuple-element.33), channel_id=1, source_target_pairs={{0,1},{1,2},{2,3},{3,4},{4,5},{5,6},{6,7},{8,9},{9,10},{10,11},{11... | collective-permute-start | bytes 786440 | tf_op jit(solution)/shard_map/ppermute | solution.py:562
  7.9 1.9 %collective-permute-start.1 = (bf16[64,2048]{1,0:T(8,128)(2,1)S(1)}, bf16[64,2048]{1,0:T(8,128)(2,1)S(1)}, u32[]{:S(2)}, u32[]{:S(2)}) collective-permute-start(bf16[64,2048]{1,0:T(8,128)(2,1)S(1)} %get-tuple-element.34), channel_id=1, source_target_pairs={{1,0},{2,1},{3,2},{4,3},{5,4},{6,5},{7,6},{9,8},{10,9},{11,10},{12... | collective-permute-start | bytes 786440 | tf_op jit(solution)/shard_map/ppermute | solution.py:562
  9.8 3.6 %collective-permute-start.2 = (bf16[128,2048]{1,0:T(8,128)(2,1)S(1)}, bf16[128,2048]{1,0:T(8,128)(2,1)S(1)}, u32[]{:S(2)}, u32[]{:S(2)}) collective-permute-start(bf16[128,2048]{1,0:T(8,128)(2,1)S(1)} %bitcast.33), channel_id=1, source_target_pairs={{0,8},{1,9},{2,10},{3,11},{4,12},{5,13},{6,14},{7,15},{8,16},{9,17... | collective-permute-start | bytes 1572872 | tf_op jit(solution)/shard_map/ppermute | solution.py:562
  13.4 1.3 %collective-permute-start.4 = (bf16[160,2048]{1,0:T(8,128)(2,1)S(1)}, bf16[160,2048]{1,0:T(8,128)(2,1)S(1)}, u32[]{:S(2)}, u32[]{:S(2)}) collective-permute-start(bf16[160,2048]{1,0:T(8,128)(2,1)S(1)} %bitcast.32), channel_id=1, source_target_pairs={{8,0},{9,1},{10,2},{11,3},{12,4},{13,5},{14,6},{15,7},{16,8},{17,9... | collective-permute-start | bytes 1966088 | tf_op jit(solution)/shard_map/ppermute | solution.py:562
  14.7 0.0 copy-done.1
  14.7 0.0 copy-done.3
  14.7 0.0 copy-done.4
  14.8 0.0 copy-done.5
  14.8 0.0 slice-start
  14.8 4.1 %own_samples.1 = (f32[512,2048]{1,0:T(8,128)S(1)}, f32[8,128]{1,0:T(8,128)S(1)}) custom-call(bf16[512,2048]{1,0:T(8,128)(2,1)S(1)} %bitcast.27, bf16[512,2048]{1,0:T(8,128)(2,1)S(1)} %bitcast.30, bf16[512,2048]{1,0:T(8,128)(2,1)S(1)} %bitcast.29, s32[2,16,4,32]{3,2,1,0:T(4,128)S(1)} %bitcast.34), custom_call_target="tpu_custom_call" | custom-call | flops 5500000256 | tf_op jit(solution)/shard_map/own_samples/pallas_call | solution.py:535
  18.9 0.0 collective-permute-done.ylo_ref.p4
  18.9 0.0 collective-permute-done.1.yhi_ref.p5
  18.9 0.0 slice-start.1
  18.9 0.0 copy-start
  18.9 0.0 copy-start.7
  18.9 0.0 copy-start.8
  19.0 4.4 %collective-permute-start.3 = (bf16[32,2048]{1,0:T(8,128)(2,1)S(1)}, bf16[32,2048]{1,0:T(8,128)(2,1)S(1)}, u32[]{:S(2)}, u32[]{:S(2)}) collective-permute-start(bf16[32,2048]{1,0:T(8,128)(2,1)S(1)} %get-tuple-element.43), channel_id=1, source_target_pairs={{0,8},{1,9},{2,10},{3,11},{4,12},{5,13},{6,14},{7,15},{8,16},{9,17... | collective-permute-start | bytes 393224 | tf_op jit(solution)/shard_map/ppermute | solution.py:562
  23.4 1.5 %collective-permute-start.5 = (bf16[48,2048]{1,0:T(8,128)(2,1)S(1)}, bf16[48,2048]{1,0:T(8,128)(2,1)S(1)}, u32[]{:S(2)}, u32[]{:S(2)}) collective-permute-start(bf16[48,2048]{1,0:T(8,128)(2,1)S(1)} %get-tuple-element.45), channel_id=1, source_target_pairs={{8,0},{9,1},{10,2},{11,3},{12,4},{13,5},{14,6},{15,7},{16,8},{17,9... | collective-permute-start | bytes 589832 | tf_op jit(solution)/shard_map/ppermute | solution.py:562
  24.9 0.0 slice-done
  24.9 0.0 slice-done.1
  24.9 0.0 copy-done
  24.9 0.0 copy-done.7
  24.9 0.0 copy-done.8
  24.9 0.0 copy-start.6
  25.0 4.6 %hessian.1 = (bf16[672,512]{1,0:T(8,128)(2,1)S(1)}, bf16[672,128]{1,0:T(8,128)(2,1)S(1)}, bf16[672,256]{1,0:T(8,128)(2,1)S(1)}, bf16[3,512,2048]{2,1,0:T(8,128)(2,1)S(1)}) custom-call(bf16[3,512,2048]{2,1,0:T(8,128)(2,1)S(1)} %bitcast.25, s32[512,2048]{1,0:T(8,128)S(1)} %bitcast.26, bf16[2048,128]{1,0:T(8,128)(2,1)S(1)} %copy-done.7, s32[8,1024]{1,0:T(8,128)S(1)} %copy-done.8), custom_call_target="tpu_custom_call" | custom-call | flops 6600000000 | tf_op jit(solution)/shard_map/hessian/pallas_call | solution.py:535
  29.6 0.0 collective-permute-done.3.p1
  29.6 5.2 %collective-permute-done.5.p3 = bf16[48,2048]{1,0:T(8,128)(2,1)S(1)} collective-permute-done((bf16[48,2048]{1,0:T(8,128)(2,1)S(1)}, bf16[48,2048]{1,0:T(8,128)(2,1)S(1)}, u32[]{:S(2)}, u32[]{:S(2)}) %collective-permute-start.5) | collective-permute-done | bytes 196640 | tf_op jit(solution)/shard_map/ppermute | solution.py:562
  34.8 0.0 collective-permute-done.2.p0
  34.8 0.0 collective-permute-done.4.p2
  34.8 0.0 copy-done.6
  34.8 6.2 %warp.1 = (f32[96,512]{1,0:T(8,128)S(1)}, bf16[864,128]{1,0:T(8,128)(2,1)S(1)}) custom-call(f32[512,2048]{1,0:T(8,128)S(1)} %get-tuple-element.40.t_ref, bf16[512,2048]{1,0:T(8,128)(2,1)S(1)} %bitcast.31, bf16[3,512,2048]{2,1,0:T(8,128)(2,1)S(1)} %get-tuple-element.41.mg_ref, bf16[128,2048]{1,0:T(8,128)(2,1)S(1)} %collective-permute-done.2.p0, ...), custom_call_target="tpu_custom_call" | custom-call | flops 6600000000 | tf_op jit(solution)/shard_map/warp/pallas_call | solution.py:535
  41.0 1.9 %collective-permute-start.7 = (bf16[864,128]{1,0:T(8,128)(2,1)S(1)}, bf16[864,128]{1,0:T(8,128)(2,1)S(1)}, u32[]{:S(2)}, u32[]{:S(2)}) collective-permute-start(bf16[864,128]{1,0:T(8,128)(2,1)S(1)} %get-tuple-element.49), channel_id=1, source_target_pairs={{1,0},{2,1},{3,2},{4,3},{5,4},{6,5},{7,6},{9,8},{10,9},{11,10},{12... | collective-permute-start | bytes 663560 | tf_op jit(solution)/shard_map/ppermute | solution.py:562
  42.9 5.2 %collective-permute-start.6 = (bf16[864,128]{1,0:T(8,128)(2,1)S(1)}, bf16[864,128]{1,0:T(8,128)(2,1)S(1)}, u32[]{:S(2)}, u32[]{:S(2)}) collective-permute-start(bf16[864,128]{1,0:T(8,128)(2,1)S(1)} %get-tuple-element.49), channel_id=1, source_target_pairs={{0,1},{1,2},{2,3},{3,4},{4,5},{5,6},{6,7},{8,9},{9,10},{10,11},{11... | collective-permute-start | bytes 663560 | tf_op jit(solution)/shard_map/ppermute | solution.py:562
  48.1 0.1 add_convert_fusion.edge_ref
  48.1 1.6 %collective-permute-done.7.above_ref = bf16[864,128]{1,0:T(8,128)(2,1)S(1)} collective-permute-done((bf16[864,128]{1,0:T(8,128)(2,1)S(1)}, bf16[864,128]{1,0:T(8,128)(2,1)S(1)}, u32[]{:S(2)}, u32[]{:S(2)}) %collective-permute-start.7) | collective-permute-done | bytes 221216 | tf_op jit(solution)/shard_map/ppermute | solution.py:562
  49.7 1.2 %collective-permute-done.6.below_ref = bf16[864,128]{1,0:T(8,128)(2,1)S(1)} collective-permute-done((bf16[864,128]{1,0:T(8,128)(2,1)S(1)}, bf16[864,128]{1,0:T(8,128)(2,1)S(1)}, u32[]{:S(2)}, u32[]{:S(2)}) %collective-permute-start.6) | collective-permute-done | bytes 221216 | tf_op jit(solution)/shard_map/ppermute | solution.py:562
  50.9 0.4 edges.1
  51.3 1.3 %collective-permute-start.9 = (bf16[864,128]{1,0:T(8,128)(2,1)S(1)}, bf16[864,128]{1,0:T(8,128)(2,1)S(1)}, u32[]{:S(2)}, u32[]{:S(2)}) collective-permute-start(bf16[864,128]{1,0:T(8,128)(2,1)S(1)} %get-tuple-element.53), channel_id=1, source_target_pairs={{8,0},{9,1},{10,2},{11,3},{12,4},{13,5},{14,6},{15,7},{16,8},{17,9... | collective-permute-start | bytes 663560 | tf_op jit(solution)/shard_map/ppermute | solution.py:562
  52.6 4.0 %collective-permute-start.8 = (bf16[1056,128]{1,0:T(8,128)(2,1)S(1)}, bf16[1056,128]{1,0:T(8,128)(2,1)S(1)}, u32[]{:S(2)}, u32[]{:S(2)}) collective-permute-start(bf16[1056,128]{1,0:T(8,128)(2,1)S(1)} %get-tuple-element.52), channel_id=1, source_target_pairs={{0,8},{1,9},{2,10},{3,11},{4,12},{5,13},{6,14},{7,15},{8,16},{9,17... | collective-permute-start | bytes 811016 | tf_op jit(solution)/shard_map/ppermute | solution.py:562
  56.6 1.8 %grid.1 = (f32[8,672,128]{2,1,0:T(8,128)S(1)}, f32[96,1024]{1,0:T(8,128)S(1)}, bf16[128,384]{1,0:T(8,128)(2,1)S(1)}, bf16[384,1024]{1,0:T(8,128)(2,1)S(1)}, bf16[1024,512]{1,0:T(8,128)(2,1)S(1)}) custom-call(bf16[672,512]{1,0:T(8,128)(2,1)S(1)} %get-tuple-element.39.own_ref, f32[96,512]{1,0:T(8,128)S(1)} %get-tuple-element.47.l_ref, ...), custom_call_target="tpu_custom_call" | custom-call | flops 3300000000 | tf_op jit(solution)/shard_map/grid/pallas_call | solution.py:535
  58.4 0.0 collective-permute-done.9.xhi_ref
  58.4 1.6 %collective-permute-done.8.xlo_ref = bf16[1056,128]{1,0:T(8,128)(2,1)S(1)} collective-permute-done((bf16[1056,128]{1,0:T(8,128)(2,1)S(1)}, bf16[1056,128]{1,0:T(8,128)(2,1)S(1)}, u32[]{:S(2)}, u32[]{:S(2)}) %collective-permute-start.8) | collective-permute-done | bytes 270368 | tf_op jit(solution)/shard_map/ppermute | solution.py:562
  60.0 5.6 %powers.1 = (f32[96,512]{1,0:T(8,128)S(1)}, f32[128,128]{1,0:T(8,128)S(1)}, f32[8,672,128]{2,1,0:T(8,128)S(1)}) custom-call(s32[2]{0:T(128)S(1)} %add_convert_fusion.edge_ref, f32[96,1024]{1,0:T(8,128)S(1)} %get-tuple-element.51.lown_ref, bf16[1056,128]{1,0:T(8,128)(2,1)S(1)} %collective-permute-done.8.xlo_ref, ...), custom_call_target="tpu_custom_call", output_to_operand_aliasing={{2}: (8, {})} | custom-call | flops 6600000000 | tf_op jit(solution)/shard_map/powers/pallas_call | solution.py:642
  65.6 24.9 %all_to_all.11 = f32[128,1,128]{2,1,0:T(1,128)S(1)} all-to-all(f32[128,1,128]{2,1,0:T(1,128)S(1)} %bitcast.21), channel_id=1, replica_groups=mesh['gx'=16,'gy'=8] {'gx','gy'}, dimensions={0} | all-to-all | bytes 131072 | tf_op jit(solution)/shard_map/all_to_all | solution.py:656
  90.5 1.4 %combine.1 = (f32[240,32]{1,0:T(8,128)}, f32[240,32]{1,0:T(8,128)}) custom-call(f32[96,512]{1,0:T(8,128)S(1)} %get-tuple-element.58.v_ref, f32[128,128]{1,0:T(8,128)S(1)} %bitcast.22), custom_call_target="tpu_custom_call" | custom-call | flops 3300000000 | tf_op jit(solution)/shard_map/combine/pallas_call | solution.py:535
  (2 shorter events, 0.0 us)
Async XLA Ops:
  0.6 1.6 %copy-start.2 = (bf16[16,32,2048]{2,1,0:T(8,128)(2,1)S(1)}, bf16[16,32,2048]{2,1,0:T(8,128)(2,1)}, u32[]{:S(2)}) copy-start(bf16[16,32,2048]{2,1,0:T(8,128)(2,1)} %param.12) | copy-start | bytes 6291460
  2.2 12.5 %copy-start.1 = (bf16[16,32,2048]{2,1,0:T(8,128)(2,1)S(1)}, bf16[16,32,2048]{2,1,0:T(8,128)(2,1)}, u32[]{:S(2)}) copy-start(bf16[16,32,2048]{2,1,0:T(8,128)(2,1)} %param.10) | copy-start | bytes 6291460
  2.2 12.5 %copy-start.3 = (bf16[16,32,2048]{2,1,0:T(8,128)(2,1)S(1)}, bf16[16,32,2048]{2,1,0:T(8,128)(2,1)}, u32[]{:S(2)}) copy-start(bf16[16,32,2048]{2,1,0:T(8,128)(2,1)} %param.12) | copy-start | bytes 6291460
  2.2 12.5 %copy-start.4 = (bf16[16,32,2048]{2,1,0:T(8,128)(2,1)S(1)}, bf16[16,32,2048]{2,1,0:T(8,128)(2,1)}, u32[]{:S(2)}) copy-start(bf16[16,32,2048]{2,1,0:T(8,128)(2,1)} %param.13) | copy-start | bytes 6291460
  2.2 12.5 %copy-start.5 = (s32[2,16,32,4]{2,3,1,0:T(4,128)S(1)}, s32[2,16,32,4]{2,3,1,0:T(4,128)}, u32[]{:S(2)}) copy-start(s32[2,16,32,4]{2,3,1,0:T(4,128)} %param.15) | copy-start | bytes 49156
  3.0 15.8 %collective-permute-start = (bf16[64,2048]{1,0:T(8,128)(2,1)S(1)}, bf16[64,2048]{1,0:T(8,128)(2,1)S(1)}, u32[]{:S(2)}, u32[]{:S(2)}) collective-permute-start(bf16[64,2048]{1,0:T(8,128)(2,1)S(1)} %get-tuple-element.33), channel_id=1, source_target_pairs={{0,1},{1,2},{2,3},{3,4},{4,5},{5,6},{6,7},{8,9},{9,10},{10,11},{11... | collective-permute-start | bytes 786440 | tf_op jit(solution)/shard_map/ppermute | solution.py:562
  7.9 11.0 %collective-permute-start.1 = (bf16[64,2048]{1,0:T(8,128)(2,1)S(1)}, bf16[64,2048]{1,0:T(8,128)(2,1)S(1)}, u32[]{:S(2)}, u32[]{:S(2)}) collective-permute-start(bf16[64,2048]{1,0:T(8,128)(2,1)S(1)} %get-tuple-element.34), channel_id=1, source_target_pairs={{1,0},{2,1},{3,2},{4,3},{5,4},{6,5},{7,6},{9,8},{10,9},{11,10},{12... | collective-permute-start | bytes 786440 | tf_op jit(solution)/shard_map/ppermute | solution.py:562
  9.8 24.9 %collective-permute-start.2 = (bf16[128,2048]{1,0:T(8,128)(2,1)S(1)}, bf16[128,2048]{1,0:T(8,128)(2,1)S(1)}, u32[]{:S(2)}, u32[]{:S(2)}) collective-permute-start(bf16[128,2048]{1,0:T(8,128)(2,1)S(1)} %bitcast.33), channel_id=1, source_target_pairs={{0,8},{1,9},{2,10},{3,11},{4,12},{5,13},{6,14},{7,15},{8,16},{9,17... | collective-permute-start | bytes 1572872 | tf_op jit(solution)/shard_map/ppermute | solution.py:562
  13.4 21.3 %collective-permute-start.4 = (bf16[160,2048]{1,0:T(8,128)(2,1)S(1)}, bf16[160,2048]{1,0:T(8,128)(2,1)S(1)}, u32[]{:S(2)}, u32[]{:S(2)}) collective-permute-start(bf16[160,2048]{1,0:T(8,128)(2,1)S(1)} %bitcast.32), channel_id=1, source_target_pairs={{8,0},{9,1},{10,2},{11,3},{12,4},{13,5},{14,6},{15,7},{16,8},{17,9... | collective-permute-start | bytes 1966088 | tf_op jit(solution)/shard_map/ppermute | solution.py:562
  14.8 10.1 %slice-start = ((s8[6291456]{0:T(1024)(128)(4,1)}), s8[4194304]{0:T(1024)(128)(4,1)S(1)}, s32[]{:S(2)}) async-start(s8[6291456]{0:T(1024)(128)(4,1)} %bitcast.23), calls=%async_computation.1 | async-start | bytes 8388608
  18.9 6.0 %slice-start.1 = ((s8[6291456]{0:T(1024)(128)(4,1)}), s8[2097152]{0:T(1024)(128)(4,1)S(1)}, s32[]{:S(2)}) async-start(s8[6291456]{0:T(1024)(128)(4,1)} %bitcast.23), calls=%async_computation.2 | async-start | bytes 4194304
  18.9 6.0 %copy-start = (s32[16,32,2048]{2,1,0:T(8,128)S(1)}, s32[16,32,2048]{2,1,0:T(8,128)}, u32[]{:S(2)}) copy-start(s32[16,32,2048]{2,1,0:T(8,128)} %param.14) | copy-start | bytes 12582916
  18.9 6.0 %copy-start.7 = (bf16[2048,128]{1,0:T(8,128)(2,1)S(1)}, bf16[2048,128]{1,0:T(8,128)(2,1)}, u32[]{:S(2)}) copy-start(bf16[2048,128]{1,0:T(8,128)(2,1)} %constant.20.clone.table_ref) | copy-start | bytes 1572868
  18.9 6.0 %copy-start.8 = (s32[8,1024]{1,0:T(8,128)S(1)}, s32[8,1024]{1,0:T(8,128)}, u32[]{:S(2)}) copy-start(s32[8,1024]{1,0:T(8,128)} %constant.19.clone.maps_ref) | copy-start | bytes 98308
  19.0 10.6 %collective-permute-start.3 = (bf16[32,2048]{1,0:T(8,128)(2,1)S(1)}, bf16[32,2048]{1,0:T(8,128)(2,1)S(1)}, u32[]{:S(2)}, u32[]{:S(2)}) collective-permute-start(bf16[32,2048]{1,0:T(8,128)(2,1)S(1)} %get-tuple-element.43), channel_id=1, source_target_pairs={{0,8},{1,9},{2,10},{3,11},{4,12},{5,13},{6,14},{7,15},{8,16},{9,17... | collective-permute-start | bytes 393224 | tf_op jit(solution)/shard_map/ppermute | solution.py:562
  23.4 11.4 %collective-permute-start.5 = (bf16[48,2048]{1,0:T(8,128)(2,1)S(1)}, bf16[48,2048]{1,0:T(8,128)(2,1)S(1)}, u32[]{:S(2)}, u32[]{:S(2)}) collective-permute-start(bf16[48,2048]{1,0:T(8,128)(2,1)S(1)} %get-tuple-element.45), channel_id=1, source_target_pairs={{8,0},{9,1},{10,2},{11,3},{12,4},{13,5},{14,6},{15,7},{16,8},{17,9... | collective-permute-start | bytes 589832 | tf_op jit(solution)/shard_map/ppermute | solution.py:562
  24.9 9.8 %copy-start.6 = (bf16[2048,128]{1,0:T(8,128)(2,1)S(1)}, bf16[2048,128]{1,0:T(8,128)(2,1)}, u32[]{:S(2)}) copy-start(bf16[2048,128]{1,0:T(8,128)(2,1)} %constant.21.clone.table_ref) | copy-start | bytes 1572868
  41.0 8.8 %collective-permute-start.7 = (bf16[864,128]{1,0:T(8,128)(2,1)S(1)}, bf16[864,128]{1,0:T(8,128)(2,1)S(1)}, u32[]{:S(2)}, u32[]{:S(2)}) collective-permute-start(bf16[864,128]{1,0:T(8,128)(2,1)S(1)} %get-tuple-element.49), channel_id=1, source_target_pairs={{1,0},{2,1},{3,2},{4,3},{5,4},{6,5},{7,6},{9,8},{10,9},{11,10},{12... | collective-permute-start | bytes 663560 | tf_op jit(solution)/shard_map/ppermute | solution.py:562
  42.9 8.0 %collective-permute-start.6 = (bf16[864,128]{1,0:T(8,128)(2,1)S(1)}, bf16[864,128]{1,0:T(8,128)(2,1)S(1)}, u32[]{:S(2)}, u32[]{:S(2)}) collective-permute-start(bf16[864,128]{1,0:T(8,128)(2,1)S(1)} %get-tuple-element.49), channel_id=1, source_target_pairs={{0,1},{1,2},{2,3},{3,4},{4,5},{5,6},{6,7},{8,9},{9,10},{10,11},{11... | collective-permute-start | bytes 663560 | tf_op jit(solution)/shard_map/ppermute | solution.py:562
  51.3 7.1 %collective-permute-start.9 = (bf16[864,128]{1,0:T(8,128)(2,1)S(1)}, bf16[864,128]{1,0:T(8,128)(2,1)S(1)}, u32[]{:S(2)}, u32[]{:S(2)}) collective-permute-start(bf16[864,128]{1,0:T(8,128)(2,1)S(1)} %get-tuple-element.53), channel_id=1, source_target_pairs={{8,0},{9,1},{10,2},{11,3},{12,4},{13,5},{14,6},{15,7},{16,8},{17,9... | collective-permute-start | bytes 663560 | tf_op jit(solution)/shard_map/ppermute | solution.py:562
  52.6 7.4 %collective-permute-start.8 = (bf16[1056,128]{1,0:T(8,128)(2,1)S(1)}, bf16[1056,128]{1,0:T(8,128)(2,1)S(1)}, u32[]{:S(2)}, u32[]{:S(2)}) collective-permute-start(bf16[1056,128]{1,0:T(8,128)(2,1)S(1)} %get-tuple-element.52), channel_id=1, source_target_pairs={{0,8},{1,9},{2,10},{3,11},{4,12},{5,13},{6,14},{7,15},{8,16},{9,17... | collective-permute-start | bytes 811016 | tf_op jit(solution)/shard_map/ppermute | solution.py:562

commit v4 on v3

--- a/solution.py
+++ b/solution.py
@@ -59,6 +59,9 @@
     return np.ascontiguousarray(both.T)
 
 
+SPARE = 112
+
+
 def edge_maps(low, high, xlo_lanes, xhi_lanes):
     ysend, ycoord = [], []
     for x in range(TX):
@@ -85,6 +88,11 @@
         return lanes, coord
 
     up, up_coord = strip(TX - low, low, -TX)
+    rest = max(len(up) - 128, 0)
+    half = (rest + 1) // 2
+    up_lanes = list(range(min(len(up), 128)))
+    up_lanes += [128 + SPARE + k for k in range(min(half, rest))]
+    up_lanes += [256 + SPARE + k for k in range(rest - half)]
     down, down_coord = strip(0, high, TX)
     source = {}
     for x in range(TX):
@@ -92,7 +100,7 @@
             source[(x, y)] = x * TY + y
     for n, c in enumerate(ycoord):
         source[c] = ROWS + n
-    for n, c in enumerate(up_coord):
+    for n, c in zip(up_lanes, up_coord):
         source[c] = ROWS + 128 + n
     for n, c in enumerate(down_coord):
         source[c] = ROWS + 128 + xlo_lanes + n
@@ -105,12 +113,14 @@
         out[0, : len(values)] = values
         return out
 
-    xsend = np.concatenate([row(up, xlo_lanes), row(down, xhi_lanes)], axis=1)
+    sent = np.full((1, xlo_lanes), -1, np.int32)
+    sent[0, up_lanes] = up
+    xsend = np.concatenate([sent, row(down, xhi_lanes)], axis=1)
     return row(ysend, 128), xsend, row(list(grid), GRID), low * TX
 
 
 H_YSEND, H_XSEND, H_GRID, H_YLOW = edge_maps(3, 2, 128, 128)
-L_YSEND, L_XSEND, L_GRID, L_YLOW = edge_maps(4, 3, 256, 128)
+L_YSEND, L_XSEND, L_GRID, L_YLOW = edge_maps(4, 3, 384, 128)
 OWN_MAP = np.array(
     [[(x + 4) * PITCH + y + 4 for x in range(TX) for y in range(TY)]], np.int32
 )
@@ -128,7 +138,7 @@
     rows[5, 128:384] = np.where(H_XSEND < ROWS, H_XSEND, -1)
     rows[5, 384:640] = H_XSEND
     rows[6, :128] = L_YSEND
-    rows[6, 128:512] = L_XSEND
+    rows[6, 128:640] = L_XSEND
     return rows
 
 
@@ -142,7 +152,7 @@
     "h_xown": (5, 128, 384),
     "h_xsend": (5, 384, 640),
     "l_ysend": (6, 0, 128),
-    "l_xsend": (6, 128, 512),
+    "l_xsend": (6, 128, 640),
 }
 
 
@@ -180,30 +190,47 @@
     return copies
 
 
-def pack_kernel(d_ref, up_ref, down_ref, last_ref, first_ref, ends, sems):
+def either(flag, yes, no):
+    return jnp.where(jnp.full(yes.shape, flag, jnp.int32) == 1, yes, no)
+
+
+def pack_kernel(flags_ref, d_ref, xa_ref, xb_ref, ya_ref, yb_ref, ends, sems):
+    odd_x, odd_y = flags_ref[2], flags_ref[3]
+    high = TX - 5
     copies = run_copies(
         sems,
         (d_ref.at[pl.ds(0, TX), pl.ds(TY // 8 - 1, 1)], ends.at[0]),
         (d_ref.at[pl.ds(0, TX), pl.ds(0, 1)], ends.at[1]),
-        (d_ref.at[pl.ds(TX - 4, 4)], up_ref),
-        (d_ref.at[pl.ds(0, 5)], down_ref),
+        (d_ref.at[pl.ds(high * odd_x, 5)], xa_ref),
+        (d_ref.at[pl.ds(high - high * odd_x, 5)], xb_ref),
     )
     row = lax.broadcasted_iota(jnp.int32, (64, 128), 0)
     pos = lax.broadcasted_iota(jnp.int32, (64, 128), 1)
-    for k, (out_ref, at) in enumerate(((last_ref, 4), (first_ref, 0))):
+    found = []
+    for k, at in enumerate((4, 0)):
         choice = jnp.where(pos == (row >> 2) * 8 + (row & 3) + at, 1.0, 0.0).astype(BF16)
         copies[k].wait()
         rows = ends[k].astype(F32).reshape(TX * 8, COL).astype(BF16)
-        out_ref[...] = jnp.dot(choice, rows, preferred_element_type=F32).astype(BF16)
+        found.append(jnp.dot(choice, rows, preferred_element_type=F32))
+    last, first = found
+    ya_ref[...] = either(odd_y, last, first).astype(BF16)
+    yb_ref[...] = either(odd_y, first, last).astype(BF16)
     copies[2].wait()
     copies[3].wait()
 
 
-def corner_kernel(ylo_ref, yhi_ref, after_ref, up_ref, down_ref):
-    up_ref[:16, :] = ylo_ref[48:, :]
-    up_ref[16:, :] = yhi_ref[48:, :]
-    down_ref[:24, :] = ylo_ref[:24, :]
-    down_ref[24:, :] = yhi_ref[:24, :]
+def corner_kernel(flags_ref, ya_ref, yb_ref, after_ref, a_ref, b_ref):
+    for odd_x in range(2):
+        for odd_y in range(2):
+
+            @pl.when((flags_ref[2] == odd_x) & (flags_ref[3] == odd_y))
+            def _():
+                low, high = (yb_ref, ya_ref) if odd_y else (ya_ref, yb_ref)
+                up, down = (a_ref, b_ref) if odd_x else (b_ref, a_ref)
+                up[:24, :] = low[40:, :]
+                up[24:, :] = high[40:, :]
+                down[:24, :] = low[:24, :]
+                down[24:, :] = high[:24, :]
 
 
 def hessian_kernel(g_ref, m_ref, table_ref, maps_ref, c_ref, cy_ref, cx_ref, mg_ref):
@@ -227,26 +254,40 @@
 
 
 def edge_kernel(
-    l_ref, cx_ref, below_ref, above_ref, maps_ref, y_ref, up_ref, down_ref
+    flags_ref, l_ref, cx_ref, ya_ref, yb_ref, maps_ref, y_ref, a_ref, b_ref
 ):
     lane = lax.broadcasted_iota(jnp.int32, (1, 128), 1)
-    ytile_c = jnp.where(lane < H_YLOW, below_ref[:CROWS, :], above_ref[:CROWS, :])
-    ytile_l = jnp.where(lane < L_YLOW, below_ref[CROWS:, :], above_ref[CROWS:, :])
+    odd_y = jnp.full((1, 128), flags_ref[3], jnp.int32) == 1
+    ytile_c = jnp.where((lane < H_YLOW) != odd_y, ya_ref[:CROWS, :], yb_ref[:CROWS, :])
+    ytile_l = jnp.where((lane < L_YLOW) != odd_y, ya_ref[CROWS:, :], yb_ref[CROWS:, :])
     y_ref[:CROWS, :] = ytile_c
     y_ref[CROWS:, :] = ytile_l
-    sent = jnp.dot(ytile_c, onehot(lane_map(maps_ref, "h_xsend") - ROWS, 128), preferred_element_type=F32)
-    sent = sent.astype(BF16) + cx_ref[...]
-    up_ref[:CROWS, :] = sent[:, :128]
-    down_ref[:CROWS, :] = sent[:, 128:]
+    sent_c = jnp.dot(
+        ytile_c, onehot(lane_map(maps_ref, "h_xsend") - ROWS, 128), preferred_element_type=F32
+    )
+    sent_c = sent_c.astype(BF16) + cx_ref[...]
     high = l_ref[...].astype(BF16)
     low = (l_ref[...] - high.astype(F32)).astype(BF16)
     source = jnp.concatenate([jnp.concatenate([high, low], axis=0), ytile_l], axis=1)
     sent = jnp.dot(
         source, onehot(lane_map(maps_ref, "l_xsend"), ROWS + 128), preferred_element_type=F32
     ).astype(BF16)
-    up_ref[CROWS : CROWS + 192, :] = sent[:, :128]
-    up_ref[CROWS + 192 :, :] = sent[:, 128:256]
-    down_ref[CROWS:, :] = sent[:, 256:]
+
+    def write(up_ref, down_ref):
+        up_ref[:192, :] = sent_c[:192, :128] + sent[:, 128:256]
+        up_ref[192:384, :] = sent_c[192:384, :128] + sent[:, 256:384]
+        up_ref[384:CROWS, :] = sent_c[384:, :128]
+        up_ref[CROWS:, :] = sent[:, :128]
+        down_ref[:CROWS, :] = sent_c[:, 128:]
+        down_ref[CROWS:, :] = sent[:, 384:]
+
+    @pl.when(flags_ref[2] == 1)
+    def _():
+        write(a_ref, b_ref)
+
+    @pl.when(flags_ref[2] == 0)
+    def _():
+        write(b_ref, a_ref)
 
 
 def grid_kernel(
@@ -265,7 +306,7 @@
     lout_ref[...] = placed[:96] + placed[96:]
     hchoice_ref[:, :256] = onehot(h_map[:, :256] - (ROWS + 128), 128)
     hchoice_ref[:, 256:] = onehot(h_map[:, 768:896] - (ROWS + 256), 128)
-    lchoice_ref[...] = onehot(l_map - (ROWS + 128), 384)
+    lchoice_ref[...] = onehot(l_map - (ROWS + 128), 512)
     ochoice_ref[...] = onehot(lane_map(maps_ref, "own"), GRID)
 
 
@@ -275,10 +316,10 @@
     xmid = (x >= 0) & (x < TX)
     xlo = x < 0
     mid = jnp.where(
-        xmid, x * TY + y, jnp.where(xlo, 512 + (x + 4) * TY + y, 672 + (x - TX) * TY + y)
-    )
-    left = jnp.where(xmid, 880 + x * 4, jnp.where(xlo, 640 + (x + 4) * 4, 832 + (x - TX) * 4))
-    right = jnp.where(xmid, 944 + x * 4, jnp.where(xlo, 656 + (x + 4) * 4, 856 + (x - TX) * 4))
+        xmid, x * TY + y, jnp.where(xlo, 512 + (x + 4) * TY + y, 688 + (x - TX) * TY + y)
+    )
+    left = jnp.where(xmid, 896 + x * 4, jnp.where(xlo, 648 + (x + 4) * 4, 848 + (x - TX) * 4))
+    right = jnp.where(xmid, 960 + x * 4, jnp.where(xlo, 672 + (x + 4) * 4, 872 + (x - TX) * 4))
     return jnp.where(ymid, mid, jnp.where(ylo, left + y + 4, right + y - TY))
 
 
@@ -315,10 +356,6 @@
     return jnp.concatenate([jnp.where(high == float(first + k), hit, zero) for k in range(4)], axis=1)
 
 
-GHOST_AT = (0, 128, 160, 320, 368, 432)
-GHOST_ROWS = (128, 32, 160, 48, 64, 64)
-
-
 def blend(both, w):
     w = w.astype(F32)
     return w * both[:ROWS] + (1.0 - w) * both[ROWS:]
@@ -336,12 +373,27 @@
 
 
 def warp_kernel(
-    t_ref, w_ref, mg_ref, p0, p1, p2, p3, p4, p5, o_ref, table_ref, maps_ref, cy_ref,
+    flags_ref, t_ref, w_ref, mg_ref, xa_ref, xb_ref, ca_ref, cb_ref, ya_ref, yb_ref, o_ref,
+    table_ref, maps_ref, cy_ref,
     l_ref, msg_ref, ghost,
 ):
-    for at, rows, piece in zip(GHOST_AT, GHOST_ROWS, (p0, p1, p2, p3, p4, p5)):
-        ghost[at : at + rows, :] = piece[...]
-    ghost[496:512, :] = jnp.zeros((16, COL), BF16)
+    for odd in range(2):
+
+        @pl.when(flags_ref[2] == odd)
+        def _():
+            xlo, xhi = (xb_ref, xa_ref) if odd else (xa_ref, xb_ref)
+            clo, chi = (cb_ref, ca_ref) if odd else (ca_ref, cb_ref)
+            ghost[:128, :] = xlo[32:, :]
+            ghost[128:176, :] = clo[...]
+            ghost[176:336, :] = xhi[...]
+            ghost[336:384, :] = chi[...]
+
+        @pl.when(flags_ref[3] == odd)
+        def _():
+            ylo, yhi = (yb_ref, ya_ref) if odd else (ya_ref, yb_ref)
+            ghost[384:448, :] = ylo[...]
+            ghost[448:, :] = yhi[...]
+
     sums = [None] * 3
     for ez in range(TZ):
         lanes = slice(ez * 512, (ez + 1) * 512)
@@ -369,12 +421,12 @@
 
 
 def powers_kernel(
-    edge_ref, lown_ref, xlo_ref, xhi_ref, hchoice_ref, lchoice_ref, maps_ref, ochoice_ref,
+    flags_ref, lown_ref, a_ref, b_ref, hchoice_ref, lchoice_ref, maps_ref, ochoice_ref,
     hown_ref, v_ref, dots_ref, h_ref, us, fs,
 ):
     row = lax.broadcasted_iota(jnp.int32, (8, GRID), 0)
-    beyond_x = (lane_map(maps_ref, "x") >= TX) & (edge_ref[0] == 1)
-    beyond_y = (lane_map(maps_ref, "y") >= TY) & (edge_ref[1] == 1)
+    beyond_x = (lane_map(maps_ref, "x") >= TX) & (flags_ref[0] == 1)
+    beyond_y = (lane_map(maps_ref, "y") >= TY) & (flags_ref[1] == 1)
     live = jnp.where(beyond_x | beyond_y, 0.0, 1.0)
 
     def scatter(f):
@@ -431,14 +483,16 @@
         lax.fori_loop(0, GRID // 128, tile_step, 0)
         return scatter(lambda j, l, c: fs[(j * 2 + l) * 3 + c])
 
-    placed = jnp.dot(xlo_ref[:CROWS, :], hchoice_ref[:, :256], preferred_element_type=F32)
+    xlo = either(flags_ref[2], b_ref[...], a_ref[...])
+    xhi = either(flags_ref[2], a_ref[...], b_ref[...])
+    placed = jnp.dot(xlo[:CROWS, :], hchoice_ref[:, :256], preferred_element_type=F32)
     for tile in range(2):
         h_ref[tile] = hown_ref[tile] + placed[:, tile * 128 : (tile + 1) * 128]
     h_ref[6] = hown_ref[6] + jnp.dot(
-        xhi_ref[:CROWS, :], hchoice_ref[:, 256:], preferred_element_type=F32
+        xhi[:CROWS, :], hchoice_ref[:, 256:], preferred_element_type=F32
     )
     source = jnp.concatenate(
-        [xlo_ref[CROWS : CROWS + 192, :], xlo_ref[CROWS + 192 :, :], xhi_ref[CROWS:, :]], axis=1
+        [xlo[CROWS:, :], xlo[:192, :], xlo[192:384, :], xhi[CROWS:, :]], axis=1
     )
     placed = jnp.dot(source, lchoice_ref[...], preferred_element_type=F32)
     loads = lown_ref[...] + placed[:96] + placed[96:]
@@ -531,17 +585,19 @@
     return pl.BlockSpec(shape, lambda *_: (0,) * len(shape))
 
 
-def call(kernel, outs, *args, name, us, scratch=(), vmem=8):
+def call(kernel, outs, *args, name, us, scratch=(), vmem=8, flags=None):
+    operands = args if flags is None else (flags, *args)
+    scalars = [] if flags is None else [pl.BlockSpec(memory_space=pltpu.SMEM)]
     return pl.pallas_call(
         kernel,
         out_shape=outs,
-        in_specs=[pl.BlockSpec(memory_space=pltpu.VMEM)] * len(args),
+        in_specs=scalars + [pl.BlockSpec(memory_space=pltpu.VMEM)] * len(args),
         out_specs=jax.tree.map(lambda _: pl.BlockSpec(memory_space=pltpu.VMEM), outs),
         scratch_shapes=scratch,
         compiler_params=pltpu.CompilerParams(vmem_limit_bytes=vmem * 2**20),
         cost_estimate=cost(us),
         name=name,
-    )(*args)
+    )(*operands)
 
 
 def struct(*shape, dtype=F32):
@@ -552,14 +608,12 @@
     return pl.CostEstimate(flops=int(us * 1.1e9), transcendentals=0, bytes_accessed=0)
 
 
-def shifted(value, dx, dy):
-    nx, ny = lax.axis_size("gx"), lax.axis_size("gy")
+def swapped(value, axis, first):
+    size = lax.axis_size(axis)
     pairs = []
-    for x in range(nx):
-        for y in range(ny):
-            if 0 <= x + dx < nx and 0 <= y + dy < ny:
-                pairs.append((x * ny + y, (x + dx) * ny + y + dy))
-    return lax.ppermute(value, ("gx", "gy"), pairs)
+    for low in range(1 if first else 0, size - 1, 2):
+        pairs += [(low, low + 1), (low + 1, low)]
+    return lax.ppermute(value, axis, pairs)
 
 
 def per_device(
@@ -577,10 +631,19 @@
     bf = functools.partial(struct, dtype=BF16)
 
     vmem = pl.BlockSpec(memory_space=pltpu.VMEM)
-    up, down, ylast, yfirst = pl.pallas_call(
+    at_x, at_y = lax.axis_index("gx"), lax.axis_index("gy")
+    flags = jnp.stack(
+        [
+            at_x == lax.axis_size("gx") - 1,
+            at_y == lax.axis_size("gy") - 1,
+            at_x % 2 == 1,
+            at_y % 2 == 1,
+        ]
+    ).astype(jnp.int32)
+    xa, xb, ya, yb = pl.pallas_call(
         pack_kernel,
-        out_shape=(bf(4, TY // 8, 8, COL), bf(5, TY // 8, 8, COL), bf(64, COL), bf(64, COL)),
-        in_specs=[pl.BlockSpec(memory_space=pltpu.HBM)],
+        out_shape=(bf(5, TY // 8, 8, COL), bf(5, TY // 8, 8, COL), bf(64, COL), bf(64, COL)),
+        in_specs=[pl.BlockSpec(memory_space=pltpu.SMEM), pl.BlockSpec(memory_space=pltpu.HBM)],
         out_specs=(vmem,) * 4,
         scratch_shapes=[
             pltpu.VMEM((2, TX, 1, 8, COL), BF16),
@@ -589,55 +652,51 @@
         compiler_params=params,
         cost_estimate=cost(8),
         name="pack",
-    )(deformed_scan.reshape(TX, TY // 8, 8, COL))
-    xlo = shifted(up.reshape(128, COL), 1, 0)
-    xhi = shifted(down.reshape(160, COL), -1, 0)
-    moves, ylast = lax.optimization_barrier((moves, ylast))
-    ylo, yhi = shifted(ylast, 0, 1), shifted(yfirst, 0, -1)
+    )(flags, deformed_scan.reshape(TX, TY // 8, 8, COL))
+    xa = swapped(xa.reshape(160, COL), "gx", True)
+    xb = swapped(xb.reshape(160, COL), "gx", False)
+    moves, ya = lax.optimization_barrier((moves, ya))
+    ya, yb = swapped(ya, "gy", True), swapped(yb, "gy", False)
     partial_image, after = call(
         own_samples_kernel, (struct(ROWS, COL), struct(8, 128)), scan, weights, moved, moves,
-        name="own_samples", us=5, vmem=14,
-    )
-    up, down = call(
-        corner_kernel, (bf(32, COL), bf(48, COL)), ylo, yhi, after, name="corners", us=6
-    )
-    maps_late, up = lax.optimization_barrier((maps, up))
-    clo, chi = shifted(up, 1, 0), shifted(down, -1, 0)
+        name="own_samples", us=2, vmem=14,
+    )
+    ca, cb = call(
+        corner_kernel, (bf(48, COL), bf(48, COL)), ya, yb, after, name="corners", us=1,
+        flags=flags,
+    )
+    maps_late, ca = lax.optimization_barrier((maps, ca))
+    ca, cb = swapped(ca, "gx", True), swapped(cb, "gx", False)
 
     coefs, coefs_y, coefs_x, masked = call(
         hessian_kernel,
         (bf(CROWS, ROWS), bf(CROWS, 128), bf(CROWS, 256), bf(3, ROWS, COL)),
         grad, mask, jnp.asarray(hessian_table()), maps_late,
-        name="hessian", us=6,
+        name="hessian", us=1,
     )
     loads, message = call(
         warp_kernel,
         (struct(96, ROWS), bf(CROWS + 192, 128)),
-        partial_image, weights, masked, xlo, clo, xhi, chi, ylo, yhi, moves,
+        partial_image, weights, masked, xa, xb, ca, cb, ya, yb, moves,
         jnp.asarray(load_table()), maps, coefs_y,
-        name="warp", us=6, vmem=14, scratch=[pltpu.VMEM((512, COL), BF16)],
-    )
-    below, above = shifted(message, 0, 1), shifted(message, 0, -1)
-    ytile, up, down = call(
-        edge_kernel,
-        (bf(CROWS + 192, 128), bf(CROWS + 384, 128), bf(CROWS + 192, 128)),
-        loads, coefs_x, below, above, maps,
-        name="edges", us=2,
-    )
-    ghosts = (shifted(up, 1, 0), shifted(down, -1, 0))
+        name="warp", us=6, vmem=14, flags=flags, scratch=[pltpu.VMEM((512, COL), BF16)],
+    )
+    ma, mb = swapped(message, "gy", True), swapped(message, "gy", False)
+    ytile, ga, gb = call(
+        edge_kernel, (bf(CROWS + 192, 128),) * 3, loads, coefs_x, ma, mb, maps,
+        name="edges", us=2, flags=flags,
+    )
+    ghosts = (swapped(ga, "gx", True), swapped(gb, "gx", False))
     stiffness, loads_grid, *choices = call(
         grid_kernel,
         (
             struct(GRID // 128, CROWS, 128), struct(96, GRID),
-            bf(128, 384), bf(384, GRID), bf(GRID, ROWS),
+            bf(128, 384), bf(512, GRID), bf(GRID, ROWS),
         ),
         coefs, loads, ytile, maps,
         name="grid", us=3,
     )
 
-    last = jnp.stack(
-        [lax.axis_index("gx") == lax.axis_size("gx") - 1, lax.axis_index("gy") == lax.axis_size("gy") - 1]
-    ).astype(jnp.int32)
     devices = lax.axis_size("gx") * lax.axis_size("gy")
     vectors, dots, _ = pl.pallas_call(
         powers_kernel,
@@ -650,7 +709,7 @@
         cost_estimate=cost(6),
         name="powers",
     )(
-        last, loads_grid, *ghosts, choices[0], choices[1], maps, choices[2],
+        flags, loads_grid, *ghosts, choices[0], choices[1], maps, choices[2],
         stiffness,
     )
     dots = lax.all_to_all(dots, ("gx", "gy"), 0, 0, tiled=True)

time: 92.2 us -> 83.9 us (0.910)
  starting transfers between devices: 29.9 us -> 22.4 us
  Pallas kernels: 24.8 us -> 27.4 us
  waiting for transfers between devices: 9.57 us -> 7 us
    ppermute x10, starting transfers between devices: 29.9 us -> 22.4 us  [swapped(): return lax.ppermute(value, axis, pairs)]
    pallas_call x8, Pallas kernels: 19.2 us -> 21.9 us  [the longest x7 20.4 us: call(): pl.pallas_call(kernel, out_shape=outs, in_specs=scalars + [pl.BlockSpec(m...]
    ppermute x10, waiting for transfers between devices: 9.57 us -> 7 us  [swapped(): return lax.ppermute(value, axis, pairs)]
  transfers between devices with their start and end apart: 10 -> 10, of which waited for: 4 -> 4; matrix products, arithmetic and copies ran while one was open for 0% -> 0% of each run, Pallas kernels for 11% -> 13%
where the time goes in v4:
time: 83.9 us; the launch traced here: 83.6 us
  Pallas kernels  27.4 us (33%)
  blocking collectives  24.1 us (29%)
  starting transfers between devices  22.4 us (27%)
  waiting for transfers between devices  7 us (8%)
  local copies, waits for them, and re-layouts  1.65 us (2%)
  between operations  0.9 us (1%)
    all_to_all x1, blocking collectives, per_device(): dots = lax.all_to_all(dots, ('gx', 'gy'), 0, 0, tiled=True)  24.1 us
    ppermute x10, starting transfers between devices, swapped(): return lax.ppermute(value, axis, pairs)  22.4 us
    pallas_call x7, Pallas kernels, call(): pl.pallas_call(kernel, out_shape=outs, in_specs=scalars + [pl.BlockSpec(m...  20.4 us
    ppermute x10, waiting for transfers between devices, swapped(): return lax.ppermute(value, axis, pairs)  7 us
    pallas_call x1, Pallas kernels, per_device(): pl.pallas_call(powers_kernel, out_shape=(struct(96, ROWS), struct(devices...  5.52 us
  transfers between devices with their start and end apart: 10, of which 4 were waited for; matrix products, arithmetic and copies ran while one was open for 0% of the time, Pallas kernels for 13%

profile of v4, /device:TPU:1, one launch (start us, length us, event | category | flops | bytes accessed | tf_op | source)
XLA Modules:
  0.0 83.6 jit_solution(2742517795653662961)
XLA Ops:
  0.7 0.1 add_convert_fusion.flags_ref
  0.7 0.0 copy-start.4
  0.7 1.6 %copy-done.4 = bf16[16,32,2048]{2,1,0:T(8,128)(2,1)S(1)} copy-done((bf16[16,32,2048]{2,1,0:T(8,128)(2,1)S(1)}, bf16[16,32,2048]{2,1,0:T(8,128)(2,1)}, u32[]{:S(2)}) %copy-start.4) | copy-done | bytes 2097176
  2.3 0.0 copy-start.3
  2.3 0.0 copy-start.5
  2.3 0.0 copy-start.6
  2.3 0.0 copy-start.7
  2.3 1.5 %pack.1 = (bf16[5,4,8,2048]{3,2,1,0:T(8,128)(2,1)S(1)}, bf16[5,4,8,2048]{3,2,1,0:T(8,128)(2,1)S(1)}, bf16[64,2048]{1,0:T(8,128)(2,1)S(1)}, bf16[64,2048]{1,0:T(8,128)(2,1)S(1)}) custom-call(s32[4]{0:T(128)S(1)} %add_convert_fusion.flags_ref, bf16[16,4,8,2048]{3,2,1,0:T(8,128)(2,1)S(1)} %bitcast.30), custom_call_target="tpu_custom_call" | custom-call | flops 8800000000 | tf_op jit(solution)/shard_map/pack/pallas_call | solution.py:643
  3.9 0.8 collective-permute-start.2
  4.7 5.4 %collective-permute-start.3 = (bf16[160,2048]{1,0:T(8,128)(2,1)S(1)}, bf16[160,2048]{1,0:T(8,128)(2,1)S(1)}, u32[]{:S(2)}, u32[]{:S(2)}) collective-permute-start(bf16[160,2048]{1,0:T(8,128)(2,1)S(1)} %bitcast.34), channel_id=1, source_target_pairs={{0,8},{8,0},{16,24},{24,16},{32,40},{40,32},{48,56},{56,48},{64,72... | collective-permute-start | bytes 1966088 | tf_op jit(solution)/shard_map/ppermute | solution.py:616
  10.1 4.3 %collective-permute-start = (bf16[64,2048]{1,0:T(8,128)(2,1)S(1)}, bf16[64,2048]{1,0:T(8,128)(2,1)S(1)}, u32[]{:S(2)}, u32[]{:S(2)}) collective-permute-start(bf16[64,2048]{1,0:T(8,128)(2,1)S(1)} %get-tuple-element.33), channel_id=1, source_target_pairs={{1,2},{2,1},{3,4},{4,3},{5,6},{6,5},{9,10},{10,9},{11,12},{12,11},... | collective-permute-start | bytes 786440 | tf_op jit(solution)/shard_map/ppermute | solution.py:616
  14.4 0.1 collective-permute-start.1
  14.5 0.0 slice-start
  14.5 0.0 copy-done.3
  14.5 0.0 copy-done.5
  14.5 0.0 copy-done.6
  14.6 0.0 copy-done.7
  14.6 0.0 slice-start.1
  14.6 0.0 copy-start
  14.6 4.1 %own_samples.1 = (f32[512,2048]{1,0:T(8,128)S(1)}, f32[8,128]{1,0:T(8,128)S(1)}) custom-call(bf16[512,2048]{1,0:T(8,128)(2,1)S(1)} %bitcast.29, bf16[512,2048]{1,0:T(8,128)(2,1)S(1)} %bitcast.32, bf16[512,2048]{1,0:T(8,128)(2,1)S(1)} %bitcast.31, s32[2,16,4,32]{3,2,1,0:T(4,128)S(1)} %bitcast.36), custom_call_target="tpu_custom_call" | custom-call | flops 2200000000 | tf_op jit(solution)/shard_map/own_samples/pallas_call | solution.py:591
  18.7 0.0 copy-start.1
  18.7 0.0 copy-start.2
  18.7 0.1 collective-permute-done.ya_ref
  18.8 0.0 collective-permute-done.1.yb_ref
  18.8 0.6 corners.1
  19.4 0.7 collective-permute-start.4
  20.0 2.5 %collective-permute-start.5 = (bf16[48,2048]{1,0:T(8,128)(2,1)S(1)}, bf16[48,2048]{1,0:T(8,128)(2,1)S(1)}, u32[]{:S(2)}, u32[]{:S(2)}) collective-permute-start(bf16[48,2048]{1,0:T(8,128)(2,1)S(1)} %get-tuple-element.45), channel_id=1, source_target_pairs={{0,8},{8,0},{16,24},{24,16},{32,40},{40,32},{48,56},{56,48},{64,72... | collective-permute-start | bytes 589832 | tf_op jit(solution)/shard_map/ppermute | solution.py:616
  22.5 0.0 slice-done
  22.5 0.0 slice-done.1
  22.6 0.0 copy-done
  22.6 0.0 copy-done.1
  22.6 0.0 copy-done.2
  22.6 0.0 copy-start.8
  22.6 4.6 %hessian.1 = (bf16[672,512]{1,0:T(8,128)(2,1)S(1)}, bf16[672,128]{1,0:T(8,128)(2,1)S(1)}, bf16[672,256]{1,0:T(8,128)(2,1)S(1)}, bf16[3,512,2048]{2,1,0:T(8,128)(2,1)S(1)}) custom-call(bf16[3,512,2048]{2,1,0:T(8,128)(2,1)S(1)} %bitcast.25, s32[512,2048]{1,0:T(8,128)S(1)} %bitcast.26, bf16[2048,128]{1,0:T(8,128)(2,1)S(1)} %copy-done.1, s32[8,1024]{1,0:T(8,128)S(1)} %copy-done.2), custom_call_target="tpu_custom_call" | custom-call | flops 1100000000 | tf_op jit(solution)/shard_map/hessian/pallas_call | solution.py:591
  27.2 0.0 collective-permute-done.4.ca_ref
  27.2 1.3 %collective-permute-done.5.cb_ref = bf16[48,2048]{1,0:T(8,128)(2,1)S(1)} collective-permute-done((bf16[48,2048]{1,0:T(8,128)(2,1)S(1)}, bf16[48,2048]{1,0:T(8,128)(2,1)S(1)}, u32[]{:S(2)}, u32[]{:S(2)}) %collective-permute-start.5) | collective-permute-done | bytes 196640 | tf_op jit(solution)/shard_map/ppermute | solution.py:616
  28.4 0.0 collective-permute-done.2.xa_ref
  28.5 0.0 collective-permute-done.3.xb_ref
  28.5 0.0 copy-done.8
  28.5 7.0 %warp.1 = (f32[96,512]{1,0:T(8,128)S(1)}, bf16[864,128]{1,0:T(8,128)(2,1)S(1)}) custom-call(s32[4]{0:T(128)S(1)} %add_convert_fusion.flags_ref, f32[512,2048]{1,0:T(8,128)S(1)} %get-tuple-element.40.t_ref, bf16[512,2048]{1,0:T(8,128)(2,1)S(1)} %bitcast.33, bf16[3,512,2048]{2,1,0:T(8,128)(2,1)S(1)} %get-tuple-element.41.mg_ref, ...), custom_call_target="tpu_custom_call" | custom-call | flops 6600000000 | tf_op jit(solution)/shard_map/warp/pallas_call | solution.py:591
  35.5 1.6 %collective-permute-start.7 = (bf16[864,128]{1,0:T(8,128)(2,1)S(1)}, bf16[864,128]{1,0:T(8,128)(2,1)S(1)}, u32[]{:S(2)}, u32[]{:S(2)}) collective-permute-start(bf16[864,128]{1,0:T(8,128)(2,1)S(1)} %get-tuple-element.49), channel_id=1, source_target_pairs={{0,1},{1,0},{2,3},{3,2},{4,5},{5,4},{6,7},{7,6},{8,9},{9,8},{10,11... | collective-permute-start | bytes 663560 | tf_op jit(solution)/shard_map/ppermute | solution.py:616
  37.1 3.1 %collective-permute-start.6 = (bf16[864,128]{1,0:T(8,128)(2,1)S(1)}, bf16[864,128]{1,0:T(8,128)(2,1)S(1)}, u32[]{:S(2)}, u32[]{:S(2)}) collective-permute-start(bf16[864,128]{1,0:T(8,128)(2,1)S(1)} %get-tuple-element.49), channel_id=1, source_target_pairs={{1,2},{2,1},{3,4},{4,3},{5,6},{6,5},{9,10},{10,9},{11,12},{12,11},... | collective-permute-start | bytes 663560 | tf_op jit(solution)/shard_map/ppermute | solution.py:616
  40.2 0.0 collective-permute-done.7.yb_ref
  40.2 4.1 %collective-permute-done.6.ya_ref = bf16[864,128]{1,0:T(8,128)(2,1)S(1)} collective-permute-done((bf16[864,128]{1,0:T(8,128)(2,1)S(1)}, bf16[864,128]{1,0:T(8,128)(2,1)S(1)}, u32[]{:S(2)}, u32[]{:S(2)}) %collective-permute-start.6) | collective-permute-done | bytes 221216 | tf_op jit(solution)/shard_map/ppermute | solution.py:616
  44.3 1.0 %edges.1 = (bf16[864,128]{1,0:T(8,128)(2,1)S(1)}, bf16[864,128]{1,0:T(8,128)(2,1)S(1)}, bf16[864,128]{1,0:T(8,128)(2,1)S(1)}) custom-call(s32[4]{0:T(128)S(1)} %add_convert_fusion.flags_ref, f32[96,512]{1,0:T(8,128)S(1)} %get-tuple-element.47.l_ref, bf16[672,256]{1,0:T(8,128)(2,1)S(1)} %get-tuple-element.48.cx_ref, ...), custom_call_target="tpu_custom_call" | custom-call | flops 2200000000 | tf_op jit(solution)/shard_map/edges/pallas_call | solution.py:591
  45.4 0.7 collective-permute-start.8
  46.1 3.2 %collective-permute-start.9 = (bf16[864,128]{1,0:T(8,128)(2,1)S(1)}, bf16[864,128]{1,0:T(8,128)(2,1)S(1)}, u32[]{:S(2)}, u32[]{:S(2)}) collective-permute-start(bf16[864,128]{1,0:T(8,128)(2,1)S(1)} %get-tuple-element.53), channel_id=1, source_target_pairs={{0,8},{8,0},{16,24},{24,16},{32,40},{40,32},{48,56},{56,48},{64,72... | collective-permute-start | bytes 663560 | tf_op jit(solution)/shard_map/ppermute | solution.py:616
  49.2 1.8 %grid.1 = (f32[8,672,128]{2,1,0:T(8,128)S(1)}, f32[96,1024]{1,0:T(8,128)S(1)}, bf16[128,384]{1,0:T(8,128)(2,1)S(1)}, bf16[512,1024]{1,0:T(8,128)(2,1)S(1)}, bf16[1024,512]{1,0:T(8,128)(2,1)S(1)}) custom-call(bf16[672,512]{1,0:T(8,128)(2,1)S(1)} %get-tuple-element.39.own_ref, f32[96,512]{1,0:T(8,128)S(1)} %get-tuple-element.47.l_ref, ...), custom_call_target="tpu_custom_call" | custom-call | flops 3300000000 | tf_op jit(solution)/shard_map/grid/pallas_call | solution.py:591
  51.0 0.0 collective-permute-done.8.a_ref
  51.0 1.5 %collective-permute-done.9.b_ref = bf16[864,128]{1,0:T(8,128)(2,1)S(1)} collective-permute-done((bf16[864,128]{1,0:T(8,128)(2,1)S(1)}, bf16[864,128]{1,0:T(8,128)(2,1)S(1)}, u32[]{:S(2)}, u32[]{:S(2)}) %collective-permute-start.9) | collective-permute-done | bytes 221216 | tf_op jit(solution)/shard_map/ppermute | solution.py:616
  52.6 5.5 %powers.1 = (f32[96,512]{1,0:T(8,128)S(1)}, f32[128,128]{1,0:T(8,128)S(1)}, f32[8,672,128]{2,1,0:T(8,128)S(1)}) custom-call(s32[4]{0:T(128)S(1)} %add_convert_fusion.flags_ref, f32[96,1024]{1,0:T(8,128)S(1)} %get-tuple-element.51.lown_ref, bf16[864,128]{1,0:T(8,128)(2,1)S(1)} %collective-permute-done.8.a_ref, ...), custom_call_target="tpu_custom_call", output_to_operand_aliasing={{2}: (8, {})} | custom-call | flops 6600000000 | tf_op jit(solution)/shard_map/powers/pallas_call | solution.py:701
  58.1 24.1 %all_to_all.11 = f32[128,1,128]{2,1,0:T(1,128)S(1)} all-to-all(f32[128,1,128]{2,1,0:T(1,128)S(1)} %bitcast.27), channel_id=1, replica_groups=mesh['gx'=16,'gy'=8] {'gx','gy'}, dimensions={0} | all-to-all | bytes 131072 | tf_op jit(solution)/shard_map/all_to_all | solution.py:715
  82.2 1.4 %combine.1 = (f32[240,32]{1,0:T(8,128)}, f32[240,32]{1,0:T(8,128)}) custom-call(f32[96,512]{1,0:T(8,128)S(1)} %get-tuple-element.58.v_ref, f32[128,128]{1,0:T(8,128)S(1)} %bitcast.28), custom_call_target="tpu_custom_call" | custom-call | flops 3300000000 | tf_op jit(solution)/shard_map/combine/pallas_call | solution.py:591
  (1 shorter events, 0.0 us)
Async XLA Ops:
  0.7 1.6 %copy-start.4 = (bf16[16,32,2048]{2,1,0:T(8,128)(2,1)S(1)}, bf16[16,32,2048]{2,1,0:T(8,128)(2,1)}, u32[]{:S(2)}) copy-start(bf16[16,32,2048]{2,1,0:T(8,128)(2,1)} %param.12) | copy-start | bytes 6291460
  2.3 12.2 %copy-start.3 = (bf16[16,32,2048]{2,1,0:T(8,128)(2,1)S(1)}, bf16[16,32,2048]{2,1,0:T(8,128)(2,1)}, u32[]{:S(2)}) copy-start(bf16[16,32,2048]{2,1,0:T(8,128)(2,1)} %param.10) | copy-start | bytes 6291460
  2.3 12.2 %copy-start.5 = (bf16[16,32,2048]{2,1,0:T(8,128)(2,1)S(1)}, bf16[16,32,2048]{2,1,0:T(8,128)(2,1)}, u32[]{:S(2)}) copy-start(bf16[16,32,2048]{2,1,0:T(8,128)(2,1)} %param.12) | copy-start | bytes 6291460
  2.3 12.2 %copy-start.6 = (bf16[16,32,2048]{2,1,0:T(8,128)(2,1)S(1)}, bf16[16,32,2048]{2,1,0:T(8,128)(2,1)}, u32[]{:S(2)}) copy-start(bf16[16,32,2048]{2,1,0:T(8,128)(2,1)} %param.13) | copy-start | bytes 6291460
  2.3 12.2 %copy-start.7 = (s32[2,16,32,4]{2,3,1,0:T(4,128)S(1)}, s32[2,16,32,4]{2,3,1,0:T(4,128)}, u32[]{:S(2)}) copy-start(s32[2,16,32,4]{2,3,1,0:T(4,128)} %param.15) | copy-start | bytes 49156
  3.9 24.6 %collective-permute-start.2 = (bf16[160,2048]{1,0:T(8,128)(2,1)S(1)}, bf16[160,2048]{1,0:T(8,128)(2,1)S(1)}, u32[]{:S(2)}, u32[]{:S(2)}) collective-permute-start(bf16[160,2048]{1,0:T(8,128)(2,1)S(1)} %bitcast.35), channel_id=1, source_target_pairs={{8,16},{16,8},{24,32},{32,24},{40,48},{48,40},{56,64},{64,56},{72,... | collective-permute-start | bytes 1966088 | tf_op jit(solution)/shard_map/ppermute | solution.py:616
  4.7 23.8 %collective-permute-start.3 = (bf16[160,2048]{1,0:T(8,128)(2,1)S(1)}, bf16[160,2048]{1,0:T(8,128)(2,1)S(1)}, u32[]{:S(2)}, u32[]{:S(2)}) collective-permute-start(bf16[160,2048]{1,0:T(8,128)(2,1)S(1)} %bitcast.34), channel_id=1, source_target_pairs={{0,8},{8,0},{16,24},{24,16},{32,40},{40,32},{48,56},{56,48},{64,72... | collective-permute-start | bytes 1966088 | tf_op jit(solution)/shard_map/ppermute | solution.py:616
  10.1 8.7 %collective-permute-start = (bf16[64,2048]{1,0:T(8,128)(2,1)S(1)}, bf16[64,2048]{1,0:T(8,128)(2,1)S(1)}, u32[]{:S(2)}, u32[]{:S(2)}) collective-permute-start(bf16[64,2048]{1,0:T(8,128)(2,1)S(1)} %get-tuple-element.33), channel_id=1, source_target_pairs={{1,2},{2,1},{3,4},{4,3},{5,6},{6,5},{9,10},{10,9},{11,12},{12,11},... | collective-permute-start | bytes 786440 | tf_op jit(solution)/shard_map/ppermute | solution.py:616
  14.4 4.3 %collective-permute-start.1 = (bf16[64,2048]{1,0:T(8,128)(2,1)S(1)}, bf16[64,2048]{1,0:T(8,128)(2,1)S(1)}, u32[]{:S(2)}, u32[]{:S(2)}) collective-permute-start(bf16[64,2048]{1,0:T(8,128)(2,1)S(1)} %get-tuple-element.34), channel_id=1, source_target_pairs={{0,1},{1,0},{2,3},{3,2},{4,5},{5,4},{6,7},{7,6},{8,9},{9,8},{10,11... | collective-permute-start | bytes 786440 | tf_op jit(solution)/shard_map/ppermute | solution.py:616
  14.5 8.0 %slice-start = ((s8[6291456]{0:T(1024)(128)(4,1)}), s8[4194304]{0:T(1024)(128)(4,1)S(1)}, s32[]{:S(2)}) async-start(s8[6291456]{0:T(1024)(128)(4,1)} %bitcast.23), calls=%async_computation.1 | async-start | bytes 8388608
  14.6 8.0 %slice-start.1 = ((s8[6291456]{0:T(1024)(128)(4,1)}), s8[2097152]{0:T(1024)(128)(4,1)S(1)}, s32[]{:S(2)}) async-start(s8[6291456]{0:T(1024)(128)(4,1)} %bitcast.23), calls=%async_computation.2 | async-start | bytes 4194304
  14.6 8.0 %copy-start = (s32[16,32,2048]{2,1,0:T(8,128)S(1)}, s32[16,32,2048]{2,1,0:T(8,128)}, u32[]{:S(2)}) copy-start(s32[16,32,2048]{2,1,0:T(8,128)} %param.14) | copy-start | bytes 12582916
  18.7 3.9 %copy-start.1 = (bf16[2048,128]{1,0:T(8,128)(2,1)S(1)}, bf16[2048,128]{1,0:T(8,128)(2,1)}, u32[]{:S(2)}) copy-start(bf16[2048,128]{1,0:T(8,128)(2,1)} %constant.38.clone.table_ref) | copy-start | bytes 1572868
  18.7 3.9 %copy-start.2 = (s32[8,1024]{1,0:T(8,128)S(1)}, s32[8,1024]{1,0:T(8,128)}, u32[]{:S(2)}) copy-start(s32[8,1024]{1,0:T(8,128)} %constant.37.clone.maps_ref) | copy-start | bytes 98308
  19.4 7.8 %collective-permute-start.4 = (bf16[48,2048]{1,0:T(8,128)(2,1)S(1)}, bf16[48,2048]{1,0:T(8,128)(2,1)S(1)}, u32[]{:S(2)}, u32[]{:S(2)}) collective-permute-start(bf16[48,2048]{1,0:T(8,128)(2,1)S(1)} %get-tuple-element.44), channel_id=1, source_target_pairs={{8,16},{16,8},{24,32},{32,24},{40,48},{48,40},{56,64},{64,56},{72,... | collective-permute-start | bytes 589832 | tf_op jit(solution)/shard_map/ppermute | solution.py:616
  20.0 8.4 %collective-permute-start.5 = (bf16[48,2048]{1,0:T(8,128)(2,1)S(1)}, bf16[48,2048]{1,0:T(8,128)(2,1)S(1)}, u32[]{:S(2)}, u32[]{:S(2)}) collective-permute-start(bf16[48,2048]{1,0:T(8,128)(2,1)S(1)} %get-tuple-element.45), channel_id=1, source_target_pairs={{0,8},{8,0},{16,24},{24,16},{32,40},{40,32},{48,56},{56,48},{64,72... | collective-permute-start | bytes 589832 | tf_op jit(solution)/shard_map/ppermute | solution.py:616
  22.6 5.9 %copy-start.8 = (bf16[2048,128]{1,0:T(8,128)(2,1)S(1)}, bf16[2048,128]{1,0:T(8,128)(2,1)}, u32[]{:S(2)}) copy-start(bf16[2048,128]{1,0:T(8,128)(2,1)} %constant.39.clone.table_ref) | copy-start | bytes 1572868
  35.5 4.7 %collective-permute-start.7 = (bf16[864,128]{1,0:T(8,128)(2,1)S(1)}, bf16[864,128]{1,0:T(8,128)(2,1)S(1)}, u32[]{:S(2)}, u32[]{:S(2)}) collective-permute-start(bf16[864,128]{1,0:T(8,128)(2,1)S(1)} %get-tuple-element.49), channel_id=1, source_target_pairs={{0,1},{1,0},{2,3},{3,2},{4,5},{5,4},{6,7},{7,6},{8,9},{9,8},{10,11... | collective-permute-start | bytes 663560 | tf_op jit(solution)/shard_map/ppermute | solution.py:616
  37.1 7.2 %collective-permute-start.6 = (bf16[864,128]{1,0:T(8,128)(2,1)S(1)}, bf16[864,128]{1,0:T(8,128)(2,1)S(1)}, u32[]{:S(2)}, u32[]{:S(2)}) collective-permute-start(bf16[864,128]{1,0:T(8,128)(2,1)S(1)} %get-tuple-element.49), channel_id=1, source_target_pairs={{1,2},{2,1},{3,4},{4,3},{5,6},{6,5},{9,10},{10,9},{11,12},{12,11},... | collective-permute-start | bytes 663560 | tf_op jit(solution)/shard_map/ppermute | solution.py:616
  45.4 5.7 %collective-permute-start.8 = (bf16[864,128]{1,0:T(8,128)(2,1)S(1)}, bf16[864,128]{1,0:T(8,128)(2,1)S(1)}, u32[]{:S(2)}, u32[]{:S(2)}) collective-permute-start(bf16[864,128]{1,0:T(8,128)(2,1)S(1)} %get-tuple-element.52), channel_id=1, source_target_pairs={{8,16},{16,8},{24,32},{32,24},{40,48},{48,40},{56,64},{64,56},{72,... | collective-permute-start | bytes 663560 | tf_op jit(solution)/shard_map/ppermute | solution.py:616
  46.1 6.5 %collective-permute-start.9 = (bf16[864,128]{1,0:T(8,128)(2,1)S(1)}, bf16[864,128]{1,0:T(8,128)(2,1)S(1)}, u32[]{:S(2)}, u32[]{:S(2)}) collective-permute-start(bf16[864,128]{1,0:T(8,128)(2,1)S(1)} %get-tuple-element.53), channel_id=1, source_target_pairs={{0,8},{8,0},{16,24},{24,16},{32,40},{40,32},{48,56},{56,48},{64,72... | collective-permute-start | bytes 663560 | tf_op jit(solution)/shard_map/ppermute | solution.py:616

commit v5 on v4

--- a/solution.py
+++ b/solution.py
@@ -59,9 +59,6 @@
     return np.ascontiguousarray(both.T)
 
 
-SPARE = 112
-
-
 def edge_maps(low, high, xlo_lanes, xhi_lanes):
     ysend, ycoord = [], []
     for x in range(TX):
@@ -88,11 +85,7 @@
         return lanes, coord
 
     up, up_coord = strip(TX - low, low, -TX)
-    rest = max(len(up) - 128, 0)
-    half = (rest + 1) // 2
-    up_lanes = list(range(min(len(up), 128)))
-    up_lanes += [128 + SPARE + k for k in range(min(half, rest))]
-    up_lanes += [256 + SPARE + k for k in range(rest - half)]
+    up_lanes = list(range(len(up)))
     down, down_coord = strip(0, high, TX)
     source = {}
     for x in range(TX):
@@ -120,7 +113,7 @@
 
 
 H_YSEND, H_XSEND, H_GRID, H_YLOW = edge_maps(3, 2, 128, 128)
-L_YSEND, L_XSEND, L_GRID, L_YLOW = edge_maps(4, 3, 384, 128)
+L_YSEND, L_XSEND, L_GRID, L_YLOW = edge_maps(4, 3, 256, 128)
 OWN_MAP = np.array(
     [[(x + 4) * PITCH + y + 4 for x in range(TX) for y in range(TY)]], np.int32
 )
@@ -138,7 +131,7 @@
     rows[5, 128:384] = np.where(H_XSEND < ROWS, H_XSEND, -1)
     rows[5, 384:640] = H_XSEND
     rows[6, :128] = L_YSEND
-    rows[6, 128:640] = L_XSEND
+    rows[6, 128:512] = L_XSEND
     return rows
 
 
@@ -152,7 +145,7 @@
     "h_xown": (5, 128, 384),
     "h_xsend": (5, 384, 640),
     "l_ysend": (6, 0, 128),
-    "l_xsend": (6, 128, 640),
+    "l_xsend": (6, 128, 512),
 }
 
 
@@ -253,60 +246,63 @@
         ref[...] = jnp.dot(c_ref[...], choice, preferred_element_type=F32).astype(BF16)
 
 
-def edge_kernel(
-    flags_ref, l_ref, cx_ref, ya_ref, yb_ref, maps_ref, y_ref, a_ref, b_ref
-):
+def y_tile(flags_ref, a_ref, b_ref, ylow):
     lane = lax.broadcasted_iota(jnp.int32, (1, 128), 1)
     odd_y = jnp.full((1, 128), flags_ref[3], jnp.int32) == 1
-    ytile_c = jnp.where((lane < H_YLOW) != odd_y, ya_ref[:CROWS, :], yb_ref[:CROWS, :])
-    ytile_l = jnp.where((lane < L_YLOW) != odd_y, ya_ref[CROWS:, :], yb_ref[CROWS:, :])
-    y_ref[:CROWS, :] = ytile_c
-    y_ref[CROWS:, :] = ytile_l
-    sent_c = jnp.dot(
-        ytile_c, onehot(lane_map(maps_ref, "h_xsend") - ROWS, 128), preferred_element_type=F32
-    )
-    sent_c = sent_c.astype(BF16) + cx_ref[...]
+    return jnp.where((lane < ylow) != odd_y, a_ref[...], b_ref[...])
+
+
+def store_pair(flags_ref, up, down, a_ref, b_ref):
+    @pl.when(flags_ref[2] == 1)
+    def _():
+        a_ref[...] = up
+        b_ref[...] = down
+
+    @pl.when(flags_ref[2] == 0)
+    def _():
+        a_ref[...] = down
+        b_ref[...] = up
+
+
+def hessian_edge_kernel(flags_ref, cx_ref, ya_ref, yb_ref, maps_ref, y_ref, a_ref, b_ref):
+    ytile = y_tile(flags_ref, ya_ref, yb_ref, H_YLOW)
+    y_ref[...] = ytile
+    choice = onehot(lane_map(maps_ref, "h_xsend") - ROWS, 128)
+    sent = jnp.dot(ytile, choice, preferred_element_type=F32).astype(BF16) + cx_ref[...]
+    store_pair(flags_ref, sent[:, :128], sent[:, 128:], a_ref, b_ref)
+
+
+def load_edge_kernel(flags_ref, l_ref, ya_ref, yb_ref, maps_ref, y_ref, a_ref, b_ref):
+    ytile = y_tile(flags_ref, ya_ref, yb_ref, L_YLOW)
+    y_ref[...] = ytile
     high = l_ref[...].astype(BF16)
     low = (l_ref[...] - high.astype(F32)).astype(BF16)
-    source = jnp.concatenate([jnp.concatenate([high, low], axis=0), ytile_l], axis=1)
+    source = jnp.concatenate([jnp.concatenate([high, low], axis=0), ytile], axis=1)
     sent = jnp.dot(
         source, onehot(lane_map(maps_ref, "l_xsend"), ROWS + 128), preferred_element_type=F32
     ).astype(BF16)
-
-    def write(up_ref, down_ref):
-        up_ref[:192, :] = sent_c[:192, :128] + sent[:, 128:256]
-        up_ref[192:384, :] = sent_c[192:384, :128] + sent[:, 256:384]
-        up_ref[384:CROWS, :] = sent_c[384:, :128]
-        up_ref[CROWS:, :] = sent[:, :128]
-        down_ref[:CROWS, :] = sent_c[:, 128:]
-        down_ref[CROWS:, :] = sent[:, 384:]
-
-    @pl.when(flags_ref[2] == 1)
-    def _():
-        write(a_ref, b_ref)
-
-    @pl.when(flags_ref[2] == 0)
-    def _():
-        write(b_ref, a_ref)
+    up = jnp.concatenate([sent[:, :128], sent[:, 128:256]], axis=0)
+    down = jnp.concatenate([sent[:, 256:], jnp.zeros((192, 128), BF16)], axis=0)
+    store_pair(flags_ref, up, down, a_ref, b_ref)
 
 
 def grid_kernel(
-    own_ref, l_ref, y_ref, maps_ref,
+    own_ref, l_ref, yh_ref, yl_ref, maps_ref,
     out_ref, lout_ref, hchoice_ref, lchoice_ref, ochoice_ref,
 ):
     h_map, l_map = lane_map(maps_ref, "h_grid"), lane_map(maps_ref, "l_grid")
-    source = jnp.concatenate([own_ref[...], y_ref[:CROWS, :]], axis=1)
+    source = jnp.concatenate([own_ref[...], yh_ref[...]], axis=1)
     placed = jnp.dot(source, onehot(h_map, ROWS + 128), preferred_element_type=F32)
     for tile in range(GRID // 128):
         out_ref[tile] = placed[:, tile * 128 : (tile + 1) * 128]
     top = l_ref[...].astype(BF16)
     rest = (l_ref[...] - top.astype(F32)).astype(BF16)
-    source = jnp.concatenate([jnp.concatenate([top, rest], axis=0), y_ref[CROWS:, :]], axis=1)
+    source = jnp.concatenate([jnp.concatenate([top, rest], axis=0), yl_ref[...]], axis=1)
     placed = jnp.dot(source, onehot(l_map, ROWS + 128), preferred_element_type=F32)
     lout_ref[...] = placed[:96] + placed[96:]
     hchoice_ref[:, :256] = onehot(h_map[:, :256] - (ROWS + 128), 128)
     hchoice_ref[:, 256:] = onehot(h_map[:, 768:896] - (ROWS + 256), 128)
-    lchoice_ref[...] = onehot(l_map - (ROWS + 128), 512)
+    lchoice_ref[...] = onehot(l_map - (ROWS + 128), 384)
     ochoice_ref[...] = onehot(lane_map(maps_ref, "own"), GRID)
 
 
@@ -349,11 +345,19 @@
     return high, low
 
 
-def slot_onehot(high, low, first):
+def slot_onehot(high, low, first, last):
     lane = lax.broadcasted_iota(jnp.int32, low.shape, 1).astype(F32).astype(BF16)
     zero = jnp.zeros(low.shape, BF16)
     hit = jnp.where(low == lane, jnp.ones(low.shape, BF16), zero)
-    return jnp.concatenate([jnp.where(high == float(first + k), hit, zero) for k in range(4)], axis=1)
+    return jnp.concatenate([jnp.where(high == float(first + k), hit, zero) for k in range(last - first)], axis=1)
+
+
+def end_rows(value):
+    return jnp.concatenate([value[:128], value[352:640], value[864:]], axis=0)
+
+
+def middle_rows(value):
+    return jnp.concatenate([value[128:352], value[640:864]], axis=0)
 
 
 def blend(both, w):
@@ -367,14 +371,14 @@
         lanes = slice(ez * 512, (ez + 1) * 512)
         high, low = slot_columns(o_ref, ez)
         both = jnp.dot(
-            slot_onehot(high, low, 0), d_ref[:, lanes], preferred_element_type=F32
+            slot_onehot(high, low, 0, 4), d_ref[:, lanes], preferred_element_type=F32
         )
         out_ref[:, lanes] = s_ref[:, lanes].astype(F32) - blend(both, w_ref[:, lanes])
 
 
 def warp_kernel(
     flags_ref, t_ref, w_ref, mg_ref, xa_ref, xb_ref, ca_ref, cb_ref, ya_ref, yb_ref, o_ref,
-    table_ref, maps_ref, cy_ref,
+    table_ref, maps_ref,
     l_ref, msg_ref, ghost,
 ):
     for odd in range(2):
@@ -398,8 +402,21 @@
     for ez in range(TZ):
         lanes = slice(ez * 512, (ez + 1) * 512)
         high, low = slot_columns(o_ref, ez)
-        both = jnp.dot(
-            slot_onehot(high, low, 4), ghost[:, lanes], preferred_element_type=F32
+        ends, middle = (
+            jnp.dot(
+                slot_onehot(pick(high), pick(low), first, 8),
+                ghost[(first - 4) * 128 :, lanes],
+                preferred_element_type=F32,
+            )
+            for pick, first in ((end_rows, 4), (middle_rows, 7))
+        )
+        count = 224
+        both = jnp.concatenate(
+            [
+                ends[:128], middle[:count], ends[128:288],
+                ends[288:416], middle[count:], ends[416:],
+            ],
+            axis=0,
         )
         resid = (t_ref[:, lanes] - blend(both, w_ref[:, lanes])).astype(BF16)
         for c in range(3):
@@ -414,14 +431,13 @@
     loads = l_ref[...]
     top = loads.astype(BF16)
     rest = (loads - top.astype(F32)).astype(BF16)
-    msg_ref[:CROWS, :] = cy_ref[...]
-    msg_ref[CROWS:, :] = jnp.dot(
+    msg_ref[...] = jnp.dot(
         jnp.concatenate([top, rest], axis=0), choice, preferred_element_type=F32
     ).astype(BF16)
 
 
 def powers_kernel(
-    flags_ref, lown_ref, a_ref, b_ref, hchoice_ref, lchoice_ref, maps_ref, ochoice_ref,
+    flags_ref, lown_ref, ha_ref, hb_ref, la_ref, lb_ref, hchoice_ref, lchoice_ref, maps_ref, ochoice_ref,
     hown_ref, v_ref, dots_ref, h_ref, us, fs,
 ):
     row = lax.broadcasted_iota(jnp.int32, (8, GRID), 0)
@@ -480,20 +496,20 @@
                 fs[key, :, lanes] = acc[key] * SCALE
             return carry
 
-        lax.fori_loop(0, GRID // 128, tile_step, 0)
+        lax.fori_loop(0, GRID // 128, tile_step, 0, unroll=4)
         return scatter(lambda j, l, c: fs[(j * 2 + l) * 3 + c])
 
-    xlo = either(flags_ref[2], b_ref[...], a_ref[...])
-    xhi = either(flags_ref[2], a_ref[...], b_ref[...])
-    placed = jnp.dot(xlo[:CROWS, :], hchoice_ref[:, :256], preferred_element_type=F32)
+    xlo = either(flags_ref[2], hb_ref[...], ha_ref[...])
+    xhi = either(flags_ref[2], ha_ref[...], hb_ref[...])
+    placed = jnp.dot(xlo, hchoice_ref[:, :256], preferred_element_type=F32)
     for tile in range(2):
         h_ref[tile] = hown_ref[tile] + placed[:, tile * 128 : (tile + 1) * 128]
     h_ref[6] = hown_ref[6] + jnp.dot(
-        xhi[:CROWS, :], hchoice_ref[:, 256:], preferred_element_type=F32
-    )
-    source = jnp.concatenate(
-        [xlo[CROWS:, :], xlo[:192, :], xlo[192:384, :], xhi[CROWS:, :]], axis=1
-    )
+        xhi, hchoice_ref[:, 256:], preferred_element_type=F32
+    )
+    xlo = either(flags_ref[2], lb_ref[...], la_ref[...])
+    xhi = either(flags_ref[2], la_ref[...], lb_ref[...])
+    source = jnp.concatenate([xlo[:192], xlo[192:], xhi[:192]], axis=1)
     placed = jnp.dot(source, lchoice_ref[...], preferred_element_type=F32)
     loads = lown_ref[...] + placed[:96] + placed[96:]
 
@@ -674,26 +690,34 @@
         grad, mask, jnp.asarray(hessian_table()), maps_late,
         name="hessian", us=1,
     )
+    ya_h, yb_h = swapped(coefs_y, "gy", True), swapped(coefs_y, "gy", False)
     loads, message = call(
         warp_kernel,
-        (struct(96, ROWS), bf(CROWS + 192, 128)),
+        (struct(96, ROWS), bf(192, 128)),
         partial_image, weights, masked, xa, xb, ca, cb, ya, yb, moves,
-        jnp.asarray(load_table()), maps, coefs_y,
+        jnp.asarray(load_table()), maps,
         name="warp", us=6, vmem=14, flags=flags, scratch=[pltpu.VMEM((512, COL), BF16)],
     )
-    ma, mb = swapped(message, "gy", True), swapped(message, "gy", False)
-    ytile, ga, gb = call(
-        edge_kernel, (bf(CROWS + 192, 128),) * 3, loads, coefs_x, ma, mb, maps,
-        name="edges", us=2, flags=flags,
-    )
-    ghosts = (swapped(ga, "gx", True), swapped(gb, "gx", False))
+    ytile_h, ha, hb = call(
+        hessian_edge_kernel, (bf(CROWS, 128),) * 3, coefs_x, ya_h, yb_h, maps,
+        name="hessian_edges", us=1, flags=flags,
+    )
+    la, lb = swapped(message, "gy", True), swapped(message, "gy", False)
+    ytile_l, la, lb = call(
+        load_edge_kernel, (bf(192, 128), bf(384, 128), bf(384, 128)), loads, la, lb, maps,
+        name="load_edges", us=1, flags=flags,
+    )
+    ghosts = (
+        swapped(ha, "gx", True), swapped(hb, "gx", False),
+        swapped(la, "gx", True), swapped(lb, "gx", False),
+    )
     stiffness, loads_grid, *choices = call(
         grid_kernel,
         (
             struct(GRID // 128, CROWS, 128), struct(96, GRID),
-            bf(128, 384), bf(512, GRID), bf(GRID, ROWS),
+            bf(128, 384), bf(384, GRID), bf(GRID, ROWS),
         ),
-        coefs, loads, ytile, maps,
+        coefs, loads, ytile_h, ytile_l, maps,
         name="grid", us=3,
     )
 
@@ -701,10 +725,10 @@
     vectors, dots, _ = pl.pallas_call(
         powers_kernel,
         out_shape=(struct(96, ROWS), struct(devices, 128), struct(GRID // 128, CROWS, 128)),
-        in_specs=[pl.BlockSpec(memory_space=pltpu.SMEM)] + [vmem] * 8,
+        in_specs=[pl.BlockSpec(memory_space=pltpu.SMEM)] + [vmem] * 10,
         out_specs=(vmem,) * 3,
         scratch_shapes=[pltpu.VMEM((24, 8, GRID), F32), pltpu.VMEM((12, 8, GRID), F32)],
-        input_output_aliases={8: 2},
+        input_output_aliases={10: 2},
         compiler_params=params,
         cost_estimate=cost(6),
         name="powers",

time: 83.9 us -> 83.5 us (level)
  starting transfers between devices: 22.4 us -> 32.4 us
  waiting for transfers between devices: 7 us -> 0.3 us
  blocking collectives: 24.1 us -> 20.1 us
    ppermute x10 -> x14, starting transfers between devices: 22.4 us -> 32.4 us  [swapped(): return lax.ppermute(value, axis, pairs)]
    ppermute x10 -> x14, waiting for transfers between devices: 7 us -> 0.3 us  [swapped(): return lax.ppermute(value, axis, pairs)]
    all_to_all x1, blocking collectives: 24.1 us -> 20.1 us  [per_device(): dots = lax.all_to_all(dots, ('gx', 'gy'), 0, 0, tiled=True)]
    pallas_call x7 -> x8, Pallas kernels: 20.4 us -> 20.7 us  [call(): pl.pallas_call(kernel, out_shape=outs, in_specs=scalars + [pl.BlockSpec(m...]
  transfers between devices with their start and end apart: 10 -> 14, of which waited for: 4 -> 2; matrix products, arithmetic and copies ran while one was open for 0% -> 0% of each run, Pallas kernels for 13% -> 23%
where the time goes in v5:
time: 83.5 us; the launch traced here: 83.2 us
  starting transfers between devices  32.4 us (39%)
  Pallas kernels  27.7 us (33%)
  blocking collectives  20.1 us (24%)
  local copies, waits for them, and re-layouts  1.65 us (2%)
  between operations  0.98 us (1%)
    ppermute x14, starting transfers between devices, swapped(): return lax.ppermute(value, axis, pairs)  32.4 us
    pallas_call x8, Pallas kernels, call(): pl.pallas_call(kernel, out_shape=outs, in_specs=scalars + [pl.BlockSpec(m...  20.7 us
    all_to_all x1, blocking collectives, per_device(): dots = lax.all_to_all(dots, ('gx', 'gy'), 0, 0, tiled=True)  20.1 us
    pallas_call x1, Pallas kernels, per_device(): pl.pallas_call(powers_kernel, out_shape=(struct(96, ROWS), struct(devices...  5.42 us
  transfers between devices with their start and end apart: 14, of which 2 were waited for; matrix products, arithmetic and copies ran while one was open for 0% of the time, Pallas kernels for 23%

profile of v5, /device:TPU:1, one launch (start us, length us, event | category | flops | bytes accessed | tf_op | source)
XLA Modules:
  0.0 83.2 jit_solution(11628327313337601619)
XLA Ops:
  0.7 0.1 add_convert_fusion.flags_ref
  0.7 0.0 copy-start.4
  0.7 1.6 %copy-done.4 = bf16[16,32,2048]{2,1,0:T(8,128)(2,1)S(1)} copy-done((bf16[16,32,2048]{2,1,0:T(8,128)(2,1)S(1)}, bf16[16,32,2048]{2,1,0:T(8,128)(2,1)}, u32[]{:S(2)}) %copy-start.4) | copy-done | bytes 2097176
  2.3 0.0 copy-start.3
  2.3 0.0 copy-start.5
  2.3 0.0 copy-start.6
  2.3 0.0 copy-start.7
  2.3 1.5 %pack.1 = (bf16[5,4,8,2048]{3,2,1,0:T(8,128)(2,1)S(1)}, bf16[5,4,8,2048]{3,2,1,0:T(8,128)(2,1)S(1)}, bf16[64,2048]{1,0:T(8,128)(2,1)S(1)}, bf16[64,2048]{1,0:T(8,128)(2,1)S(1)}) custom-call(s32[4]{0:T(128)S(1)} %add_convert_fusion.flags_ref, bf16[16,4,8,2048]{3,2,1,0:T(8,128)(2,1)S(1)} %bitcast.30), custom_call_target="tpu_custom_call" | custom-call | flops 8800000000 | tf_op jit(solution)/shard_map/pack/pallas_call | solution.py:659
  3.9 0.8 %collective-permute-start.2 = (bf16[160,2048]{1,0:T(8,128)(2,1)S(1)}, bf16[160,2048]{1,0:T(8,128)(2,1)S(1)}, u32[]{:S(2)}, u32[]{:S(2)}) collective-permute-start(bf16[160,2048]{1,0:T(8,128)(2,1)S(1)} %bitcast.35), channel_id=1, source_target_pairs={{8,16},{16,8},{24,32},{32,24},{40,48},{48,40},{56,64},{64,56},{72,... | collective-permute-start | bytes 1966088 | tf_op jit(solution)/shard_map/ppermute | solution.py:632
  4.7 5.4 %collective-permute-start.3 = (bf16[160,2048]{1,0:T(8,128)(2,1)S(1)}, bf16[160,2048]{1,0:T(8,128)(2,1)S(1)}, u32[]{:S(2)}, u32[]{:S(2)}) collective-permute-start(bf16[160,2048]{1,0:T(8,128)(2,1)S(1)} %bitcast.34), channel_id=1, source_target_pairs={{0,8},{8,0},{16,24},{24,16},{32,40},{40,32},{48,56},{56,48},{64,72... | collective-permute-start | bytes 1966088 | tf_op jit(solution)/shard_map/ppermute | solution.py:632
  10.1 4.3 %collective-permute-start = (bf16[64,2048]{1,0:T(8,128)(2,1)S(1)}, bf16[64,2048]{1,0:T(8,128)(2,1)S(1)}, u32[]{:S(2)}, u32[]{:S(2)}) collective-permute-start(bf16[64,2048]{1,0:T(8,128)(2,1)S(1)} %get-tuple-element.36), channel_id=1, source_target_pairs={{1,2},{2,1},{3,4},{4,3},{5,6},{6,5},{9,10},{10,9},{11,12},{12,11},... | collective-permute-start | bytes 786440 | tf_op jit(solution)/shard_map/ppermute | solution.py:632
  14.4 0.1 collective-permute-start.1
  14.5 0.0 slice-start
  14.5 0.0 copy-done.3
  14.5 0.0 copy-done.5
  14.5 0.0 copy-done.6
  14.6 0.0 copy-done.7
  14.6 0.0 slice-start.1
  14.6 0.0 copy-start
  14.6 4.1 %own_samples.1 = (f32[512,2048]{1,0:T(8,128)S(1)}, f32[8,128]{1,0:T(8,128)S(1)}) custom-call(bf16[512,2048]{1,0:T(8,128)(2,1)S(1)} %bitcast.29, bf16[512,2048]{1,0:T(8,128)(2,1)S(1)} %bitcast.32, bf16[512,2048]{1,0:T(8,128)(2,1)S(1)} %bitcast.31, s32[2,16,4,32]{3,2,1,0:T(4,128)S(1)} %bitcast.36), custom_call_target="tpu_custom_call" | custom-call | flops 2200000000 | tf_op jit(solution)/shard_map/own_samples/pallas_call | solution.py:607
  18.7 0.0 copy-start.1
  18.7 0.0 copy-start.2
  18.7 0.1 collective-permute-done.ya_ref
  18.8 0.0 collective-permute-done.1.yb_ref
  18.8 0.6 corners.1
  19.4 0.7 collective-permute-start.4
  20.0 2.5 %collective-permute-start.5 = (bf16[48,2048]{1,0:T(8,128)(2,1)S(1)}, bf16[48,2048]{1,0:T(8,128)(2,1)S(1)}, u32[]{:S(2)}, u32[]{:S(2)}) collective-permute-start(bf16[48,2048]{1,0:T(8,128)(2,1)S(1)} %get-tuple-element.48), channel_id=1, source_target_pairs={{0,8},{8,0},{16,24},{24,16},{32,40},{40,32},{48,56},{56,48},{64,72... | collective-permute-start | bytes 589832 | tf_op jit(solution)/shard_map/ppermute | solution.py:632
  22.5 0.0 slice-done
  22.5 0.0 slice-done.1
  22.6 0.0 copy-done
  22.6 0.0 copy-done.1
  22.6 0.0 copy-done.2
  22.6 0.0 copy-start.8
  22.6 4.6 %hessian.1 = (bf16[672,512]{1,0:T(8,128)(2,1)S(1)}, bf16[672,128]{1,0:T(8,128)(2,1)S(1)}, bf16[672,256]{1,0:T(8,128)(2,1)S(1)}, bf16[3,512,2048]{2,1,0:T(8,128)(2,1)S(1)}) custom-call(bf16[3,512,2048]{2,1,0:T(8,128)(2,1)S(1)} %bitcast.25, s32[512,2048]{1,0:T(8,128)S(1)} %bitcast.26, bf16[2048,128]{1,0:T(8,128)(2,1)S(1)} %copy-done.1, s32[8,1024]{1,0:T(8,128)S(1)} %copy-done.2), custom_call_target="tpu_custom_call" | custom-call | flops 1100000000 | tf_op jit(solution)/shard_map/hessian/pallas_call | solution.py:607
  27.2 1.1 %collective-permute-start.7 = (bf16[672,128]{1,0:T(8,128)(2,1)S(1)}, bf16[672,128]{1,0:T(8,128)(2,1)S(1)}, u32[]{:S(2)}, u32[]{:S(2)}) collective-permute-start(bf16[672,128]{1,0:T(8,128)(2,1)S(1)} %get-tuple-element.51), channel_id=1, source_target_pairs={{0,1},{1,0},{2,3},{3,2},{4,5},{5,4},{6,7},{7,6},{8,9},{9,8},{10,11... | collective-permute-start | bytes 516104 | tf_op jit(solution)/shard_map/ppermute | solution.py:632
  28.2 0.0 collective-permute-done.4.ca_ref
  28.2 3.1 %collective-permute-start.6 = (bf16[672,128]{1,0:T(8,128)(2,1)S(1)}, bf16[672,128]{1,0:T(8,128)(2,1)S(1)}, u32[]{:S(2)}, u32[]{:S(2)}) collective-permute-start(bf16[672,128]{1,0:T(8,128)(2,1)S(1)} %get-tuple-element.51), channel_id=1, source_target_pairs={{1,2},{2,1},{3,4},{4,3},{5,6},{6,5},{9,10},{10,9},{11,12},{12,11},... | collective-permute-start | bytes 516104 | tf_op jit(solution)/shard_map/ppermute | solution.py:632
  31.3 0.0 collective-permute-done.5.cb_ref
  31.4 0.0 collective-permute-done.2.xa_ref
  31.4 0.0 collective-permute-done.3.xb_ref
  31.4 0.0 copy-done.8
  31.4 6.7 %warp.1 = (f32[96,512]{1,0:T(8,128)S(1)}, bf16[192,128]{1,0:T(8,128)(2,1)S(1)}) custom-call(s32[4]{0:T(128)S(1)} %add_convert_fusion.flags_ref, f32[512,2048]{1,0:T(8,128)S(1)} %get-tuple-element.43.t_ref, bf16[512,2048]{1,0:T(8,128)(2,1)S(1)} %bitcast.33, bf16[3,512,2048]{2,1,0:T(8,128)(2,1)S(1)} %get-tuple-element.44.mg_ref, ...), custom_call_target="tpu_custom_call" | custom-call | flops 6600000000 | tf_op jit(solution)/shard_map/warp/pallas_call | solution.py:607
  38.1 0.1 collective-permute-start.9
  38.1 3.4 %collective-permute-start.8 = (bf16[192,128]{1,0:T(8,128)(2,1)S(1)}, bf16[192,128]{1,0:T(8,128)(2,1)S(1)}, u32[]{:S(2)}, u32[]{:S(2)}) collective-permute-start(bf16[192,128]{1,0:T(8,128)(2,1)S(1)} %get-tuple-element.53), channel_id=1, source_target_pairs={{1,2},{2,1},{3,4},{4,3},{5,6},{6,5},{9,10},{10,9},{11,12},{12,11},... | collective-permute-start | bytes 147464 | tf_op jit(solution)/shard_map/ppermute | solution.py:632
  41.6 0.0 collective-permute-done.7.yb_ref
  41.6 0.0 collective-permute-done.6.ya_ref
  41.6 0.8 %hessian_edges.1 = (bf16[672,128]{1,0:T(8,128)(2,1)S(1)}, bf16[672,128]{1,0:T(8,128)(2,1)S(1)}, bf16[672,128]{1,0:T(8,128)(2,1)S(1)}) custom-call(s32[4]{0:T(128)S(1)} %add_convert_fusion.flags_ref, bf16[672,256]{1,0:T(8,128)(2,1)S(1)} %get-tuple-element.50.cx_ref, bf16[672,128]{1,0:T(8,128)(2,1)S(1)} %collective-permute-done.6.ya_ref, ...), custom_call_target="tpu_custom_call" | custom-call | flops 1100000000 | tf_op jit(solution)/shard_map/hessian_edges/pallas_call | solution.py:607
  42.4 0.7 collective-permute-start.10
  43.1 4.8 %collective-permute-start.11 = (bf16[672,128]{1,0:T(8,128)(2,1)S(1)}, bf16[672,128]{1,0:T(8,128)(2,1)S(1)}, u32[]{:S(2)}, u32[]{:S(2)}) collective-permute-start(bf16[672,128]{1,0:T(8,128)(2,1)S(1)} %get-tuple-element.57), channel_id=1, source_target_pairs={{0,8},{8,0},{16,24},{24,16},{32,40},{40,32},{48,56},{56,48},{64,72... | collective-permute-start | bytes 516104 | tf_op jit(solution)/shard_map/ppermute | solution.py:632
  47.9 0.0 collective-permute-done.9.yb_ref
  47.9 0.0 collective-permute-done.8.ya_ref
  47.9 0.9 %load_edges.1 = (bf16[192,128]{1,0:T(8,128)(2,1)S(1)}, bf16[384,128]{1,0:T(8,128)(2,1)S(1)}, bf16[384,128]{1,0:T(8,128)(2,1)S(1)}) custom-call(s32[4]{0:T(128)S(1)} %add_convert_fusion.flags_ref, f32[96,512]{1,0:T(8,128)S(1)} %get-tuple-element.49.l_ref, bf16[192,128]{1,0:T(8,128)(2,1)S(1)} %collective-permute-done.8.ya_ref, ...), custom_call_target="tpu_custom_call" | custom-call | flops 1100000000 | tf_op jit(solution)/shard_map/load_edges/pallas_call | solution.py:607
  48.8 0.7 collective-permute-start.12
  49.5 4.8 %collective-permute-start.13 = (bf16[384,128]{1,0:T(8,128)(2,1)S(1)}, bf16[384,128]{1,0:T(8,128)(2,1)S(1)}, u32[]{:S(2)}, u32[]{:S(2)}) collective-permute-start(bf16[384,128]{1,0:T(8,128)(2,1)S(1)} %get-tuple-element.59), channel_id=1, source_target_pairs={{0,8},{8,0},{16,24},{24,16},{32,40},{40,32},{48,56},{56,48},{64,72... | collective-permute-start | bytes 294920 | tf_op jit(solution)/shard_map/ppermute | solution.py:632
  54.3 1.8 %grid.1 = (f32[8,672,128]{2,1,0:T(8,128)S(1)}, f32[96,1024]{1,0:T(8,128)S(1)}, bf16[128,384]{1,0:T(8,128)(2,1)S(1)}, bf16[384,1024]{1,0:T(8,128)(2,1)S(1)}, bf16[1024,512]{1,0:T(8,128)(2,1)S(1)}) custom-call(bf16[672,512]{1,0:T(8,128)(2,1)S(1)} %get-tuple-element.42.own_ref, f32[96,512]{1,0:T(8,128)S(1)} %get-tuple-element.49.l_ref, ...), custom_call_target="tpu_custom_call" | custom-call | flops 3300000000 | tf_op jit(solution)/shard_map/grid/pallas_call | solution.py:607
  56.0 0.0 collective-permute-done.10.ha_ref
  56.1 0.0 collective-permute-done.11.hb_ref
  56.1 0.0 collective-permute-done.12.la_ref
  56.1 0.2 collective-permute-done.13.lb_ref
  56.3 5.4 %powers.1 = (f32[96,512]{1,0:T(8,128)S(1)}, f32[128,128]{1,0:T(8,128)S(1)}, f32[8,672,128]{2,1,0:T(8,128)S(1)}) custom-call(s32[4]{0:T(128)S(1)} %add_convert_fusion.flags_ref, f32[96,1024]{1,0:T(8,128)S(1)} %get-tuple-element.55.lown_ref, bf16[672,128]{1,0:T(8,128)(2,1)S(1)} %collective-permute-done.10.ha_ref, ...), custom_call_target="tpu_custom_call", output_to_operand_aliasing={{2}: (10, {})} | custom-call | flops 6600000000 | tf_op jit(solution)/shard_map/powers/pallas_call | solution.py:725
  61.7 20.1 %all_to_all.11 = f32[128,1,128]{2,1,0:T(1,128)S(1)} all-to-all(f32[128,1,128]{2,1,0:T(1,128)S(1)} %bitcast.27), channel_id=1, replica_groups=mesh['gx'=16,'gy'=8] {'gx','gy'}, dimensions={0} | all-to-all | bytes 131072 | tf_op jit(solution)/shard_map/all_to_all | solution.py:739
  81.8 1.4 %combine.1 = (f32[240,32]{1,0:T(8,128)}, f32[240,32]{1,0:T(8,128)}) custom-call(f32[96,512]{1,0:T(8,128)S(1)} %get-tuple-element.64.v_ref, f32[128,128]{1,0:T(8,128)S(1)} %bitcast.28), custom_call_target="tpu_custom_call" | custom-call | flops 3300000000 | tf_op jit(solution)/shard_map/combine/pallas_call | solution.py:607
  (1 shorter events, 0.0 us)
Async XLA Ops:
  0.7 1.6 %copy-start.4 = (bf16[16,32,2048]{2,1,0:T(8,128)(2,1)S(1)}, bf16[16,32,2048]{2,1,0:T(8,128)(2,1)}, u32[]{:S(2)}) copy-start(bf16[16,32,2048]{2,1,0:T(8,128)(2,1)} %param.12) | copy-start | bytes 6291460
  2.3 12.2 %copy-start.3 = (bf16[16,32,2048]{2,1,0:T(8,128)(2,1)S(1)}, bf16[16,32,2048]{2,1,0:T(8,128)(2,1)}, u32[]{:S(2)}) copy-start(bf16[16,32,2048]{2,1,0:T(8,128)(2,1)} %param.10) | copy-start | bytes 6291460
  2.3 12.2 %copy-start.5 = (bf16[16,32,2048]{2,1,0:T(8,128)(2,1)S(1)}, bf16[16,32,2048]{2,1,0:T(8,128)(2,1)}, u32[]{:S(2)}) copy-start(bf16[16,32,2048]{2,1,0:T(8,128)(2,1)} %param.12) | copy-start | bytes 6291460
  2.3 12.2 %copy-start.6 = (bf16[16,32,2048]{2,1,0:T(8,128)(2,1)S(1)}, bf16[16,32,2048]{2,1,0:T(8,128)(2,1)}, u32[]{:S(2)}) copy-start(bf16[16,32,2048]{2,1,0:T(8,128)(2,1)} %param.13) | copy-start | bytes 6291460
  2.3 12.2 %copy-start.7 = (s32[2,16,32,4]{2,3,1,0:T(4,128)S(1)}, s32[2,16,32,4]{2,3,1,0:T(4,128)}, u32[]{:S(2)}) copy-start(s32[2,16,32,4]{2,3,1,0:T(4,128)} %param.15) | copy-start | bytes 49156
  3.9 27.5 %collective-permute-start.2 = (bf16[160,2048]{1,0:T(8,128)(2,1)S(1)}, bf16[160,2048]{1,0:T(8,128)(2,1)S(1)}, u32[]{:S(2)}, u32[]{:S(2)}) collective-permute-start(bf16[160,2048]{1,0:T(8,128)(2,1)S(1)} %bitcast.35), channel_id=1, source_target_pairs={{8,16},{16,8},{24,32},{32,24},{40,48},{48,40},{56,64},{64,56},{72,... | collective-permute-start | bytes 1966088 | tf_op jit(solution)/shard_map/ppermute | solution.py:632
  4.7 26.7 %collective-permute-start.3 = (bf16[160,2048]{1,0:T(8,128)(2,1)S(1)}, bf16[160,2048]{1,0:T(8,128)(2,1)S(1)}, u32[]{:S(2)}, u32[]{:S(2)}) collective-permute-start(bf16[160,2048]{1,0:T(8,128)(2,1)S(1)} %bitcast.34), channel_id=1, source_target_pairs={{0,8},{8,0},{16,24},{24,16},{32,40},{40,32},{48,56},{56,48},{64,72... | collective-permute-start | bytes 1966088 | tf_op jit(solution)/shard_map/ppermute | solution.py:632
  10.1 8.7 %collective-permute-start = (bf16[64,2048]{1,0:T(8,128)(2,1)S(1)}, bf16[64,2048]{1,0:T(8,128)(2,1)S(1)}, u32[]{:S(2)}, u32[]{:S(2)}) collective-permute-start(bf16[64,2048]{1,0:T(8,128)(2,1)S(1)} %get-tuple-element.36), channel_id=1, source_target_pairs={{1,2},{2,1},{3,4},{4,3},{5,6},{6,5},{9,10},{10,9},{11,12},{12,11},... | collective-permute-start | bytes 786440 | tf_op jit(solution)/shard_map/ppermute | solution.py:632
  14.4 4.3 %collective-permute-start.1 = (bf16[64,2048]{1,0:T(8,128)(2,1)S(1)}, bf16[64,2048]{1,0:T(8,128)(2,1)S(1)}, u32[]{:S(2)}, u32[]{:S(2)}) collective-permute-start(bf16[64,2048]{1,0:T(8,128)(2,1)S(1)} %get-tuple-element.37), channel_id=1, source_target_pairs={{0,1},{1,0},{2,3},{3,2},{4,5},{5,4},{6,7},{7,6},{8,9},{9,8},{10,11... | collective-permute-start | bytes 786440 | tf_op jit(solution)/shard_map/ppermute | solution.py:632
  14.5 8.0 %slice-start = ((s8[6291456]{0:T(1024)(128)(4,1)}), s8[4194304]{0:T(1024)(128)(4,1)S(1)}, s32[]{:S(2)}) async-start(s8[6291456]{0:T(1024)(128)(4,1)} %bitcast.23), calls=%async_computation.1 | async-start | bytes 8388608
  14.6 8.0 %slice-start.1 = ((s8[6291456]{0:T(1024)(128)(4,1)}), s8[2097152]{0:T(1024)(128)(4,1)S(1)}, s32[]{:S(2)}) async-start(s8[6291456]{0:T(1024)(128)(4,1)} %bitcast.23), calls=%async_computation.2 | async-start | bytes 4194304
  14.6 8.0 %copy-start = (s32[16,32,2048]{2,1,0:T(8,128)S(1)}, s32[16,32,2048]{2,1,0:T(8,128)}, u32[]{:S(2)}) copy-start(s32[16,32,2048]{2,1,0:T(8,128)} %param.14) | copy-start | bytes 12582916
  18.7 3.9 %copy-start.1 = (bf16[2048,128]{1,0:T(8,128)(2,1)S(1)}, bf16[2048,128]{1,0:T(8,128)(2,1)}, u32[]{:S(2)}) copy-start(bf16[2048,128]{1,0:T(8,128)(2,1)} %constant.38.clone.table_ref) | copy-start | bytes 1572868
  18.7 3.9 %copy-start.2 = (s32[8,1024]{1,0:T(8,128)S(1)}, s32[8,1024]{1,0:T(8,128)}, u32[]{:S(2)}) copy-start(s32[8,1024]{1,0:T(8,128)} %constant.37.clone.maps_ref) | copy-start | bytes 98308
  19.4 8.9 %collective-permute-start.4 = (bf16[48,2048]{1,0:T(8,128)(2,1)S(1)}, bf16[48,2048]{1,0:T(8,128)(2,1)S(1)}, u32[]{:S(2)}, u32[]{:S(2)}) collective-permute-start(bf16[48,2048]{1,0:T(8,128)(2,1)S(1)} %get-tuple-element.47), channel_id=1, source_target_pairs={{8,16},{16,8},{24,32},{32,24},{40,48},{48,40},{56,64},{64,56},{72,... | collective-permute-start | bytes 589832 | tf_op jit(solution)/shard_map/ppermute | solution.py:632
  20.0 11.3 %collective-permute-start.5 = (bf16[48,2048]{1,0:T(8,128)(2,1)S(1)}, bf16[48,2048]{1,0:T(8,128)(2,1)S(1)}, u32[]{:S(2)}, u32[]{:S(2)}) collective-permute-start(bf16[48,2048]{1,0:T(8,128)(2,1)S(1)} %get-tuple-element.48), channel_id=1, source_target_pairs={{0,8},{8,0},{16,24},{24,16},{32,40},{40,32},{48,56},{56,48},{64,72... | collective-permute-start | bytes 589832 | tf_op jit(solution)/shard_map/ppermute | solution.py:632
  22.6 8.8 %copy-start.8 = (bf16[2048,128]{1,0:T(8,128)(2,1)S(1)}, bf16[2048,128]{1,0:T(8,128)(2,1)}, u32[]{:S(2)}) copy-start(bf16[2048,128]{1,0:T(8,128)(2,1)} %constant.39.clone.table_ref) | copy-start | bytes 1572868
  27.2 14.4 %collective-permute-start.7 = (bf16[672,128]{1,0:T(8,128)(2,1)S(1)}, bf16[672,128]{1,0:T(8,128)(2,1)S(1)}, u32[]{:S(2)}, u32[]{:S(2)}) collective-permute-start(bf16[672,128]{1,0:T(8,128)(2,1)S(1)} %get-tuple-element.51), channel_id=1, source_target_pairs={{0,1},{1,0},{2,3},{3,2},{4,5},{5,4},{6,7},{7,6},{8,9},{9,8},{10,11... | collective-permute-start | bytes 516104 | tf_op jit(solution)/shard_map/ppermute | solution.py:632
  28.2 13.3 %collective-permute-start.6 = (bf16[672,128]{1,0:T(8,128)(2,1)S(1)}, bf16[672,128]{1,0:T(8,128)(2,1)S(1)}, u32[]{:S(2)}, u32[]{:S(2)}) collective-permute-start(bf16[672,128]{1,0:T(8,128)(2,1)S(1)} %get-tuple-element.51), channel_id=1, source_target_pairs={{1,2},{2,1},{3,4},{4,3},{5,6},{6,5},{9,10},{10,9},{11,12},{12,11},... | collective-permute-start | bytes 516104 | tf_op jit(solution)/shard_map/ppermute | solution.py:632
  38.1 9.9 %collective-permute-start.9 = (bf16[192,128]{1,0:T(8,128)(2,1)S(1)}, bf16[192,128]{1,0:T(8,128)(2,1)S(1)}, u32[]{:S(2)}, u32[]{:S(2)}) collective-permute-start(bf16[192,128]{1,0:T(8,128)(2,1)S(1)} %get-tuple-element.53), channel_id=1, source_target_pairs={{0,1},{1,0},{2,3},{3,2},{4,5},{5,4},{6,7},{7,6},{8,9},{9,8},{10,11... | collective-permute-start | bytes 147464 | tf_op jit(solution)/shard_map/ppermute | solution.py:632
  38.1 9.8 %collective-permute-start.8 = (bf16[192,128]{1,0:T(8,128)(2,1)S(1)}, bf16[192,128]{1,0:T(8,128)(2,1)S(1)}, u32[]{:S(2)}, u32[]{:S(2)}) collective-permute-start(bf16[192,128]{1,0:T(8,128)(2,1)S(1)} %get-tuple-element.53), channel_id=1, source_target_pairs={{1,2},{2,1},{3,4},{4,3},{5,6},{6,5},{9,10},{10,9},{11,12},{12,11},... | collective-permute-start | bytes 147464 | tf_op jit(solution)/shard_map/ppermute | solution.py:632
  42.4 13.6 %collective-permute-start.10 = (bf16[672,128]{1,0:T(8,128)(2,1)S(1)}, bf16[672,128]{1,0:T(8,128)(2,1)S(1)}, u32[]{:S(2)}, u32[]{:S(2)}) collective-permute-start(bf16[672,128]{1,0:T(8,128)(2,1)S(1)} %get-tuple-element.56), channel_id=1, source_target_pairs={{8,16},{16,8},{24,32},{32,24},{40,48},{48,40},{56,64},{64,56},{72,... | collective-permute-start | bytes 516104 | tf_op jit(solution)/shard_map/ppermute | solution.py:632
  43.1 12.9 %collective-permute-start.11 = (bf16[672,128]{1,0:T(8,128)(2,1)S(1)}, bf16[672,128]{1,0:T(8,128)(2,1)S(1)}, u32[]{:S(2)}, u32[]{:S(2)}) collective-permute-start(bf16[672,128]{1,0:T(8,128)(2,1)S(1)} %get-tuple-element.57), channel_id=1, source_target_pairs={{0,8},{8,0},{16,24},{24,16},{32,40},{40,32},{48,56},{56,48},{64,72... | collective-permute-start | bytes 516104 | tf_op jit(solution)/shard_map/ppermute | solution.py:632
  48.8 7.3 %collective-permute-start.12 = (bf16[384,128]{1,0:T(8,128)(2,1)S(1)}, bf16[384,128]{1,0:T(8,128)(2,1)S(1)}, u32[]{:S(2)}, u32[]{:S(2)}) collective-permute-start(bf16[384,128]{1,0:T(8,128)(2,1)S(1)} %get-tuple-element.58), channel_id=1, source_target_pairs={{8,16},{16,8},{24,32},{32,24},{40,48},{48,40},{56,64},{64,56},{72,... | collective-permute-start | bytes 294920 | tf_op jit(solution)/shard_map/ppermute | solution.py:632
  49.5 6.8 %collective-permute-start.13 = (bf16[384,128]{1,0:T(8,128)(2,1)S(1)}, bf16[384,128]{1,0:T(8,128)(2,1)S(1)}, u32[]{:S(2)}, u32[]{:S(2)}) collective-permute-start(bf16[384,128]{1,0:T(8,128)(2,1)S(1)} %get-tuple-element.59), channel_id=1, source_target_pairs={{0,8},{8,0},{16,24},{24,16},{32,40},{40,32},{48,56},{56,48},{64,72... | collective-permute-start | bytes 294920 | tf_op jit(solution)/shard_map/ppermute | solution.py:632

commit v6 on v5

--- a/solution.py
+++ b/solution.py
@@ -286,24 +286,28 @@
     store_pair(flags_ref, up, down, a_ref, b_ref)
 
 
-def grid_kernel(
-    own_ref, l_ref, yh_ref, yl_ref, maps_ref,
-    out_ref, lout_ref, hchoice_ref, lchoice_ref, ochoice_ref,
-):
+def own_grid_kernel(own_ref, maps_ref, out_ref, hchoice_ref, lchoice_ref, ochoice_ref):
     h_map, l_map = lane_map(maps_ref, "h_grid"), lane_map(maps_ref, "l_grid")
-    source = jnp.concatenate([own_ref[...], yh_ref[...]], axis=1)
-    placed = jnp.dot(source, onehot(h_map, ROWS + 128), preferred_element_type=F32)
+    placed = jnp.dot(own_ref[...], onehot(h_map, ROWS), preferred_element_type=F32)
     for tile in range(GRID // 128):
         out_ref[tile] = placed[:, tile * 128 : (tile + 1) * 128]
-    top = l_ref[...].astype(BF16)
-    rest = (l_ref[...] - top.astype(F32)).astype(BF16)
-    source = jnp.concatenate([jnp.concatenate([top, rest], axis=0), yl_ref[...]], axis=1)
-    placed = jnp.dot(source, onehot(l_map, ROWS + 128), preferred_element_type=F32)
-    lout_ref[...] = placed[:96] + placed[96:]
     hchoice_ref[:, :256] = onehot(h_map[:, :256] - (ROWS + 128), 128)
     hchoice_ref[:, 256:] = onehot(h_map[:, 768:896] - (ROWS + 256), 128)
     lchoice_ref[...] = onehot(l_map - (ROWS + 128), 384)
     ochoice_ref[...] = onehot(lane_map(maps_ref, "own"), GRID)
+
+
+def grid_kernel(h_ref, l_ref, yh_ref, yl_ref, maps_ref, out_ref, lout_ref):
+    choice = onehot(lane_map(maps_ref, "h_grid") - ROWS, 128)
+    placed = jnp.dot(yh_ref[...], choice, preferred_element_type=F32)
+    for tile in range(GRID // 128):
+        out_ref[tile] = h_ref[tile] + placed[:, tile * 128 : (tile + 1) * 128]
+    top = l_ref[...].astype(BF16)
+    rest = (l_ref[...] - top.astype(F32)).astype(BF16)
+    source = jnp.concatenate([jnp.concatenate([top, rest], axis=0), yl_ref[...]], axis=1)
+    choice = onehot(lane_map(maps_ref, "l_grid"), ROWS + 128)
+    placed = jnp.dot(source, choice, preferred_element_type=F32)
+    lout_ref[...] = placed[:96] + placed[96:]
 
 
 def sample_slot(x, y):
@@ -690,6 +694,12 @@
         grad, mask, jnp.asarray(hessian_table()), maps_late,
         name="hessian", us=1,
     )
+    stiffness, *choices = call(
+        own_grid_kernel,
+        (struct(GRID // 128, CROWS, 128), bf(128, 384), bf(384, GRID), bf(GRID, ROWS)),
+        coefs, maps, name="own_grid", us=1,
+    )
+    moves, stiffness = lax.optimization_barrier((moves, stiffness))
     ya_h, yb_h = swapped(coefs_y, "gy", True), swapped(coefs_y, "gy", False)
     loads, message = call(
         warp_kernel,
@@ -711,14 +721,10 @@
         swapped(ha, "gx", True), swapped(hb, "gx", False),
         swapped(la, "gx", True), swapped(lb, "gx", False),
     )
-    stiffness, loads_grid, *choices = call(
-        grid_kernel,
-        (
-            struct(GRID // 128, CROWS, 128), struct(96, GRID),
-            bf(128, 384), bf(384, GRID), bf(GRID, ROWS),
-        ),
-        coefs, loads, ytile_h, ytile_l, maps,
-        name="grid", us=3,
+    stiffness, loads_grid = call(
+        grid_kernel, (struct(GRID // 128, CROWS, 128), struct(96, GRID)),
+        stiffness, loads, ytile_h, ytile_l, maps,
+        name="grid", us=1,
     )
 
     devices = lax.axis_size("gx") * lax.axis_size("gy")

time: 83.5 us -> 83.4 us (level)
  starting transfers between devices: 32.4 us -> 31.2 us
  waiting for transfers between devices: 0.3 us -> 1.2 us
    ppermute x14, starting transfers between devices: 32.4 us -> 31.2 us  [swapped(): return lax.ppermute(value, axis, pairs)]
    ppermute x14, waiting for transfers between devices: 0.3 us -> 1.2 us  [swapped(): return lax.ppermute(value, axis, pairs)]
    pallas_call x8 -> x9, Pallas kernels: 20.7 us -> 21.1 us  [call(): pl.pallas_call(kernel, out_shape=outs, in_specs=scalars + [pl.BlockSpec(m...]
  transfers between devices with their start and end apart: 14 -> 14, of which waited for: 2 -> 2; matrix products, arithmetic and copies ran while one was open for 0% -> 0% of each run, Pallas kernels for 23% -> 24%
where the time goes in v6:
time: 83.4 us; the launch traced here: 83.1 us
  starting transfers between devices  31.2 us (37%)
  Pallas kernels  27.9 us (33%)
  blocking collectives  20.1 us (24%)
  local copies, waits for them, and re-layouts  1.65 us (2%)
  waiting for transfers between devices  1.2 us (1%)
  between operations  0.99 us (1%)
    ppermute x14, starting transfers between devices, swapped(): return lax.ppermute(value, axis, pairs)  31.2 us
    pallas_call x9, Pallas kernels, call(): pl.pallas_call(kernel, out_shape=outs, in_specs=scalars + [pl.BlockSpec(m...  21.1 us
    all_to_all x1, blocking collectives, per_device(): dots = lax.all_to_all(dots, ('gx', 'gy'), 0, 0, tiled=True)  20.1 us
    pallas_call x1, Pallas kernels, per_device(): pl.pallas_call(powers_kernel, out_shape=(struct(96, ROWS), struct(devices...  5.34 us
  transfers between devices with their start and end apart: 14, of which 2 were waited for; matrix products, arithmetic and copies ran while one was open for 0% of the time, Pallas kernels for 24%

profile of v6, /device:TPU:1, one launch (start us, length us, event | category | flops | bytes accessed | tf_op | source)
XLA Modules:
  0.0 83.1 jit_solution(13240787341339423349)
XLA Ops:
  0.7 0.1 add_convert_fusion.flags_ref
  0.7 0.0 copy-start.4
  0.7 1.6 %copy-done.4 = bf16[16,32,2048]{2,1,0:T(8,128)(2,1)S(1)} copy-done((bf16[16,32,2048]{2,1,0:T(8,128)(2,1)S(1)}, bf16[16,32,2048]{2,1,0:T(8,128)(2,1)}, u32[]{:S(2)}) %copy-start.4) | copy-done | bytes 2097176
  2.3 0.0 copy-start.3
  2.3 0.0 copy-start.5
  2.3 0.0 copy-start.6
  2.3 0.0 copy-start.7
  2.3 1.5 %pack.1 = (bf16[5,4,8,2048]{3,2,1,0:T(8,128)(2,1)S(1)}, bf16[5,4,8,2048]{3,2,1,0:T(8,128)(2,1)S(1)}, bf16[64,2048]{1,0:T(8,128)(2,1)S(1)}, bf16[64,2048]{1,0:T(8,128)(2,1)S(1)}) custom-call(s32[4]{0:T(128)S(1)} %add_convert_fusion.flags_ref, bf16[16,4,8,2048]{3,2,1,0:T(8,128)(2,1)S(1)} %bitcast.30), custom_call_target="tpu_custom_call" | custom-call | flops 8800000000 | tf_op jit(solution)/shard_map/pack/pallas_call | solution.py:663
  3.9 0.8 %collective-permute-start.2 = (bf16[160,2048]{1,0:T(8,128)(2,1)S(1)}, bf16[160,2048]{1,0:T(8,128)(2,1)S(1)}, u32[]{:S(2)}, u32[]{:S(2)}) collective-permute-start(bf16[160,2048]{1,0:T(8,128)(2,1)S(1)} %bitcast.35), channel_id=1, source_target_pairs={{8,16},{16,8},{24,32},{32,24},{40,48},{48,40},{56,64},{64,56},{72,... | collective-permute-start | bytes 1966088 | tf_op jit(solution)/shard_map/ppermute | solution.py:636
  4.7 5.4 %collective-permute-start.3 = (bf16[160,2048]{1,0:T(8,128)(2,1)S(1)}, bf16[160,2048]{1,0:T(8,128)(2,1)S(1)}, u32[]{:S(2)}, u32[]{:S(2)}) collective-permute-start(bf16[160,2048]{1,0:T(8,128)(2,1)S(1)} %bitcast.34), channel_id=1, source_target_pairs={{0,8},{8,0},{16,24},{24,16},{32,40},{40,32},{48,56},{56,48},{64,72... | collective-permute-start | bytes 1966088 | tf_op jit(solution)/shard_map/ppermute | solution.py:636
  10.1 4.3 %collective-permute-start = (bf16[64,2048]{1,0:T(8,128)(2,1)S(1)}, bf16[64,2048]{1,0:T(8,128)(2,1)S(1)}, u32[]{:S(2)}, u32[]{:S(2)}) collective-permute-start(bf16[64,2048]{1,0:T(8,128)(2,1)S(1)} %get-tuple-element.40), channel_id=1, source_target_pairs={{1,2},{2,1},{3,4},{4,3},{5,6},{6,5},{9,10},{10,9},{11,12},{12,11},... | collective-permute-start | bytes 786440 | tf_op jit(solution)/shard_map/ppermute | solution.py:636
  14.4 0.1 collective-permute-start.1
  14.5 0.0 slice-start
  14.5 0.0 copy-done.3
  14.5 0.0 copy-done.5
  14.5 0.0 copy-done.6
  14.6 0.0 copy-done.7
  14.6 0.0 slice-start.1
  14.6 0.0 copy-start
  14.6 4.1 %own_samples.1 = (f32[512,2048]{1,0:T(8,128)S(1)}, f32[8,128]{1,0:T(8,128)S(1)}) custom-call(bf16[512,2048]{1,0:T(8,128)(2,1)S(1)} %bitcast.29, bf16[512,2048]{1,0:T(8,128)(2,1)S(1)} %bitcast.32, bf16[512,2048]{1,0:T(8,128)(2,1)S(1)} %bitcast.31, s32[2,16,4,32]{3,2,1,0:T(4,128)S(1)} %bitcast.36), custom_call_target="tpu_custom_call" | custom-call | flops 2200000000 | tf_op jit(solution)/shard_map/own_samples/pallas_call | solution.py:611
  18.7 0.0 copy-start.1
  18.7 0.0 copy-start.2
  18.7 0.1 collective-permute-done.ya_ref
  18.8 0.0 collective-permute-done.1.yb_ref
  18.8 0.6 corners.1
  19.4 0.7 collective-permute-start.4
  20.0 2.5 %collective-permute-start.5 = (bf16[48,2048]{1,0:T(8,128)(2,1)S(1)}, bf16[48,2048]{1,0:T(8,128)(2,1)S(1)}, u32[]{:S(2)}, u32[]{:S(2)}) collective-permute-start(bf16[48,2048]{1,0:T(8,128)(2,1)S(1)} %get-tuple-element.53), channel_id=1, source_target_pairs={{0,8},{8,0},{16,24},{24,16},{32,40},{40,32},{48,56},{56,48},{64,72... | collective-permute-start | bytes 589832 | tf_op jit(solution)/shard_map/ppermute | solution.py:636
  22.5 0.0 slice-done
  22.5 0.0 slice-done.1
  22.6 0.0 copy-done
  22.6 0.0 copy-done.1
  22.6 0.0 copy-done.2
  22.6 4.6 %hessian.1 = (bf16[672,512]{1,0:T(8,128)(2,1)S(1)}, bf16[672,128]{1,0:T(8,128)(2,1)S(1)}, bf16[672,256]{1,0:T(8,128)(2,1)S(1)}, bf16[3,512,2048]{2,1,0:T(8,128)(2,1)S(1)}) custom-call(bf16[3,512,2048]{2,1,0:T(8,128)(2,1)S(1)} %bitcast.25, s32[512,2048]{1,0:T(8,128)S(1)} %bitcast.26, bf16[2048,128]{1,0:T(8,128)(2,1)S(1)} %copy-done.1, s32[8,1024]{1,0:T(8,128)S(1)} %copy-done.2), custom_call_target="tpu_custom_call" | custom-call | flops 1100000000 | tf_op jit(solution)/shard_map/hessian/pallas_call | solution.py:611
  27.2 0.0 copy-start.8
  27.2 1.1 %collective-permute-start.7 = (bf16[672,128]{1,0:T(8,128)(2,1)S(1)}, bf16[672,128]{1,0:T(8,128)(2,1)S(1)}, u32[]{:S(2)}, u32[]{:S(2)}) collective-permute-start(bf16[672,128]{1,0:T(8,128)(2,1)S(1)} %get-tuple-element.57), channel_id=1, source_target_pairs={{0,1},{1,0},{2,3},{3,2},{4,5},{5,4},{6,7},{7,6},{8,9},{9,8},{10,11... | collective-permute-start | bytes 516104 | tf_op jit(solution)/shard_map/ppermute | solution.py:636
  28.2 1.2 %own_grid.1 = (f32[8,672,128]{2,1,0:T(8,128)S(1)}, bf16[128,384]{1,0:T(8,128)(2,1)S(1)}, bf16[384,1024]{1,0:T(8,128)(2,1)S(1)}, bf16[1024,512]{1,0:T(8,128)(2,1)S(1)}) custom-call(bf16[672,512]{1,0:T(8,128)(2,1)S(1)} %get-tuple-element.45.own_ref, s32[8,1024]{1,0:T(8,128)S(1)} %copy-done.2), custom_call_target="tpu_custom_call" | custom-call | flops 1100000000 | tf_op jit(solution)/shard_map/own_grid/pallas_call | solution.py:611
  29.4 0.0 collective-permute-done.4.ca_ref
  29.5 3.1 %collective-permute-start.6 = (bf16[672,128]{1,0:T(8,128)(2,1)S(1)}, bf16[672,128]{1,0:T(8,128)(2,1)S(1)}, u32[]{:S(2)}, u32[]{:S(2)}) collective-permute-start(bf16[672,128]{1,0:T(8,128)(2,1)S(1)} %get-tuple-element.57), channel_id=1, source_target_pairs={{1,2},{2,1},{3,4},{4,3},{5,6},{6,5},{9,10},{10,9},{11,12},{12,11},... | collective-permute-start | bytes 516104 | tf_op jit(solution)/shard_map/ppermute | solution.py:636
  32.6 0.0 collective-permute-done.5.cb_ref
  32.6 0.0 collective-permute-done.2.xa_ref
  32.6 0.0 collective-permute-done.3.xb_ref
  32.6 0.0 copy-done.8
  32.6 6.7 %warp.1 = (f32[96,512]{1,0:T(8,128)S(1)}, bf16[192,128]{1,0:T(8,128)(2,1)S(1)}) custom-call(s32[4]{0:T(128)S(1)} %add_convert_fusion.flags_ref, f32[512,2048]{1,0:T(8,128)S(1)} %get-tuple-element.48.t_ref, bf16[512,2048]{1,0:T(8,128)(2,1)S(1)} %bitcast.33, bf16[3,512,2048]{2,1,0:T(8,128)(2,1)S(1)} %get-tuple-element.49.mg_ref, ...), custom_call_target="tpu_custom_call" | custom-call | flops 6600000000 | tf_op jit(solution)/shard_map/warp/pallas_call | solution.py:611
  39.3 0.1 collective-permute-start.9
  39.4 3.4 %collective-permute-start.8 = (bf16[192,128]{1,0:T(8,128)(2,1)S(1)}, bf16[192,128]{1,0:T(8,128)(2,1)S(1)}, u32[]{:S(2)}, u32[]{:S(2)}) collective-permute-start(bf16[192,128]{1,0:T(8,128)(2,1)S(1)} %get-tuple-element.59), channel_id=1, source_target_pairs={{1,2},{2,1},{3,4},{4,3},{5,6},{6,5},{9,10},{10,9},{11,12},{12,11},... | collective-permute-start | bytes 147464 | tf_op jit(solution)/shard_map/ppermute | solution.py:636
  42.8 0.0 collective-permute-done.7.yb_ref
  42.8 0.0 collective-permute-done.6.ya_ref
  42.8 0.8 %hessian_edges.1 = (bf16[672,128]{1,0:T(8,128)(2,1)S(1)}, bf16[672,128]{1,0:T(8,128)(2,1)S(1)}, bf16[672,128]{1,0:T(8,128)(2,1)S(1)}) custom-call(s32[4]{0:T(128)S(1)} %add_convert_fusion.flags_ref, bf16[672,256]{1,0:T(8,128)(2,1)S(1)} %get-tuple-element.56.cx_ref, bf16[672,128]{1,0:T(8,128)(2,1)S(1)} %collective-permute-done.6.ya_ref, ...), custom_call_target="tpu_custom_call" | custom-call | flops 1100000000 | tf_op jit(solution)/shard_map/hessian_edges/pallas_call | solution.py:611
  43.7 0.7 collective-permute-start.10
  44.4 4.8 %collective-permute-start.11 = (bf16[672,128]{1,0:T(8,128)(2,1)S(1)}, bf16[672,128]{1,0:T(8,128)(2,1)S(1)}, u32[]{:S(2)}, u32[]{:S(2)}) collective-permute-start(bf16[672,128]{1,0:T(8,128)(2,1)S(1)} %get-tuple-element.63), channel_id=1, source_target_pairs={{0,8},{8,0},{16,24},{24,16},{32,40},{40,32},{48,56},{56,48},{64,72... | collective-permute-start | bytes 516104 | tf_op jit(solution)/shard_map/ppermute | solution.py:636
  49.1 0.0 collective-permute-done.9.yb_ref
  49.2 0.0 collective-permute-done.8.ya_ref
  49.2 0.9 %load_edges.1 = (bf16[192,128]{1,0:T(8,128)(2,1)S(1)}, bf16[384,128]{1,0:T(8,128)(2,1)S(1)}, bf16[384,128]{1,0:T(8,128)(2,1)S(1)}) custom-call(s32[4]{0:T(128)S(1)} %add_convert_fusion.flags_ref, f32[96,512]{1,0:T(8,128)S(1)} %get-tuple-element.55.l_ref, bf16[192,128]{1,0:T(8,128)(2,1)S(1)} %collective-permute-done.8.ya_ref, ...), custom_call_target="tpu_custom_call" | custom-call | flops 1100000000 | tf_op jit(solution)/shard_map/load_edges/pallas_call | solution.py:611
  50.0 0.7 collective-permute-start.12
  50.7 3.6 %collective-permute-start.13 = (bf16[384,128]{1,0:T(8,128)(2,1)S(1)}, bf16[384,128]{1,0:T(8,128)(2,1)S(1)}, u32[]{:S(2)}, u32[]{:S(2)}) collective-permute-start(bf16[384,128]{1,0:T(8,128)(2,1)S(1)} %get-tuple-element.65), channel_id=1, source_target_pairs={{0,8},{8,0},{16,24},{24,16},{32,40},{40,32},{48,56},{56,48},{64,72... | collective-permute-start | bytes 294920 | tf_op jit(solution)/shard_map/ppermute | solution.py:636
  54.3 0.9 %grid.1 = (f32[8,672,128]{2,1,0:T(8,128)S(1)}, f32[96,1024]{1,0:T(8,128)S(1)}) custom-call(f32[8,672,128]{2,1,0:T(8,128)S(1)} %get-tuple-element.47.h_ref, f32[96,512]{1,0:T(8,128)S(1)} %get-tuple-element.55.l_ref, bf16[672,128]{1,0:T(8,128)(2,1)S(1)} %get-tuple-element.58.yh_ref, bf16[192,128]{1,0:T(8,128)(2,1)S(1)} %get-tuple-element.60.yl_ref, ...), custom_call_target="tpu_custom_call" | custom-call | flops 1100000000 | tf_op jit(solution)/shard_map/grid/pallas_call | solution.py:611
  55.1 0.0 collective-permute-done.10.ha_ref
  55.2 0.0 collective-permute-done.11.hb_ref
  55.2 0.0 collective-permute-done.12.la_ref
  55.2 1.1 %collective-permute-done.13.lb_ref = bf16[384,128]{1,0:T(8,128)(2,1)S(1)} collective-permute-done((bf16[384,128]{1,0:T(8,128)(2,1)S(1)}, bf16[384,128]{1,0:T(8,128)(2,1)S(1)}, u32[]{:S(2)}, u32[]{:S(2)}) %collective-permute-start.13) | collective-permute-done | bytes 98336 | tf_op jit(solution)/shard_map/ppermute | solution.py:636
  56.3 5.3 %powers.1 = (f32[96,512]{1,0:T(8,128)S(1)}, f32[128,128]{1,0:T(8,128)S(1)}, f32[8,672,128]{2,1,0:T(8,128)S(1)}) custom-call(s32[4]{0:T(128)S(1)} %add_convert_fusion.flags_ref, f32[96,1024]{1,0:T(8,128)S(1)} %get-tuple-element.61.lown_ref, bf16[672,128]{1,0:T(8,128)(2,1)S(1)} %collective-permute-done.10.ha_ref, ...), custom_call_target="tpu_custom_call", output_to_operand_aliasing={{2}: (10, {})} | custom-call | flops 6600000000 | tf_op jit(solution)/shard_map/powers/pallas_call | solution.py:731
  61.6 20.1 %all_to_all.11 = f32[128,1,128]{2,1,0:T(1,128)S(1)} all-to-all(f32[128,1,128]{2,1,0:T(1,128)S(1)} %bitcast.27), channel_id=1, replica_groups=mesh['gx'=16,'gy'=8] {'gx','gy'}, dimensions={0} | all-to-all | bytes 131072 | tf_op jit(solution)/shard_map/all_to_all | solution.py:745
  81.7 1.4 %combine.1 = (f32[240,32]{1,0:T(8,128)}, f32[240,32]{1,0:T(8,128)}) custom-call(f32[96,512]{1,0:T(8,128)S(1)} %get-tuple-element.70.v_ref, f32[128,128]{1,0:T(8,128)S(1)} %bitcast.28), custom_call_target="tpu_custom_call" | custom-call | flops 3300000000 | tf_op jit(solution)/shard_map/combine/pallas_call | solution.py:611
  (1 shorter events, 0.0 us)
Async XLA Ops:
  0.7 1.6 %copy-start.4 = (bf16[16,32,2048]{2,1,0:T(8,128)(2,1)S(1)}, bf16[16,32,2048]{2,1,0:T(8,128)(2,1)}, u32[]{:S(2)}) copy-start(bf16[16,32,2048]{2,1,0:T(8,128)(2,1)} %param.12) | copy-start | bytes 6291460
  2.3 12.2 %copy-start.3 = (bf16[16,32,2048]{2,1,0:T(8,128)(2,1)S(1)}, bf16[16,32,2048]{2,1,0:T(8,128)(2,1)}, u32[]{:S(2)}) copy-start(bf16[16,32,2048]{2,1,0:T(8,128)(2,1)} %param.10) | copy-start | bytes 6291460
  2.3 12.2 %copy-start.5 = (bf16[16,32,2048]{2,1,0:T(8,128)(2,1)S(1)}, bf16[16,32,2048]{2,1,0:T(8,128)(2,1)}, u32[]{:S(2)}) copy-start(bf16[16,32,2048]{2,1,0:T(8,128)(2,1)} %param.12) | copy-start | bytes 6291460
  2.3 12.2 %copy-start.6 = (bf16[16,32,2048]{2,1,0:T(8,128)(2,1)S(1)}, bf16[16,32,2048]{2,1,0:T(8,128)(2,1)}, u32[]{:S(2)}) copy-start(bf16[16,32,2048]{2,1,0:T(8,128)(2,1)} %param.13) | copy-start | bytes 6291460
  2.3 12.2 %copy-start.7 = (s32[2,16,32,4]{2,3,1,0:T(4,128)S(1)}, s32[2,16,32,4]{2,3,1,0:T(4,128)}, u32[]{:S(2)}) copy-start(s32[2,16,32,4]{2,3,1,0:T(4,128)} %param.15) | copy-start | bytes 49156
  3.9 28.7 %collective-permute-start.2 = (bf16[160,2048]{1,0:T(8,128)(2,1)S(1)}, bf16[160,2048]{1,0:T(8,128)(2,1)S(1)}, u32[]{:S(2)}, u32[]{:S(2)}) collective-permute-start(bf16[160,2048]{1,0:T(8,128)(2,1)S(1)} %bitcast.35), channel_id=1, source_target_pairs={{8,16},{16,8},{24,32},{32,24},{40,48},{48,40},{56,64},{64,56},{72,... | collective-permute-start | bytes 1966088 | tf_op jit(solution)/shard_map/ppermute | solution.py:636
  4.7 27.9 %collective-permute-start.3 = (bf16[160,2048]{1,0:T(8,128)(2,1)S(1)}, bf16[160,2048]{1,0:T(8,128)(2,1)S(1)}, u32[]{:S(2)}, u32[]{:S(2)}) collective-permute-start(bf16[160,2048]{1,0:T(8,128)(2,1)S(1)} %bitcast.34), channel_id=1, source_target_pairs={{0,8},{8,0},{16,24},{24,16},{32,40},{40,32},{48,56},{56,48},{64,72... | collective-permute-start | bytes 1966088 | tf_op jit(solution)/shard_map/ppermute | solution.py:636
  10.1 8.7 %collective-permute-start = (bf16[64,2048]{1,0:T(8,128)(2,1)S(1)}, bf16[64,2048]{1,0:T(8,128)(2,1)S(1)}, u32[]{:S(2)}, u32[]{:S(2)}) collective-permute-start(bf16[64,2048]{1,0:T(8,128)(2,1)S(1)} %get-tuple-element.40), channel_id=1, source_target_pairs={{1,2},{2,1},{3,4},{4,3},{5,6},{6,5},{9,10},{10,9},{11,12},{12,11},... | collective-permute-start | bytes 786440 | tf_op jit(solution)/shard_map/ppermute | solution.py:636
  14.4 4.3 %collective-permute-start.1 = (bf16[64,2048]{1,0:T(8,128)(2,1)S(1)}, bf16[64,2048]{1,0:T(8,128)(2,1)S(1)}, u32[]{:S(2)}, u32[]{:S(2)}) collective-permute-start(bf16[64,2048]{1,0:T(8,128)(2,1)S(1)} %get-tuple-element.41), channel_id=1, source_target_pairs={{0,1},{1,0},{2,3},{3,2},{4,5},{5,4},{6,7},{7,6},{8,9},{9,8},{10,11... | collective-permute-start | bytes 786440 | tf_op jit(solution)/shard_map/ppermute | solution.py:636
  14.5 8.0 %slice-start = ((s8[6291456]{0:T(1024)(128)(4,1)}), s8[4194304]{0:T(1024)(128)(4,1)S(1)}, s32[]{:S(2)}) async-start(s8[6291456]{0:T(1024)(128)(4,1)} %bitcast.23), calls=%async_computation.1 | async-start | bytes 8388608
  14.6 8.0 %slice-start.1 = ((s8[6291456]{0:T(1024)(128)(4,1)}), s8[2097152]{0:T(1024)(128)(4,1)S(1)}, s32[]{:S(2)}) async-start(s8[6291456]{0:T(1024)(128)(4,1)} %bitcast.23), calls=%async_computation.2 | async-start | bytes 4194304
  14.6 8.0 %copy-start = (s32[16,32,2048]{2,1,0:T(8,128)S(1)}, s32[16,32,2048]{2,1,0:T(8,128)}, u32[]{:S(2)}) copy-start(s32[16,32,2048]{2,1,0:T(8,128)} %param.14) | copy-start | bytes 12582916
  18.7 3.9 %copy-start.1 = (bf16[2048,128]{1,0:T(8,128)(2,1)S(1)}, bf16[2048,128]{1,0:T(8,128)(2,1)}, u32[]{:S(2)}) copy-start(bf16[2048,128]{1,0:T(8,128)(2,1)} %constant.38.clone.table_ref) | copy-start | bytes 1572868
  18.7 3.9 %copy-start.2 = (s32[8,1024]{1,0:T(8,128)S(1)}, s32[8,1024]{1,0:T(8,128)}, u32[]{:S(2)}) copy-start(s32[8,1024]{1,0:T(8,128)} %constant.37.clone.maps_ref) | copy-start | bytes 98308
  19.4 10.1 %collective-permute-start.4 = (bf16[48,2048]{1,0:T(8,128)(2,1)S(1)}, bf16[48,2048]{1,0:T(8,128)(2,1)S(1)}, u32[]{:S(2)}, u32[]{:S(2)}) collective-permute-start(bf16[48,2048]{1,0:T(8,128)(2,1)S(1)} %get-tuple-element.52), channel_id=1, source_target_pairs={{8,16},{16,8},{24,32},{32,24},{40,48},{48,40},{56,64},{64,56},{72,... | collective-permute-start | bytes 589832 | tf_op jit(solution)/shard_map/ppermute | solution.py:636
  20.0 12.5 %collective-permute-start.5 = (bf16[48,2048]{1,0:T(8,128)(2,1)S(1)}, bf16[48,2048]{1,0:T(8,128)(2,1)S(1)}, u32[]{:S(2)}, u32[]{:S(2)}) collective-permute-start(bf16[48,2048]{1,0:T(8,128)(2,1)S(1)} %get-tuple-element.53), channel_id=1, source_target_pairs={{0,8},{8,0},{16,24},{24,16},{32,40},{40,32},{48,56},{56,48},{64,72... | collective-permute-start | bytes 589832 | tf_op jit(solution)/shard_map/ppermute | solution.py:636
  27.2 5.4 %copy-start.8 = (bf16[2048,128]{1,0:T(8,128)(2,1)S(1)}, bf16[2048,128]{1,0:T(8,128)(2,1)}, u32[]{:S(2)}) copy-start(bf16[2048,128]{1,0:T(8,128)(2,1)} %constant.39.clone.table_ref) | copy-start | bytes 1572868
  27.2 15.6 %collective-permute-start.7 = (bf16[672,128]{1,0:T(8,128)(2,1)S(1)}, bf16[672,128]{1,0:T(8,128)(2,1)S(1)}, u32[]{:S(2)}, u32[]{:S(2)}) collective-permute-start(bf16[672,128]{1,0:T(8,128)(2,1)S(1)} %get-tuple-element.57), channel_id=1, source_target_pairs={{0,1},{1,0},{2,3},{3,2},{4,5},{5,4},{6,7},{7,6},{8,9},{9,8},{10,11... | collective-permute-start | bytes 516104 | tf_op jit(solution)/shard_map/ppermute | solution.py:636
  29.5 13.4 %collective-permute-start.6 = (bf16[672,128]{1,0:T(8,128)(2,1)S(1)}, bf16[672,128]{1,0:T(8,128)(2,1)S(1)}, u32[]{:S(2)}, u32[]{:S(2)}) collective-permute-start(bf16[672,128]{1,0:T(8,128)(2,1)S(1)} %get-tuple-element.57), channel_id=1, source_target_pairs={{1,2},{2,1},{3,4},{4,3},{5,6},{6,5},{9,10},{10,9},{11,12},{12,11},... | collective-permute-start | bytes 516104 | tf_op jit(solution)/shard_map/ppermute | solution.py:636
  39.3 9.9 %collective-permute-start.9 = (bf16[192,128]{1,0:T(8,128)(2,1)S(1)}, bf16[192,128]{1,0:T(8,128)(2,1)S(1)}, u32[]{:S(2)}, u32[]{:S(2)}) collective-permute-start(bf16[192,128]{1,0:T(8,128)(2,1)S(1)} %get-tuple-element.59), channel_id=1, source_target_pairs={{0,1},{1,0},{2,3},{3,2},{4,5},{5,4},{6,7},{7,6},{8,9},{9,8},{10,11... | collective-permute-start | bytes 147464 | tf_op jit(solution)/shard_map/ppermute | solution.py:636
  39.4 9.8 %collective-permute-start.8 = (bf16[192,128]{1,0:T(8,128)(2,1)S(1)}, bf16[192,128]{1,0:T(8,128)(2,1)S(1)}, u32[]{:S(2)}, u32[]{:S(2)}) collective-permute-start(bf16[192,128]{1,0:T(8,128)(2,1)S(1)} %get-tuple-element.59), channel_id=1, source_target_pairs={{1,2},{2,1},{3,4},{4,3},{5,6},{6,5},{9,10},{10,9},{11,12},{12,11},... | collective-permute-start | bytes 147464 | tf_op jit(solution)/shard_map/ppermute | solution.py:636
  43.7 11.5 %collective-permute-start.10 = (bf16[672,128]{1,0:T(8,128)(2,1)S(1)}, bf16[672,128]{1,0:T(8,128)(2,1)S(1)}, u32[]{:S(2)}, u32[]{:S(2)}) collective-permute-start(bf16[672,128]{1,0:T(8,128)(2,1)S(1)} %get-tuple-element.62), channel_id=1, source_target_pairs={{8,16},{16,8},{24,32},{32,24},{40,48},{48,40},{56,64},{64,56},{72,... | collective-permute-start | bytes 516104 | tf_op jit(solution)/shard_map/ppermute | solution.py:636
  44.4 10.8 %collective-permute-start.11 = (bf16[672,128]{1,0:T(8,128)(2,1)S(1)}, bf16[672,128]{1,0:T(8,128)(2,1)S(1)}, u32[]{:S(2)}, u32[]{:S(2)}) collective-permute-start(bf16[672,128]{1,0:T(8,128)(2,1)S(1)} %get-tuple-element.63), channel_id=1, source_target_pairs={{0,8},{8,0},{16,24},{24,16},{32,40},{40,32},{48,56},{56,48},{64,72... | collective-permute-start | bytes 516104 | tf_op jit(solution)/shard_map/ppermute | solution.py:636
  50.0 5.2 %collective-permute-start.12 = (bf16[384,128]{1,0:T(8,128)(2,1)S(1)}, bf16[384,128]{1,0:T(8,128)(2,1)S(1)}, u32[]{:S(2)}, u32[]{:S(2)}) collective-permute-start(bf16[384,128]{1,0:T(8,128)(2,1)S(1)} %get-tuple-element.64), channel_id=1, source_target_pairs={{8,16},{16,8},{24,32},{32,24},{40,48},{48,40},{56,64},{64,56},{72,... | collective-permute-start | bytes 294920 | tf_op jit(solution)/shard_map/ppermute | solution.py:636
  50.7 5.6 %collective-permute-start.13 = (bf16[384,128]{1,0:T(8,128)(2,1)S(1)}, bf16[384,128]{1,0:T(8,128)(2,1)S(1)}, u32[]{:S(2)}, u32[]{:S(2)}) collective-permute-start(bf16[384,128]{1,0:T(8,128)(2,1)S(1)} %get-tuple-element.65), channel_id=1, source_target_pairs={{0,8},{8,0},{16,24},{24,16},{32,40},{40,32},{48,56},{56,48},{64,72... | collective-permute-start | bytes 294920 | tf_op jit(solution)/shard_map/ppermute | solution.py:636
